TPU v7x, 512 devices: a whole 4x4x16 slice. The times are simulated.
512 devices in a mesh: dp: 32 (over z, y_lo), tensor: 16 (over y_hi, x, core).
Axes of the slice: x: 4, y: 4 (y_hi: 2, y_lo: 2; y = y_hi * 2 + y_lo), z: 16, core: 2. Of those that a mesh axis runs over, the one named last changes fastest.
Arguments:
- activations: bfloat16 [32768, 8192], P('dp', 'tensor'), may hold values from -6 to 6
- out_grads: bfloat16 [32768, 8192], P('dp', 'tensor'), may hold values from -6 to 6
- proj_in: bfloat16 [8192, 64], P('tensor'), may hold values from -0.0625 to 0.0625
- proj_out: bfloat16 [8192, 64], P('tensor'), may hold values from -0.0625 to 0.0625
- segment_ids: int32 [32, 1024], P('dp'), may hold values from 0 to 23, never falling along the last dimension, each value on 1 to 80 neighbouring positions
- train_logs: bfloat16 [131072, 4096], P('dp', 'tensor'), may hold values from -6 to 6
- doc_ids: int32 [131072], P(('dp', 'tensor')), may hold values from 0 to 255
Outputs:
- scores: float32 [768, 131072], P(None, ('dp', 'tensor'))
- doc_influence: float32 [768, 256], replicated
Inputs may be any that keep to these rules, and one draw needn't show every extreme that they name: `segment_ids`: in each row the example numbers never fall; each of the 24 examples has 1 to 80 tokens, and one has exactly 80.
All inputs are finite; a program needn't handle non-finite values.
Results may differ from a plain program's by a relative error of at most 0.0052.
Values may be sent and summed in bfloat16 or wider, within the bound.
No kernel may reach another device: no remote copies, remote signals or barrier semaphores. Data moves between devices by JAX's collectives and lax.ppermute only.
A program may use at most 64 MiB of HBM per device.

v0:
```python
import math

import jax
import jax.numpy as jnp
from jax import lax
from jax.sharding import PartitionSpec as P

EX_DEV = 24
DOCS = 256


def per_device(activations, out_grads, proj_in, proj_out, segment_ids, train_logs, doc_ids):
    width_parts = lax.axis_size("tensor")
    position = lax.axis_index("tensor")
    tok_rows = activations.shape[0]
    rank = proj_in.shape[1]
    partial_value = jnp.concatenate(
        [
            jnp.dot(activations, proj_in, preferred_element_type=jnp.float32),
            jnp.dot(out_grads, proj_out, preferred_element_type=jnp.float32),
        ],
        axis=1,
    )
    seg_row = segment_ids[0]
    labels = jnp.arange(EX_DEV, dtype=jnp.int32)
    counts = jnp.sum((seg_row[:, None] == labels[None, :]).astype(jnp.float32), axis=0)
    block_rank = rank // width_parts
    summed = lax.psum(partial_value, "tensor").astype(jnp.bfloat16)
    in_proj = summed[:, :rank]
    out_proj = summed[:, rank:]
    own_out = lax.dynamic_slice_in_dim(out_proj, position * block_rank, block_rank, 1)
    member = (seg_row[:, None] == labels[None, :]).astype(jnp.bfloat16)
    masked = (member[:, :, None] * own_out[:, None, :]).reshape(tok_rows, EX_DEV * block_rank)
    log_sums = jnp.einsum("ta,tj->aj", masked, in_proj, preferred_element_type=jnp.float32)
    log_sums = log_sums.reshape(EX_DEV, block_rank * rank)
    query_block = (log_sums / counts[:, None]).astype(jnp.bfloat16)
    train_full = lax.all_to_all(train_logs, "tensor", split_axis=0, concat_axis=1, tiled=True)
    local_rows = train_full.shape[0]
    wide_block = lax.all_gather(query_block, "tensor", axis=1, tiled=True)
    rows = lax.dot_general(
        lax.all_gather(wide_block, "dp", axis=0, tiled=True),
        train_full,
        (((1,), (1,)), ((), ())),
        preferred_element_type=jnp.float32,
    )
    scores = rows * 0.125
    doc_labels = jnp.arange(DOCS, dtype=jnp.int32)
    doc_hot = (doc_ids[:, None] == doc_labels[None, :]).astype(jnp.float32)
    doc_part = jnp.dot(scores, doc_hot, precision=lax.Precision.HIGHEST)
    total_rows = local_rows * lax.axis_size("tensor") * lax.axis_size("dp")
    doc_total = lax.psum(doc_part, ("dp", "tensor"))
    doc_influence = doc_total / math.sqrt(total_rows / DOCS)
    return (scores, doc_influence)


def solution(mesh):
    placed = (
        P("dp", "tensor"),
        P("dp", "tensor"),
        P("tensor", None),
        P("tensor", None),
        P("dp", None),
        P("dp", "tensor"),
        P(("dp", "tensor")),
    )
    return jax.shard_map(
        per_device,
        mesh=mesh,
        in_specs=placed,
        out_specs=(P(None, ("dp", "tensor")), P()),
        check_vma=False,
    )
```

profile of v0, /device:TPU:1, one launch (start us, length us, event | category | flops | bytes accessed | tf_op | source)
XLA Modules:
  0.0 760.7 jit_solution(6124716450737580398)
XLA Ops:
  7.2 0.0 copy-start
  7.2 0.0 all-gather.2.cloned.1.call-start
  7.2 0.9 convert_reduce_fusion
  8.1 0.7 fusion.4
  8.8 0.0 copy-done
  8.8 1.3 fusion.5
  10.1 1.7 fusion.6
  11.8 0.1 pad_maximum_fusion
  11.8 71.0 %all-reduce.4 = bf16[1024,128]{0,1:T(8,128)(2,1)S(1)} all-reduce(f32[1024,128]{0,1:T(8,128)S(1)} %pad_maximum_fusion), channel_id=1, replica_groups=mesh['dp'=32,'tensor'=16] {'tensor'}, use_global_device_ids=true, to_apply=%region_0.0 | all-reduce | flops 131072 | bytes 786432 | tf_op jit(solution)/shard_map/psum | solution.py:28
  82.9 0.1 broadcast_multiply_fusion.1
  83.0 0.1 mul.30
  83.0 0.2 fusion.1
  83.2 0.1 reshape.42
  83.3 0.1 divide_convert_fusion
  83.4 26.8 %all_gather.6 = bf16[24,4096]{1,0:T(8,128)(2,1)} all-gather(bf16[24,256]{1,0:T(8,128)(2,1)S(1)} %divide_convert_fusion), channel_id=1, replica_groups=mesh['dp'=32,'tensor'=16] {'tensor'}, dimensions={1}, use_global_device_ids=true | all-gather | bytes 208896 | tf_op jit(solution)/shard_map/all_gather | solution.py:39
  110.2 0.0 all-gather.2.cloned.1.call-update
  110.2 0.0 all-reduce.3.cloned.1.call-start
  110.3 33.9 %all_to_all.19 = bf16[16,256,256]{2,1,0:T(8,128)(2,1)S(1)} all-to-all(bf16[16,256,256]{2,1,0:T(8,128)(2,1)} %bitcast.15), channel_id=1, replica_groups=mesh['dp'=32,'tensor'=16] {'tensor'}, dimensions={0} | all-to-all | bytes 4194304 | tf_op jit(solution)/shard_map/all_to_all | solution.py:37
  144.2 2.4 copy.12
  146.6 130.0 %all-gather.2.cloned.1.call-done = bf16[768,4096]{1,0:T(8,128)(2,1)} async-done(((bf16[24,4096]{1,0:T(8,128)(2,1)}), bf16[768,4096]{1,0:T(8,128)(2,1)}) %all-gather.2.cloned.1.call-update) | async-done | bytes 6291472 | tf_op jit(solution)/shard_map/all_gather | solution.py:41
  276.7 0.0 copy-start.2
  276.7 5.2 convolution_multiply_fusion
  281.9 0.0 copy-done.2
  281.9 0.0 copy-start.1
  281.9 1.5 fusion
  283.4 0.0 all-reduce.3.cloned.1.call-update
  283.4 468.4 %all-reduce.3.cloned.1.call-done = f32[768,256]{1,0:T(8,128)} async-done(((f32[768,256]{1,0:T(8,128)}), f32[768,256]{1,0:T(8,128)}) %all-reduce.3.cloned.1.call-update) | async-done | bytes 786448 | tf_op jit(solution)/shard_map/psum | solution.py:51
  751.8 2.1 broadcast_multiply_fusion
  753.9 0.0 copy-done.1
  (2 shorter events, 0.0 us)
Async XLA Ops:
  7.2 1.7 copy-start
  7.2 269.5 %all-gather.2.cloned.1.call-start = ((), (), s32[]{:S(2)}) async-start(), calls=%async_computation.1 | async-start | bytes 6488064 | tf_op jit(solution)/shard_map/all_gather | solution.py:41
  110.2 641.6 %all-reduce.3.cloned.1.call-start = ((), (), s32[]{:S(2)}) async-start(), calls=%async_computation.2 | async-start | bytes 1572864 | tf_op jit(solution)/shard_map/psum | solution.py:51
  276.7 5.2 copy-start.2
  281.9 472.0 %copy-start.1 = (f32[768,256]{1,0:T(8,128)}, f32[768,256]{1,0:T(8,128)S(1)}, u32[]{:S(2)}) copy-start(f32[768,256]{1,0:T(8,128)S(1)} %convolution_multiply_fusion) | copy-start | bytes 2359300
Sparse Core Ops, SparseCore 0:
  110.4 166.2 all-gather.1
  283.5 468.2 all-reduce.2
where the time goes:
time: 762 us; the launch traced here: 761 us
  waiting for transfers between devices  598 us (78%)
  blocking collectives  132 us (17%)
  between operations  14.1 us (2%)
  matrix products  9.8 us (1%)
    psum x1, waiting for transfers between devices, per_device(): doc_total = lax.psum(doc_part, ('dp', 'tensor'))  468 us
    all_gather x1, waiting for transfers between devices, per_device(): lax.all_gather(wide_block, 'dp', axis=0, tiled=True)  130 us
    psum x1, blocking collectives, per_device(): summed = lax.psum(partial_value, 'tensor').astype(jnp.bfloat16)  71 us
    all_to_all x1, blocking collectives, per_device(): lax.all_to_all(train_logs, 'tensor', split_axis=0, concat_axis=1, tiled=T...  33.9 us
    all_gather x1, blocking collectives, per_device(): wide_block = lax.all_gather(query_block, 'tensor', axis=1, tiled=True)  26.8 us
  transfers between devices with their start and end apart: 2, of which 2 were waited for; matrix products, arithmetic and copies ran while one was open for 0% of the time, Pallas kernels for 0%

commit v1 on v0

v1 whole, which is shorter than its diff:
```python
import math

import jax
import jax.numpy as jnp
from jax import lax
from jax.sharding import Mesh
from jax.sharding import PartitionSpec as P

EX_DEV = 24
DOCS = 256
AXES = ("z", "yl", "yh", "x", "c")
SIZES = (16, 2, 2, 4, 2)
DP = ("z", "yl")
TENSOR = ("yh", "x", "c")
BF16 = jnp.bfloat16
F32 = jnp.float32


def swap(value, axis):
    return lax.ppermute(value, axis, [(0, 1), (1, 0)])


def exchange(value, axes):
    return lax.all_to_all(value, axes, 0, 0, tiled=True)


def split(value):
    high = lax.reduce_precision(value, 8, 7)
    return high.astype(BF16), (value - high).astype(BF16)


def dot_t(left, right):
    return lax.dot_general(left, right, (((1,), (1,)), ((), ())), preferred_element_type=F32)


def per_device(activations, out_grads, proj_in, proj_out, segment_ids, train_logs, doc_ids):
    yh, x, c = (lax.axis_index(name) for name in TENSOR)
    position = (yh * 4 + x) * 2 + c
    tokens = activations.shape[0]
    rank = proj_in.shape[1]
    logs, width = train_logs.shape

    blocks = train_logs.reshape(2, 4, 2, logs // 16, width)

    def rows_for(target):
        def block(row, col):
            return lax.dynamic_slice(blocks, (row, target, col, 0, 0), (1, 1, 1, logs // 16, width)).reshape(logs // 16, width)

        return jnp.concatenate([block(1 - yh, 1 - c), block(yh, 1 - c), block(1 - yh, c), block(yh, c)])

    rows = [rows_for(x)]
    for d in range(1, 4):
        rows.append(lax.ppermute(rows_for((x + d) % 4), "x", [(i, (i + d) % 4) for i in range(4)]))

    part = jnp.concatenate(
        [
            jnp.dot(activations, proj_in, preferred_element_type=F32),
            jnp.dot(out_grads, proj_out, preferred_element_type=F32),
        ],
        axis=1,
    )
    chunk = tokens // 16
    owners = jnp.pad(doc_ids.astype(F32).reshape(-1, 2 * rank), ((0, 6), (0, 0)))
    first = jnp.concatenate(
        [part.reshape(16, chunk, 2 * rank), jnp.broadcast_to(owners[None], (16, 8, 2 * rank))], axis=1
    )
    first = exchange(first.reshape(16 * (chunk + 8), 2 * rank), TENSOR).reshape(16, chunk + 8, 2 * rank)
    own = jnp.sum(first[:, :chunk], axis=0).astype(BF16)
    all_owners = first[:, chunk : chunk + 2].reshape(logs).astype(jnp.int32)
    both = exchange(jnp.broadcast_to(own[None], (16, chunk, 2 * rank)).reshape(tokens, 2 * rank), TENSOR)
    in_proj = both[:, :rank]
    out_proj = both[:, rank:]

    seg_row = segment_ids[0]
    labels = jnp.arange(EX_DEV, dtype=jnp.int32)
    hot = seg_row[:, None] == labels[None, :]
    counts = jnp.sum(hot.astype(F32), axis=0)
    block_rank = rank // 16
    own_out = lax.dynamic_slice_in_dim(out_proj, position * block_rank, block_rank, 1)
    masked = (hot.astype(BF16)[:, :, None] * own_out[:, None, :]).reshape(tokens, EX_DEV * block_rank)
    log_sums = jnp.einsum("ta,tj->aj", masked, in_proj, preferred_element_type=F32)
    query_block = (log_sums.reshape(EX_DEV, block_rank * rank) / counts[:, None]).astype(BF16)

    doc_hot = (jnp.arange(DOCS, dtype=jnp.int32)[:, None] == all_owners[None, :]).astype(BF16)
    doc_sums = jnp.dot(doc_hot, train_logs, preferred_element_type=F32)
    doc_high, doc_low = split(doc_sums)
    own_docs = DOCS // 32
    second = jnp.concatenate(
        [
            jnp.broadcast_to(query_block[None], (32, EX_DEV, width)),
            doc_high.reshape(32, own_docs, width),
            doc_low.reshape(32, own_docs, width),
        ],
        axis=1,
    )
    each = EX_DEV + 2 * own_docs
    second = exchange(second.reshape(32 * each, width), DP).reshape(32, each, width)
    queries = second[:, :EX_DEV].reshape(32 * EX_DEV, width)
    total_docs = jnp.sum(second[:, EX_DEV:].astype(F32), axis=0)
    total_docs = total_docs[:own_docs] + total_docs[own_docs:]
    high, low = split(total_docs)
    doc_part = dot_t(high, queries) + dot_t(low, queries)

    high, low = split(doc_part)
    tail = jnp.concatenate([high, low]).reshape(-1, width)
    height = queries.shape[0]
    third = jnp.concatenate([queries, tail])
    third = exchange(jnp.broadcast_to(third[None], (4, *third.shape)).reshape(-1, width), "x")
    third = third.reshape(4, -1, width)
    doc_part = jnp.sum(third[:, height:].reshape(4, 2 * own_docs, height).astype(F32), axis=0)
    doc_part = doc_part[:own_docs] + doc_part[own_docs:]
    doc_part = doc_part + swap(doc_part, "c")
    doc_part = doc_part + swap(doc_part, "yh")

    wide = jnp.concatenate([third[(x - d) % 4, :height] for d in range(4)], axis=1)
    stored = jnp.concatenate(rows, axis=1)
    half = stored.shape[0] // 2
    quarter = half // 2
    away = dot_t(wide, stored[:half]).astype(BF16)
    away = swap(away, "c")
    kept = dot_t(wide, stored[half:]) + away.astype(F32)
    far = swap(kept[:, :quarter].astype(BF16), "yh")
    scores = (kept[:, quarter:] + far.astype(F32)) * 0.125

    total_rows = logs * 32
    final = (doc_part * (0.125 / math.sqrt(total_rows / DOCS))).astype(BF16)
    final = exchange(jnp.broadcast_to(final[None], (32, own_docs, height)).reshape(DOCS, height), DP)
    doc_influence = final.T.astype(F32)
    return (scores, doc_influence)


def solution(mesh):
    inner = Mesh(mesh.devices.reshape(SIZES), AXES)
    placed = (
        P(DP, TENSOR),
        P(DP, TENSOR),
        P(TENSOR, None),
        P(TENSOR, None),
        P(DP, None),
        P(DP, TENSOR),
        P(AXES),
    )
    return jax.shard_map(
        per_device,
        mesh=inner,
        in_specs=placed,
        out_specs=(P(None, AXES), P()),
        check_vma=False,
    )
```

time: 762 us -> 200 us (0.26)
  waiting for transfers between devices: 598 us -> 104 us
  blocking collectives: 132 us -> 0 us
  starting transfers between devices: 0.08 us -> 61.2 us
  between operations: 14.1 us -> 1.05 us
  other arithmetic: 3.91 us -> 11.9 us
    psum x1 -> x0, waiting for transfers between devices: 468 us -> none  [per_device(): doc_total = lax.psum(doc_part, ('dp', 'tensor'))]
    all_gather x1 -> x0, waiting for transfers between devices: 130 us -> none  [per_device(): lax.all_gather(wide_block, 'dp', axis=0, tiled=True)]
    psum x1 -> x0, blocking collectives: 71 us -> none  [per_device(): summed = lax.psum(partial_value, 'tensor').astype(jnp.bfloat16)]
    all_to_all x0 -> x5, waiting for transfers between devices: none -> 61.8 us  [exchange(): return lax.all_to_all(value, axes, 0, 0, tiled=True)]
    ppermute x0 -> x7, waiting for transfers between devices: none -> 42.6 us  [the longest x3 27.8 us: per_device(): lax.ppermute(rows_for((x + d) % 4), 'x', [(i, (i + d) % 4) for i in range...]
    all_to_all x0 -> x5, starting transfers between devices: none -> 36.9 us  [exchange(): return lax.all_to_all(value, axes, 0, 0, tiled=True)]
    all_to_all x1 -> x0, blocking collectives: 33.9 us -> none  [per_device(): lax.all_to_all(train_logs, 'tensor', split_axis=0, concat_axis=1, tiled=T...]
    all_gather x1 -> x0, blocking collectives: 26.8 us -> none  [per_device(): wide_block = lax.all_gather(query_block, 'tensor', axis=1, tiled=True)]
  transfers between devices with their start and end apart: 2 -> 12, of which waited for: 2 -> 10; matrix products, arithmetic and copies ran while one was open for 0% -> 8% of each run, Pallas kernels for 0% -> 0%
where the time goes in v1:
time: 200 us; the launch traced here: 198 us
  waiting for transfers between devices  104 us (52%)
  starting transfers between devices  61.2 us (31%)
  other arithmetic  11.9 us (6%)
  matrix products  10.5 us (5%)
  local copies, waits for them, and re-layouts  8.94 us (4%)
    all_to_all x5, waiting for transfers between devices, exchange(): return lax.all_to_all(value, axes, 0, 0, tiled=True)  61.8 us
    all_to_all x5, starting transfers between devices, exchange(): return lax.all_to_all(value, axes, 0, 0, tiled=True)  36.9 us
    ppermute x3, waiting for transfers between devices, per_device(): lax.ppermute(rows_for((x + d) % 4), 'x', [(i, (i + d) % 4) for i in range...  27.8 us
    ppermute x4, waiting for transfers between devices, swap(): return lax.ppermute(value, axis, [(0, 1), (1, 0)])  14.8 us
    ppermute x4, starting transfers between devices, swap(): return lax.ppermute(value, axis, [(0, 1), (1, 0)])  13.5 us
    ppermute x3, starting transfers between devices, per_device(): lax.ppermute(rows_for((x + d) % 4), 'x', [(i, (i + d) % 4) for i in range...  10.7 us
    concatenate x1, other arithmetic, per_device(): stored = jnp.concatenate(rows, axis=1)  5.26 us
    dot_general x4, matrix products, dot_t(): lax.dot_general(left, right, (((1,), (1,)), ((), ())), preferred_element_...  5.07 us
  transfers between devices with their start and end apart: 12, of which 10 were waited for; matrix products, arithmetic and copies ran while one was open for 8% of the time, Pallas kernels for 0%

profile of v1, /device:TPU:1, one launch (start us, length us, event | category | flops | bytes accessed | tf_op | source)
XLA Modules:
  0.0 197.9 jit_solution(13159381075118603035)
XLA Ops:
  0.6 0.0 copy-start
  0.6 0.8 convert_bitcast_fusion.1
  1.4 0.5 copy-done
  1.9 1.3 fusion.17
  3.1 1.7 fusion.18
  4.8 0.0 copy-start.4
  4.9 0.2 copy.16
  5.1 0.9 pad_maximum_fusion.3
  6.0 10.3 %all-to-all-start = ((f32[16,72,128]{2,1,0:T(8,128)}), f32[16,72,128]{2,1,0:T(8,128)S(1)}, u32[]{:S(2)}, u32[]{:S(2)}) async-start(f32[16,72,128]{2,1,0:T(8,128)} %pad_maximum_fusion.3), calls=%async_computation | async-start | bytes 1179648 | tf_op jit(solution)/shard_map/all_to_all | solution.py:24
  16.2 0.1 convert_reduce_fusion.2
  16.4 12.1 %all-to-all-done = f32[16,72,128]{2,1,0:T(8,128)S(1)} async-done(((f32[16,72,128]{2,1,0:T(8,128)}), f32[16,72,128]{2,1,0:T(8,128)S(1)}, u32[]{:S(2)}, u32[]{:S(2)}) %all-to-all-start) | async-done | bytes 589856 | tf_op jit(solution)/shard_map/all_to_all | solution.py:24
  28.5 0.8 broadcast_in_dim.11
  29.3 4.3 %all-to-all-start.1 = ((bf16[16,64,128]{2,1,0:T(8,128)(2,1)}), bf16[16,64,128]{2,1,0:T(8,128)(2,1)S(1)}, u32[]{:S(2)}, u32[]{:S(2)}) async-start(bf16[16,64,128]{2,1,0:T(8,128)(2,1)} %broadcast_in_dim.11), calls=%async_computation.1 | async-start | bytes 524288 | tf_op jit(solution)/shard_map/all_to_all | solution.py:24
  33.6 2.3 %fusion.9 = (bf16[32,8,256]{2,1,0:T(8,128)(2,1)S(1)}, bf16[32,8,256]{2,1,0:T(8,128)(2,1)S(1)}) fusion(bf16[4096,256]{1,0:T(8,128)(2,1)} %param.12, s32[4096]{0:T(1024)S(1)} %bitcast.74), kind=kOutput, calls=%fused_computation.34 | convolution fusion | flops 538181632 | bytes 2375680 | tf_op jit(solution)/shard_map/dot_general | solution.py:85
  35.9 6.4 %all-to-all-done.1 = bf16[16,64,128]{2,1,0:T(8,128)(2,1)S(1)} async-done(((bf16[16,64,128]{2,1,0:T(8,128)(2,1)}), bf16[16,64,128]{2,1,0:T(8,128)(2,1)S(1)}, u32[]{:S(2)}, u32[]{:S(2)}) %all-to-all-start.1) | async-done | bytes 262176 | tf_op jit(solution)/shard_map/all_to_all | solution.py:24
  42.3 0.1 slice.64
  42.5 0.1 constant_dynamic-slice_fusion
  42.6 0.1 copy.17
  42.7 0.1 broadcast_multiply_fusion
  42.9 0.1 mul.44
  42.9 0.2 fusion.6
  43.1 0.1 reshape.173
  43.2 0.1 divide_convert_fusion
  43.3 0.9 pad_maximum_fusion.2
  44.2 13.4 %all-to-all-start.2 = ((bf16[32,40,256]{2,1,0:T(8,128)(2,1)}), bf16[32,40,256]{2,1,0:T(8,128)(2,1)S(1)}, u32[]{:S(2)}, u32[]{:S(2)}) async-start(bf16[32,40,256]{2,1,0:T(8,128)(2,1)} %pad_maximum_fusion.2), calls=%async_computation.2 | async-start | bytes 1310720 | tf_op jit(solution)/shard_map/all_to_all | solution.py:24
  57.7 36.4 %all-to-all-done.2 = bf16[32,40,256]{2,1,0:T(8,128)(2,1)S(1)} async-done(((bf16[32,40,256]{2,1,0:T(8,128)(2,1)}), bf16[32,40,256]{2,1,0:T(8,128)(2,1)S(1)}, u32[]{:S(2)}, u32[]{:S(2)}) %all-to-all-start.2) | async-done | bytes 655392 | tf_op jit(solution)/shard_map/all_to_all | solution.py:24
  94.2 0.2 fusion.14
  94.4 0.3 reduce-precision_convert_fusion.1
  94.6 0.1 reshape.177
  94.7 1.3 broadcast_in_dim.13
  96.0 4.0 %all-to-all-start.3 = ((bf16[4,816,256]{2,1,0:T(8,128)(2,1)}), bf16[4,816,256]{2,1,0:T(8,128)(2,1)S(1)}, u32[]{:S(2)}, u32[]{:S(2)}) async-start(bf16[4,816,256]{2,1,0:T(8,128)(2,1)} %broadcast_in_dim.13), calls=%async_computation.3 | async-start | bytes 3342336 | tf_op jit(solution)/shard_map/all_to_all | solution.py:24
  100.0 1.7 dynamic-slice_bitcast_fusion.19
  101.8 0.8 pad_maximum_fusion.5
  102.6 4.0 %collective-permute-start = (bf16[1024,256]{1,0:T(8,128)(2,1)}, bf16[1024,256]{1,0:T(8,128)(2,1)}, u32[]{:S(2)}, u32[]{:S(2)}) collective-permute-start(bf16[1024,256]{1,0:T(8,128)(2,1)} %pad_maximum_fusion.5), channel_id=1, source_target_pairs={{0,2},{2,4},{4,6},{6,0},{1,3},{3,5},{5,7},{7,1},{8,10},{10,12},{12... | collective-permute-start | bytes 1572872 | tf_op jit(solution)/shard_map/ppermute | solution.py:53
  106.5 0.8 pad_maximum_fusion.6
  107.4 3.7 %collective-permute-start.1 = (bf16[1024,256]{1,0:T(8,128)(2,1)}, bf16[1024,256]{1,0:T(8,128)(2,1)}, u32[]{:S(2)}, u32[]{:S(2)}) collective-permute-start(bf16[1024,256]{1,0:T(8,128)(2,1)} %pad_maximum_fusion.6), channel_id=1, source_target_pairs={{0,4},{2,6},{4,0},{6,2},{1,5},{3,7},{5,1},{7,3},{8,12},{10,14},{12... | collective-permute-start | bytes 1572872 | tf_op jit(solution)/shard_map/ppermute | solution.py:53
  111.1 0.8 pad_maximum_fusion.7
  111.9 3.1 %collective-permute-start.2 = (bf16[1024,256]{1,0:T(8,128)(2,1)}, bf16[1024,256]{1,0:T(8,128)(2,1)}, u32[]{:S(2)}, u32[]{:S(2)}) collective-permute-start(bf16[1024,256]{1,0:T(8,128)(2,1)} %pad_maximum_fusion.7), channel_id=1, source_target_pairs={{0,6},{2,0},{4,2},{6,4},{1,7},{3,1},{5,3},{7,5},{8,14},{10,8},{12,... | collective-permute-start | bytes 1572872 | tf_op jit(solution)/shard_map/ppermute | solution.py:53
  115.1 15.1 %collective-permute-done = bf16[1024,256]{1,0:T(8,128)(2,1)} collective-permute-done((bf16[1024,256]{1,0:T(8,128)(2,1)}, bf16[1024,256]{1,0:T(8,128)(2,1)}, u32[]{:S(2)}, u32[]{:S(2)}) %collective-permute-start) | collective-permute-done | bytes 524320 | tf_op jit(solution)/shard_map/ppermute | solution.py:53
  130.2 11.6 %collective-permute-done.1 = bf16[1024,256]{1,0:T(8,128)(2,1)} collective-permute-done((bf16[1024,256]{1,0:T(8,128)(2,1)}, bf16[1024,256]{1,0:T(8,128)(2,1)}, u32[]{:S(2)}, u32[]{:S(2)}) %collective-permute-start.1) | collective-permute-done | bytes 524320 | tf_op jit(solution)/shard_map/ppermute | solution.py:53
  141.8 1.1 collective-permute-done.2
  142.9 5.3 %pad_maximum_fusion = bf16[1024,1024]{1,0:T(8,128)(2,1)} fusion(bf16[1024,256]{1,0:T(8,128)(2,1)} %collective-permute-done.2, bf16[1024,256]{1,0:T(8,128)(2,1)} %collective-permute-done.1, bf16[1024,256]{1,0:T(8,128)(2,1)} %collective-permute-done, bf16[256,256]{1,0:T(8,128)(2,1)S(1)} %get-tuple-element.21, bf16[256,256]{1,0:T(8,128)(2,1)S(1)} %get-tuple-element.22, ...), kind=kLoop, calls=%fused_computation.2 | loop fusion | flops 14680064 | bytes 4194304 | tf_op jit(solution)/shard_map/concatenate | solution.py:116
  148.1 0.0 all-to-all-done.3
  148.1 0.1 dynamic-slice_bitcast_fusion.3
  148.2 0.0 copy-start.2
  148.3 1.7 copy-done.1
  150.0 1.9 convolution_convert_fusion
  151.9 0.0 copy-done.2
  151.9 4.4 %collective-permute-start.3 = (bf16[768,512]{1,0:T(8,128)(2,1)}, bf16[768,512]{1,0:T(8,128)(2,1)}, u32[]{:S(2)}, u32[]{:S(2)}) collective-permute-start(bf16[768,512]{1,0:T(8,128)(2,1)} %convolution_convert_fusion), channel_id=1, source_target_pairs={{0,1},{1,0},{2,3},{3,2},{4,5},{5,4},{6,7},{7,6},{8,9},{9,8},{10,11... | collective-permute-start | bytes 2359304 | tf_op jit(solution)/shard_map/ppermute | solution.py:20
  156.4 1.9 collective-permute-start.5
  158.3 1.2 collective-permute-done.5
  159.5 3.8 %collective-permute-start.6 = (f32[8,768]{1,0:T(8,128)S(1)}, f32[8,768]{1,0:T(8,128)S(1)}, u32[]{:S(2)}, u32[]{:S(2)}) collective-permute-start(f32[8,768]{1,0:T(8,128)S(1)} %add.178), channel_id=1, source_target_pairs={{0,8},{8,0},{1,9},{9,1},{2,10},{10,2},{3,11},{11,3},{4,12},{12,4},... | collective-permute-start | bytes 73736 | tf_op jit(solution)/shard_map/ppermute | solution.py:20
  163.3 2.3 %collective-permute-done.6 = f32[8,768]{1,0:T(8,128)S(1)} collective-permute-done((f32[8,768]{1,0:T(8,128)S(1)}, f32[8,768]{1,0:T(8,128)S(1)}, u32[]{:S(2)}, u32[]{:S(2)}) %collective-permute-start.6) | collective-permute-done | bytes 24608 | tf_op jit(solution)/shard_map/ppermute | solution.py:20
  165.5 0.8 broadcast_in_dim.14
  166.3 4.9 %all-to-all-start.4 = ((bf16[32,8,768]{2,1,0:T(8,128)(2,1)}), bf16[32,8,768]{2,1,0:T(8,128)(2,1)S(1)}, u32[]{:S(2)}, u32[]{:S(2)}) async-start(bf16[32,8,768]{2,1,0:T(8,128)(2,1)} %broadcast_in_dim.14), calls=%async_computation.4 | async-start | bytes 786432 | tf_op jit(solution)/shard_map/all_to_all | solution.py:24
  171.3 0.0 collective-permute-done.3
  171.3 2.7 %convert_add_fusion = f32[768,512]{1,0:T(8,128)S(1)} fusion(bf16[768,512]{1,0:T(8,128)(2,1)} %collective-permute-done.3, bf16[1024,1024]{1,0:T(8,128)(2,1)} %pad_maximum_fusion, bf16[768,256]{1,0:T(8,128)(2,1)S(1)} %get-tuple-element.25, bf16[768,256]{1,0:T(8,128)(2,1)} %copy-done.2, bf16[768,256]{1,0:T(8,128)(2,1)} %copy-done.3, ...), kind=kOutput, calls=%fused_computation.5 | convolution fusion | flops 812384256 | bytes 4980736 | tf_op jit(solution)/shard_map/dot_general | solution.py:33
  174.0 0.1 slice.108
  174.1 3.4 %collective-permute-start.4 = (bf16[768,256]{1,0:T(8,128)(2,1)S(1)}, bf16[768,256]{1,0:T(8,128)(2,1)S(1)}, u32[]{:S(2)}, u32[]{:S(2)}) collective-permute-start(bf16[768,256]{1,0:T(8,128)(2,1)S(1)} %slice.108), channel_id=1, source_target_pairs={{0,8},{8,0},{1,9},{9,1},{2,10},{10,2},{3,11},{11,3},{4,12},{12,4},... | collective-permute-start | bytes 1179656 | tf_op jit(solution)/shard_map/ppermute | solution.py:20
  177.4 11.4 %collective-permute-done.4 = bf16[768,256]{1,0:T(8,128)(2,1)S(1)} collective-permute-done((bf16[768,256]{1,0:T(8,128)(2,1)S(1)}, bf16[768,256]{1,0:T(8,128)(2,1)S(1)}, u32[]{:S(2)}, u32[]{:S(2)}) %collective-permute-start.4) | collective-permute-done | bytes 393248 | tf_op jit(solution)/shard_map/ppermute | solution.py:20
  188.8 1.0 fusion.4
  189.8 6.9 %all-to-all-done.4 = bf16[32,8,768]{2,1,0:T(8,128)(2,1)S(1)} async-done(((bf16[32,8,768]{2,1,0:T(8,128)(2,1)}), bf16[32,8,768]{2,1,0:T(8,128)(2,1)S(1)}, u32[]{:S(2)}, u32[]{:S(2)}) %all-to-all-start.4) | async-done | bytes 393248 | tf_op jit(solution)/shard_map/all_to_all | solution.py:24
  196.7 0.1 convert_bitcast_fusion
  196.8 1.1 copy.19
  (20 shorter events, 0.3 us)
Async XLA Ops:
  0.6 1.2 copy-start
  4.8 11.4 %copy-start.4 = (s32[1,1024]{1,0:T(1,128)S(1)}, s32[1,1024]{1,0:T(1,128)}, u32[]{:S(2)}) copy-start(s32[1,1024]{1,0:T(1,128)} %param.11) | copy-start | bytes 12292
  6.0 22.5 %all-to-all-start = ((f32[16,72,128]{2,1,0:T(8,128)}), f32[16,72,128]{2,1,0:T(8,128)S(1)}, u32[]{:S(2)}, u32[]{:S(2)}) async-start(f32[16,72,128]{2,1,0:T(8,128)} %pad_maximum_fusion.3), calls=%async_computation | async-start | bytes 1179648 | tf_op jit(solution)/shard_map/all_to_all | solution.py:24
  29.3 13.1 %all-to-all-start.1 = ((bf16[16,64,128]{2,1,0:T(8,128)(2,1)}), bf16[16,64,128]{2,1,0:T(8,128)(2,1)S(1)}, u32[]{:S(2)}, u32[]{:S(2)}) async-start(bf16[16,64,128]{2,1,0:T(8,128)(2,1)} %broadcast_in_dim.11), calls=%async_computation.1 | async-start | bytes 524288 | tf_op jit(solution)/shard_map/all_to_all | solution.py:24
  44.2 49.9 %all-to-all-start.2 = ((bf16[32,40,256]{2,1,0:T(8,128)(2,1)}), bf16[32,40,256]{2,1,0:T(8,128)(2,1)S(1)}, u32[]{:S(2)}, u32[]{:S(2)}) async-start(bf16[32,40,256]{2,1,0:T(8,128)(2,1)} %pad_maximum_fusion.2), calls=%async_computation.2 | async-start | bytes 1310720 | tf_op jit(solution)/shard_map/all_to_all | solution.py:24
  96.0 52.1 %all-to-all-start.3 = ((bf16[4,816,256]{2,1,0:T(8,128)(2,1)}), bf16[4,816,256]{2,1,0:T(8,128)(2,1)S(1)}, u32[]{:S(2)}, u32[]{:S(2)}) async-start(bf16[4,816,256]{2,1,0:T(8,128)(2,1)} %broadcast_in_dim.13), calls=%async_computation.3 | async-start | bytes 3342336 | tf_op jit(solution)/shard_map/all_to_all | solution.py:24
  102.6 27.6 %collective-permute-start = (bf16[1024,256]{1,0:T(8,128)(2,1)}, bf16[1024,256]{1,0:T(8,128)(2,1)}, u32[]{:S(2)}, u32[]{:S(2)}) collective-permute-start(bf16[1024,256]{1,0:T(8,128)(2,1)} %pad_maximum_fusion.5), channel_id=1, source_target_pairs={{0,2},{2,4},{4,6},{6,0},{1,3},{3,5},{5,7},{7,1},{8,10},{10,12},{12... | collective-permute-start | bytes 1572872 | tf_op jit(solution)/shard_map/ppermute | solution.py:53
  107.4 34.4 %collective-permute-start.1 = (bf16[1024,256]{1,0:T(8,128)(2,1)}, bf16[1024,256]{1,0:T(8,128)(2,1)}, u32[]{:S(2)}, u32[]{:S(2)}) collective-permute-start(bf16[1024,256]{1,0:T(8,128)(2,1)} %pad_maximum_fusion.6), channel_id=1, source_target_pairs={{0,4},{2,6},{4,0},{6,2},{1,5},{3,7},{5,1},{7,3},{8,12},{10,14},{12... | collective-permute-start | bytes 1572872 | tf_op jit(solution)/shard_map/ppermute | solution.py:53
  111.9 30.9 %collective-permute-start.2 = (bf16[1024,256]{1,0:T(8,128)(2,1)}, bf16[1024,256]{1,0:T(8,128)(2,1)}, u32[]{:S(2)}, u32[]{:S(2)}) collective-permute-start(bf16[1024,256]{1,0:T(8,128)(2,1)} %pad_maximum_fusion.7), channel_id=1, source_target_pairs={{0,6},{2,0},{4,2},{6,4},{1,7},{3,1},{5,3},{7,5},{8,14},{10,8},{12,... | collective-permute-start | bytes 1572872 | tf_op jit(solution)/shard_map/ppermute | solution.py:53
  148.1 1.9 copy-start.1
  148.2 3.7 %copy-start.2 = (bf16[768,256]{1,0:T(8,128)(2,1)}, bf16[768,256]{1,0:T(8,128)(2,1)S(1)}, u32[]{:S(2)}) copy-start(bf16[768,256]{1,0:T(8,128)(2,1)S(1)} %get-tuple-element.26) | copy-start | bytes 1179652
  148.3 3.6 %copy-start.3 = (bf16[768,256]{1,0:T(8,128)(2,1)}, bf16[768,256]{1,0:T(8,128)(2,1)S(1)}, u32[]{:S(2)}) copy-start(bf16[768,256]{1,0:T(8,128)(2,1)S(1)} %get-tuple-element.27) | copy-start | bytes 1179652
  151.9 19.4 %collective-permute-start.3 = (bf16[768,512]{1,0:T(8,128)(2,1)}, bf16[768,512]{1,0:T(8,128)(2,1)}, u32[]{:S(2)}, u32[]{:S(2)}) collective-permute-start(bf16[768,512]{1,0:T(8,128)(2,1)} %convolution_convert_fusion), channel_id=1, source_target_pairs={{0,1},{1,0},{2,3},{3,2},{4,5},{5,4},{6,7},{7,6},{8,9},{9,8},{10,11... | collective-permute-start | bytes 2359304 | tf_op jit(solution)/shard_map/ppermute | solution.py:20
  156.4 3.1 %collective-permute-start.5 = (f32[8,768]{1,0:T(8,128)S(1)}, f32[8,768]{1,0:T(8,128)S(1)}, u32[]{:S(2)}, u32[]{:S(2)}) collective-permute-start(f32[8,768]{1,0:T(8,128)S(1)} %add.177), channel_id=1, source_target_pairs={{0,1},{1,0},{2,3},{3,2},{4,5},{5,4},{6,7},{7,6},{8,9},{9,8},{10,11... | collective-permute-start | bytes 73736 | tf_op jit(solution)/shard_map/ppermute | solution.py:20
  159.5 6.1 %collective-permute-start.6 = (f32[8,768]{1,0:T(8,128)S(1)}, f32[8,768]{1,0:T(8,128)S(1)}, u32[]{:S(2)}, u32[]{:S(2)}) collective-permute-start(f32[8,768]{1,0:T(8,128)S(1)} %add.178), channel_id=1, source_target_pairs={{0,8},{8,0},{1,9},{9,1},{2,10},{10,2},{3,11},{11,3},{4,12},{12,4},... | collective-permute-start | bytes 73736 | tf_op jit(solution)/shard_map/ppermute | solution.py:20
  166.3 30.4 %all-to-all-start.4 = ((bf16[32,8,768]{2,1,0:T(8,128)(2,1)}), bf16[32,8,768]{2,1,0:T(8,128)(2,1)S(1)}, u32[]{:S(2)}, u32[]{:S(2)}) async-start(bf16[32,8,768]{2,1,0:T(8,128)(2,1)} %broadcast_in_dim.14), calls=%async_computation.4 | async-start | bytes 786432 | tf_op jit(solution)/shard_map/all_to_all | solution.py:24
  174.1 14.8 %collective-permute-start.4 = (bf16[768,256]{1,0:T(8,128)(2,1)S(1)}, bf16[768,256]{1,0:T(8,128)(2,1)S(1)}, u32[]{:S(2)}, u32[]{:S(2)}) collective-permute-start(bf16[768,256]{1,0:T(8,128)(2,1)S(1)} %slice.108), channel_id=1, source_target_pairs={{0,8},{8,0},{1,9},{9,1},{2,10},{10,2},{3,11},{11,3},{4,12},{12,4},... | collective-permute-start | bytes 1179656 | tf_op jit(solution)/shard_map/ppermute | solution.py:20

commit v2 on v1

v2 whole, which is shorter than its diff:
```python
import functools
import math

import jax
import jax.numpy as jnp
from jax import lax
from jax.experimental import pallas as pl
from jax.experimental.pallas import tpu as pltpu
from jax.sharding import Mesh
from jax.sharding import PartitionSpec as P

EX_DEV = 24
DOCS = 256
AXES = ("zh", "zl", "yl", "yh", "x", "c")
SIZES = (4, 4, 2, 2, 4, 2)
DP = ("zh", "zl", "yl")
NEAR = ("zl", "yl")
TENSOR = ("yh", "x", "c")
BF16 = jnp.bfloat16
F32 = jnp.float32


def swap(value, axis):
    return lax.ppermute(value, axis, [(0, 1), (1, 0)])


def exchange(value, axes):
    shape = value.shape
    flat = value.reshape(shape[0] * shape[1], shape[2])
    return lax.all_to_all(flat, axes, 0, 0, tiled=True).reshape(shape)


def to_all(value, members):
    return jnp.broadcast_to(value[None], (members, *value.shape))


def split(value):
    high = lax.reduce_precision(value, 8, 7)
    return high.astype(BF16), (value - high).astype(BF16)


def dot_t(left, right):
    return lax.dot_general(left, right, (((1,), (1,)), ((), ())), preferred_element_type=F32)


def partial_kernel(first, tile, place_ref, queries_ref, *refs):
    stored, out_ref = refs[:4], refs[4]
    height, count = out_ref.shape
    x = place_ref[0]
    for start in range(0, height, tile):
        total = None
        for d in range(4):
            left = queries_ref[lax.rem(x + 4 - d, 4), pl.ds(start, tile), :]
            term = dot_t(left, stored[d][pl.ds(first, count), :])
            total = term if total is None else total + term
        out_ref[pl.ds(start, tile), :] = total.astype(out_ref.dtype)


def partial(place, queries, stored, height, first, count, dtype):
    vmem = pl.BlockSpec(memory_space=pltpu.VMEM)
    return pl.pallas_call(
        functools.partial(partial_kernel, first, 128),
        out_shape=jax.ShapeDtypeStruct((height, count), dtype),
        in_specs=[pl.BlockSpec(memory_space=pltpu.SMEM)] + [vmem] * 5,
        out_specs=vmem,
        compiler_params=pltpu.CompilerParams(vmem_limit_bytes=32 * 1024 * 1024),
        cost_estimate=pl.CostEstimate(flops=2 * height * count * 1024, bytes_accessed=5 << 20, transcendentals=0),
    )(place, queries, *stored)


def per_device(activations, out_grads, proj_in, proj_out, segment_ids, train_logs, doc_ids):
    yh, x, c = (lax.axis_index(name) for name in TENSOR)
    position = (yh * 4 + x) * 2 + c
    tokens = activations.shape[0]
    rank = proj_in.shape[1]
    logs, width = train_logs.shape

    part = jnp.concatenate(
        [
            jnp.dot(activations, proj_in, preferred_element_type=F32),
            jnp.dot(out_grads, proj_out, preferred_element_type=F32),
        ],
        axis=1,
    )
    chunk = tokens // 16
    owners = jnp.pad(doc_ids.astype(F32).reshape(-1, 2 * rank), ((0, 6), (0, 0)))
    first = jnp.concatenate([part.reshape(16, chunk, 2 * rank), to_all(owners, 16)], axis=1)
    first = exchange(first, TENSOR)
    own = jnp.sum(first[:, :chunk], axis=0).astype(BF16)
    all_owners = first[:, chunk : chunk + 2].reshape(logs).astype(jnp.int32)
    both = exchange(to_all(own, 16), TENSOR).reshape(tokens, 2 * rank)
    in_proj = both[:, :rank]
    out_proj = both[:, rank:]

    seg_row = segment_ids[0]
    labels = jnp.arange(EX_DEV, dtype=jnp.int32)
    hot = seg_row[:, None] == labels[None, :]
    counts = jnp.sum(hot.astype(F32), axis=0)
    block_rank = rank // 16
    own_out = lax.dynamic_slice_in_dim(out_proj, position * block_rank, block_rank, 1)
    masked = (hot.astype(BF16)[:, :, None] * own_out[:, None, :]).reshape(tokens, EX_DEV * block_rank)
    log_sums = jnp.einsum("ta,tj->aj", masked, in_proj, preferred_element_type=F32)
    query_block = (log_sums.reshape(EX_DEV, block_rank * rank) / counts[:, None]).astype(BF16)

    doc_hot = (jnp.arange(DOCS, dtype=jnp.int32)[:, None] == all_owners[None, :]).astype(BF16)
    high, low = split(jnp.dot(doc_hot, train_logs, preferred_element_type=F32))
    far = jnp.concatenate(
        [to_all(query_block, 4), high.reshape(4, DOCS // 4, width), low.reshape(4, DOCS // 4, width)], axis=1
    )

    blocks = train_logs.reshape(2, 4, 2, logs // 16, width)

    def rows_for(target):
        def block(row, col):
            return lax.dynamic_slice(blocks, (row, target, col, 0, 0), (1, 1, 1, logs // 16, width)).reshape(logs // 16, width)

        return jnp.concatenate([block(1 - yh, 1 - c), block(yh, 1 - c), block(1 - yh, c), block(yh, c)])

    far, *moving = lax.optimization_barrier((far, *(rows_for((x + d) % 4) for d in range(1, 4))))
    far = exchange(far, "zh")
    stored = [rows_for(x)]
    for d in range(1, 4):
        stored.append(lax.ppermute(moving[d - 1], "x", [(i, (i + d) % 4) for i in range(4)]))

    docs = jnp.sum(far[:, EX_DEV:].astype(F32), axis=0)
    high, low = split(docs[: DOCS // 4] + docs[DOCS // 4 :])
    own_docs = DOCS // 32
    near = jnp.concatenate(
        [
            to_all(far[:, :EX_DEV].reshape(4 * EX_DEV, width), 8),
            high.reshape(8, own_docs, width),
            low.reshape(8, own_docs, width),
        ],
        axis=1,
    )
    near, stored[1], stored[3] = lax.optimization_barrier((near, stored[1], stored[3]))
    near = exchange(near, NEAR)
    queries = near[:, : 4 * EX_DEV].reshape(8, 4, EX_DEV, width).transpose(1, 0, 2, 3).reshape(32 * EX_DEV, width)
    docs = jnp.sum(near[:, 4 * EX_DEV :].astype(F32), axis=0)
    high, low = split(docs[:own_docs] + docs[own_docs:])
    doc_part = dot_t(high, queries) + dot_t(low, queries)

    height = queries.shape[0]
    high, low = split(doc_part)
    third = jnp.concatenate([queries, high.reshape(-1, width), low.reshape(-1, width)])
    third, *stored = lax.optimization_barrier((third, *stored))
    third = exchange(to_all(third, 4), "x")
    doc_part = jnp.sum(third[:, height:].astype(F32), axis=0).reshape(2, own_docs, height)
    doc_part = doc_part[0] + doc_part[1]
    doc_part = doc_part + swap(doc_part, "c")
    doc_part = doc_part + swap(doc_part, "yh")

    place = x.reshape(1)
    half = logs // 8
    away = swap(partial(place, third, stored, height, 0, half, BF16), "c")
    kept = partial(place, third, stored, height, half, half, F32) + away.astype(F32)
    quarter = half // 2
    beyond = swap(kept[:, :quarter].astype(BF16), "yh")
    scores = (kept[:, quarter:] + beyond.astype(F32)) * 0.125

    scale = 0.125 / math.sqrt(logs * 32 / DOCS)
    own_half = lax.dynamic_slice_in_dim(doc_part, c * (height // 2), height // 2, 1)
    final = exchange(to_all((own_half * scale).astype(BF16), 32), DP).reshape(DOCS, height // 2)
    final = lax.all_gather(final, "c", axis=0)
    doc_influence = final.transpose(0, 2, 1).reshape(height, DOCS).astype(F32)
    return (scores, doc_influence)


def solution(mesh):
    inner = Mesh(mesh.devices.reshape(SIZES), AXES)
    placed = (
        P(DP, TENSOR),
        P(DP, TENSOR),
        P(TENSOR, None),
        P(TENSOR, None),
        P(DP, None),
        P(DP, TENSOR),
        P(AXES),
    )
    return jax.shard_map(
        per_device,
        mesh=inner,
        in_specs=placed,
        out_specs=(P(None, AXES), P()),
        check_vma=False,
    )
```

time: 200 us -> 174 us (0.87)
  waiting for transfers between devices: 104 us -> 43.3 us
  blocking collectives: 0 us -> 27 us
  starting transfers between devices: 61.2 us -> 68.7 us
  Pallas kernels: 0 us -> 5.16 us
  matrix products: 10.5 us -> 5.52 us
  local copies, waits for them, and re-layouts: 8.94 us -> 11.2 us
    all_to_all x5, waiting for transfers between devices: 61.8 us -> 36.6 us  [exchange(): return lax.all_to_all(flat, axes, 0, 0, tiled=True).reshape(shape)]
    ppermute x3, waiting for transfers between devices: 27.8 us -> 2.75 us  [per_device(): lax.ppermute(moving[d - 1], 'x', [(i, (i + d) % 4) for i in range(4)])]
    all_to_all x0 -> x1, blocking collectives: none -> 21.6 us  [exchange(): return lax.all_to_all(flat, axes, 0, 0, tiled=True).reshape(shape)]
    ppermute x4, waiting for transfers between devices: 14.8 us -> 4 us  [swap(): return lax.ppermute(value, axis, [(0, 1), (1, 0)])]
    all_to_all x5, starting transfers between devices: 36.9 us -> 44.7 us  [exchange(): return lax.all_to_all(flat, axes, 0, 0, tiled=True).reshape(shape)]
    all_gather x0 -> x1, blocking collectives: none -> 5.42 us  [per_device(): final = lax.all_gather(final, 'c', axis=0)]
    pallas_call x0 -> x2, Pallas kernels: none -> 5.16 us  [partial(): pl.pallas_call(functools.partial(partial_kernel, first, 128), out_shape=j...]
    concatenate x5 -> x4, other arithmetic: 7.04 us -> 2.43 us  [the longest x1 0.86 us: per_device(): jnp.concatenate([part.reshape(16, chunk, 2 * rank), to_all(owners, 16)],...]
  transfers between devices with their start and end apart: 12 -> 12, of which waited for: 10 -> 10; matrix products, arithmetic and copies ran while one was open for 8% -> 8% of each run, Pallas kernels for 0% -> 1%
where the time goes in v2:
time: 174 us; the launch traced here: 173 us
  starting transfers between devices  68.7 us (39%)
  waiting for transfers between devices  43.3 us (25%)
  blocking collectives  27 us (16%)
  local copies, waits for them, and re-layouts  11.2 us (6%)
  other arithmetic  10.9 us (6%)
  matrix products  5.52 us (3%)
  Pallas kernels  5.16 us (3%)
    all_to_all x5, starting transfers between devices, exchange(): return lax.all_to_all(flat, axes, 0, 0, tiled=True).reshape(shape)  44.7 us
    all_to_all x5, waiting for transfers between devices, exchange(): return lax.all_to_all(flat, axes, 0, 0, tiled=True).reshape(shape)  36.6 us
    all_to_all x1, blocking collectives, exchange(): return lax.all_to_all(flat, axes, 0, 0, tiled=True).reshape(shape)  21.6 us
    ppermute x4, starting transfers between devices, swap(): return lax.ppermute(value, axis, [(0, 1), (1, 0)])  14.3 us
    ppermute x3, starting transfers between devices, per_device(): lax.ppermute(moving[d - 1], 'x', [(i, (i + d) % 4) for i in range(4)])  9.61 us
    all_gather x1, blocking collectives, per_device(): final = lax.all_gather(final, 'c', axis=0)  5.42 us
    pallas_call x2, Pallas kernels, partial(): pl.pallas_call(functools.partial(partial_kernel, first, 128), out_shape=j...  5.16 us
    unnamed x24, local copies, waits for them, and re-layouts  4.33 us
  transfers between devices with their start and end apart: 12, of which 10 were waited for; matrix products, arithmetic and copies ran while one was open for 8% of the time, Pallas kernels for 1%

profile of v2, /device:TPU:1, one launch (start us, length us, event | category | flops | bytes accessed | tf_op | source)
XLA Modules:
  0.0 172.8 jit_solution(12609251329769605495)
XLA Ops:
  0.7 0.8 convert_bitcast_fusion
  1.5 0.4 copy-done
  1.9 1.3 fusion.17
  3.2 1.3 fusion.16
  4.5 0.2 copy.16
  4.7 0.9 pad_maximum_fusion
  5.6 10.3 %all-to-all-start = ((f32[16,72,128]{2,1,0:T(8,128)}), f32[16,72,128]{2,1,0:T(8,128)S(1)}, u32[]{:S(2)}, u32[]{:S(2)}) async-start(f32[16,72,128]{2,1,0:T(8,128)} %pad_maximum_fusion), calls=%async_computation | async-start | bytes 1179648 | tf_op jit(solution)/shard_map/all_to_all | solution.py:30
  15.8 2.5 %dynamic-slice_bitcast_fusion.3 = (bf16[256,256]{1,0:T(8,128)(2,1)S(1)}, bf16[256,256]{1,0:T(8,128)(2,1)S(1)}, bf16[256,256]{1,0:T(8,128)(2,1)S(1)}, bf16[256,25...) fusion(bf16[2,4,2,256,256]{4,3,2,1,0:T(8,128)(2,1)} %bitcast.70, ...), kind=kLoop, calls=%fused_computation.28 | loop fusion | bytes 4194336 | tf_op jit(solution)/shard_map/reshape | solution.py:115
  18.3 0.1 convert_reduce_fusion.3
  18.5 1.0 pad_maximum_fusion.2
  19.5 8.6 %all-to-all-done = f32[16,72,128]{2,1,0:T(8,128)S(1)} async-done(((f32[16,72,128]{2,1,0:T(8,128)}), f32[16,72,128]{2,1,0:T(8,128)S(1)}, u32[]{:S(2)}, u32[]{:S(2)}) %all-to-all-start) | async-done | bytes 589856 | tf_op jit(solution)/shard_map/all_to_all | solution.py:30
  28.1 0.8 broadcast_in_dim.15
  28.9 4.3 %all-to-all-start.1 = ((bf16[16,64,128]{2,1,0:T(8,128)(2,1)}), bf16[16,64,128]{2,1,0:T(8,128)(2,1)S(1)}, u32[]{:S(2)}, u32[]{:S(2)}) async-start(bf16[16,64,128]{2,1,0:T(8,128)(2,1)} %broadcast_in_dim.15), calls=%async_computation.1 | async-start | bytes 524288 | tf_op jit(solution)/shard_map/all_to_all | solution.py:30
  33.2 2.3 %reduce-precision_convert_fusion = (bf16[256,256]{1,0:T(8,128)(2,1)S(1)}, bf16[256,256]{1,0:T(8,128)(2,1)S(1)}) fusion(bf16[4096,256]{1,0:T(8,128)(2,1)} %param.12, s32[4096]{0:T(1024)S(1)} %bitcast.78), kind=kOutput, calls=%fused_computation.19 | convolution fusion | flops 538181632 | bytes 2375680 | tf_op jit(solution)/shard_map/dot_general | solution.py:106
  35.5 6.4 %all-to-all-done.1 = bf16[16,64,128]{2,1,0:T(8,128)(2,1)S(1)} async-done(((bf16[16,64,128]{2,1,0:T(8,128)(2,1)}), bf16[16,64,128]{2,1,0:T(8,128)(2,1)S(1)}, u32[]{:S(2)}, u32[]{:S(2)}) %all-to-all-start.1) | async-done | bytes 262176 | tf_op jit(solution)/shard_map/all_to_all | solution.py:30
  41.9 0.1 slice.72
  42.1 0.1 constant_dynamic-slice_fusion
  42.2 0.1 copy.17
  42.3 0.1 broadcast_multiply_fusion
  42.5 0.1 mul.47
  42.5 0.2 fusion.4
  42.7 0.1 reshape.197
  42.8 0.1 divide_convert_fusion
  42.9 0.7 pad_maximum_fusion.8
  43.6 12.9 %all-to-all-start.2 = ((bf16[4,152,256]{2,1,0:T(8,128)(2,1)}), bf16[4,152,256]{2,1,0:T(8,128)(2,1)S(1)}, u32[]{:S(2)}, u32[]{:S(2)}) async-start(bf16[4,152,256]{2,1,0:T(8,128)(2,1)} %pad_maximum_fusion.8), calls=%async_computation.2 | async-start | bytes 622592 | tf_op jit(solution)/shard_map/all_to_all | solution.py:30
  56.6 2.2 %collective-permute-start = (bf16[1024,256]{1,0:T(8,128)(2,1)}, bf16[1024,256]{1,0:T(8,128)(2,1)S(1)}, u32[]{:S(2)}, u32[]{:S(2)}) collective-permute-start(bf16[1024,256]{1,0:T(8,128)(2,1)} %get-tuple-element.15), channel_id=1, source_target_pairs={{0,2},{2,4},{4,6},{6,0},{1,3},{3,5},{5,7},{7,1},{8,10},{10,12},{12... | collective-permute-start | bytes 1572872 | tf_op jit(solution)/shard_map/ppermute | solution.py:123
  58.8 4.3 %collective-permute-start.1 = (bf16[1024,256]{1,0:T(8,128)(2,1)S(1)}, bf16[1024,256]{1,0:T(8,128)(2,1)S(1)}, u32[]{:S(2)}, u32[]{:S(2)}) collective-permute-start(bf16[1024,256]{1,0:T(8,128)(2,1)S(1)} %pad_maximum_fusion.4), channel_id=1, source_target_pairs={{0,6},{2,0},{4,2},{6,4},{1,7},{3,1},{5,3},{7,5},{8,14},{10,8},{12,... | collective-permute-start | bytes 1572872 | tf_op jit(solution)/shard_map/ppermute | solution.py:123
  63.1 7.8 %all-to-all-done.2 = bf16[4,152,256]{2,1,0:T(8,128)(2,1)S(1)} async-done(((bf16[4,152,256]{2,1,0:T(8,128)(2,1)}), bf16[4,152,256]{2,1,0:T(8,128)(2,1)S(1)}, u32[]{:S(2)}, u32[]{:S(2)}) %all-to-all-start.2) | async-done | bytes 311328 | tf_op jit(solution)/shard_map/all_to_all | solution.py:30
  70.9 0.8 pad_maximum_fusion.6
  71.7 0.5 collective-permute-done.refs_1_
  72.2 1.1 collective-permute-done.1.refs_3_
  73.3 9.1 %all-to-all-start.3 = ((bf16[8,112,256]{2,1,0:T(8,128)(2,1)}), bf16[8,112,256]{2,1,0:T(8,128)(2,1)}, u32[]{:S(2)}, u32[]{:S(2)}) async-start(bf16[8,112,256]{2,1,0:T(8,128)(2,1)} %pad_maximum_fusion.6), calls=%async_computation.3 | async-start | bytes 917504 | tf_op jit(solution)/shard_map/all_to_all | solution.py:30
  82.4 0.9 pad_maximum_fusion.5.refs_0_
  83.3 3.1 %collective-permute-start.2 = (bf16[1024,256]{1,0:T(8,128)(2,1)}, bf16[1024,256]{1,0:T(8,128)(2,1)S(1)}, u32[]{:S(2)}, u32[]{:S(2)}) collective-permute-start(bf16[1024,256]{1,0:T(8,128)(2,1)} %get-tuple-element.19), channel_id=1, source_target_pairs={{0,4},{2,6},{4,0},{6,2},{1,5},{3,7},{5,1},{7,3},{8,12},{10,14},{12... | collective-permute-start | bytes 1572872 | tf_op jit(solution)/shard_map/ppermute | solution.py:123
  86.5 8.4 %all-to-all-done.3 = bf16[8,112,256]{2,1,0:T(8,128)(2,1)} async-done(((bf16[8,112,256]{2,1,0:T(8,128)(2,1)}), bf16[8,112,256]{2,1,0:T(8,128)(2,1)}, u32[]{:S(2)}, u32[]{:S(2)}) %all-to-all-start.3) | async-done | bytes 458784 | tf_op jit(solution)/shard_map/all_to_all | solution.py:30
  94.9 1.0 slice.79
  95.9 0.9 convert_reduce_fusion.2
  96.8 0.2 fusion.15
  97.0 0.3 reduce-precision_convert_fusion.2
  97.3 0.1 reshape.218
  97.4 1.2 collective-permute-done.2.refs_2_
  98.6 0.8 copy-done.7
  99.4 0.1 broadcast_in_dim.19
  99.5 21.6 %all_to_all.39.queries_ref = bf16[4,816,256]{2,1,0:T(8,128)(2,1)S(1)} all-to-all(bf16[4,816,256]{2,1,0:T(8,128)(2,1)S(1)} %broadcast_in_dim.19), channel_id=1, replica_groups=mesh['zh'=4,'zl'=4,'yl'=2,'yh'=2,'x'=4,'c'=2] {'x'}, dimensions={0} | all-to-all | bytes 3342336 | tf_op jit(solution)/shard_map/all_to_all | solution.py:30
  121.1 3.0 %shard_map.87 = bf16[768,512]{1,0:T(8,128)(2,1)} custom-call(s32[1]{0:T(128)} %bitcast.place_ref, bf16[4,816,256]{2,1,0:T(8,128)(2,1)S(1)} %all_to_all.39.queries_ref, bf16[1024,256]{1,0:T(8,128)(2,1)S(1)} %pad_maximum_fusion.5.refs_0_, bf16[1024,256]{1,0:T(8,128)(2,1)S(1)} %copy-done.2, bf16[1024,256]{1,0:T(8,128)(2,1)S(1)} %copy-done.8, ...), custom_call_target="tpu_custom_call" | custom-call | flops 805306368 | bytes 5242880 | tf_op jit(solution)/shard_map/pallas_call | solution.py:61
  124.1 5.7 %collective-permute-start.3 = (bf16[768,512]{1,0:T(8,128)(2,1)}, bf16[768,512]{1,0:T(8,128)(2,1)}, u32[]{:S(2)}, u32[]{:S(2)}) collective-permute-start(bf16[768,512]{1,0:T(8,128)(2,1)} %shard_map.87), channel_id=1, source_target_pairs={{0,1},{1,0},{2,3},{3,2},{4,5},{5,4},{6,7},{7,6},{8,9},{9,8},{10,11... | collective-permute-start | bytes 2359304 | tf_op jit(solution)/shard_map/ppermute | solution.py:24
  129.9 1.9 %collective-permute-start.5 = (f32[8,768]{1,0:T(8,128)S(1)}, f32[8,768]{1,0:T(8,128)S(1)}, u32[]{:S(2)}, u32[]{:S(2)}) collective-permute-start(f32[8,768]{1,0:T(8,128)S(1)} %add.149), channel_id=1, source_target_pairs={{0,1},{1,0},{2,3},{3,2},{4,5},{5,4},{6,7},{7,6},{8,9},{9,8},{10,11... | collective-permute-start | bytes 73736 | tf_op jit(solution)/shard_map/ppermute | solution.py:24
  131.8 1.2 collective-permute-done.5
  133.0 3.2 %collective-permute-start.6 = (f32[8,768]{1,0:T(8,128)S(1)}, f32[8,768]{1,0:T(8,128)S(1)}, u32[]{:S(2)}, u32[]{:S(2)}) collective-permute-start(f32[8,768]{1,0:T(8,128)S(1)} %add.150), channel_id=1, source_target_pairs={{0,8},{8,0},{1,9},{9,1},{2,10},{10,2},{3,11},{11,3},{4,12},{12,4},... | collective-permute-start | bytes 73736 | tf_op jit(solution)/shard_map/ppermute | solution.py:24
  136.2 2.8 %collective-permute-done.6 = f32[8,768]{1,0:T(8,128)S(1)} collective-permute-done((f32[8,768]{1,0:T(8,128)S(1)}, f32[8,768]{1,0:T(8,128)S(1)}, u32[]{:S(2)}, u32[]{:S(2)}) %collective-permute-start.6) | collective-permute-done | bytes 24608 | tf_op jit(solution)/shard_map/ppermute | solution.py:24
  139.0 0.7 broadcast_in_dim.20
  139.7 8.2 %all-to-all-start.5 = ((bf16[32,8,384]{2,1,0:T(8,128)(2,1)}), bf16[32,8,384]{2,1,0:T(8,128)(2,1)S(1)}, u32[]{:S(2)}, u32[]{:S(2)}) async-start(bf16[32,8,384]{2,1,0:T(8,128)(2,1)} %broadcast_in_dim.20), calls=%async_computation.5 | async-start | bytes 393216 | tf_op jit(solution)/shard_map/all_to_all | solution.py:30
  147.9 1.0 copy-done.3
  149.0 1.0 copy-done.6
  150.0 1.0 copy-done.9
  151.0 2.1 %shard_map.86 = f32[768,512]{1,0:T(8,128)S(1)} custom-call(s32[1]{0:T(128)} %bitcast.place_ref, bf16[4,816,256]{2,1,0:T(8,128)(2,1)S(1)} %all_to_all.39.queries_ref, bf16[1024,256]{1,0:T(8,128)(2,1)S(1)} %pad_maximum_fusion.5.refs_0_, bf16[1024,256]{1,0:T(8,128)(2,1)S(1)} %copy-done.3, bf16[1024,256]{1,0:T(8,128)(2,1)S(1)} %copy-done.9, ...), custom_call_target="tpu_custom_call" | custom-call | flops 805306368 | bytes 5242880 | tf_op jit(solution)/shard_map/pallas_call | solution.py:61
  153.2 1.4 convert_add_fusion
  154.6 0.8 slice.125
  155.4 3.5 %collective-permute-start.4 = (bf16[768,256]{1,0:T(8,128)(2,1)}, bf16[768,256]{1,0:T(8,128)(2,1)}, u32[]{:S(2)}, u32[]{:S(2)}) collective-permute-start(bf16[768,256]{1,0:T(8,128)(2,1)} %slice.125), channel_id=1, source_target_pairs={{0,8},{8,0},{1,9},{9,1},{2,10},{10,2},{3,11},{11,3},{4,12},{12,4},... | collective-permute-start | bytes 1179656 | tf_op jit(solution)/shard_map/ppermute | solution.py:24
  158.9 5.4 %all-to-all-done.5 = bf16[32,8,384]{2,1,0:T(8,128)(2,1)S(1)} async-done(((bf16[32,8,384]{2,1,0:T(8,128)(2,1)}), bf16[32,8,384]{2,1,0:T(8,128)(2,1)S(1)}, u32[]{:S(2)}, u32[]{:S(2)}) %all-to-all-start.5) | async-done | bytes 196640 | tf_op jit(solution)/shard_map/all_to_all | solution.py:30
  164.3 5.4 %all_gather.3 = bf16[2,256,384]{2,1,0:T(8,128)(2,1)S(1)} all-gather(bf16[1,256,384]{2,1,0:T(8,128)(2,1)S(1)} %bitcast.74), channel_id=1, replica_groups=mesh['zh'=4,'zl'=4,'yl'=2,'yh'=2,'x'=4,'c'=2] {'c'}, dimensions={0}, use_global_device_ids=true | all-gather | bytes 589824 | tf_op jit(solution)/shard_map/all_gather | solution.py:164
  169.7 0.2 copy.20
  169.9 0.9 convert_element_type.117
  170.8 2.0 %fusion.2 = f32[768,256]{1,0:T(8,128)} fusion(f32[768,512]{1,0:T(8,128)S(1)} %convert_add_fusion, bf16[768,256]{1,0:T(8,128)(2,1)} %collective-permute-done.4), kind=kLoop, calls=%fused_computation.7 | loop fusion | flops 589824 | bytes 1966080 | tf_op jit(solution)/shard_map/mul | solution.py:159
  (41 shorter events, 0.4 us)
Async XLA Ops:
  0.6 1.2 copy-start
  0.6 2.5 %copy-start.10 = (bf16[1024,512]{1,0:T(8,128)(2,1)S(1)}, bf16[1024,512]{1,0:T(8,128)(2,1)}, u32[]{:S(2)}) copy-start(bf16[1024,512]{1,0:T(8,128)(2,1)} %param.7) | copy-start | bytes 3145732
  5.6 22.5 %all-to-all-start = ((f32[16,72,128]{2,1,0:T(8,128)}), f32[16,72,128]{2,1,0:T(8,128)S(1)}, u32[]{:S(2)}, u32[]{:S(2)}) async-start(f32[16,72,128]{2,1,0:T(8,128)} %pad_maximum_fusion), calls=%async_computation | async-start | bytes 1179648 | tf_op jit(solution)/shard_map/all_to_all | solution.py:30
  15.8 2.5 %copy-start.11 = (s32[1,1024]{1,0:T(1,128)S(1)}, s32[1,1024]{1,0:T(1,128)}, u32[]{:S(2)}) copy-start(s32[1,1024]{1,0:T(1,128)} %param.11) | copy-start | bytes 12292
  28.9 13.1 %all-to-all-start.1 = ((bf16[16,64,128]{2,1,0:T(8,128)(2,1)}), bf16[16,64,128]{2,1,0:T(8,128)(2,1)S(1)}, u32[]{:S(2)}, u32[]{:S(2)}) async-start(bf16[16,64,128]{2,1,0:T(8,128)(2,1)} %broadcast_in_dim.15), calls=%async_computation.1 | async-start | bytes 524288 | tf_op jit(solution)/shard_map/all_to_all | solution.py:30
  43.6 27.2 %all-to-all-start.2 = ((bf16[4,152,256]{2,1,0:T(8,128)(2,1)}), bf16[4,152,256]{2,1,0:T(8,128)(2,1)S(1)}, u32[]{:S(2)}, u32[]{:S(2)}) async-start(bf16[4,152,256]{2,1,0:T(8,128)(2,1)} %pad_maximum_fusion.8), calls=%async_computation.2 | async-start | bytes 622592 | tf_op jit(solution)/shard_map/all_to_all | solution.py:30
  56.6 15.6 %collective-permute-start = (bf16[1024,256]{1,0:T(8,128)(2,1)}, bf16[1024,256]{1,0:T(8,128)(2,1)S(1)}, u32[]{:S(2)}, u32[]{:S(2)}) collective-permute-start(bf16[1024,256]{1,0:T(8,128)(2,1)} %get-tuple-element.15), channel_id=1, source_target_pairs={{0,2},{2,4},{4,6},{6,0},{1,3},{3,5},{5,7},{7,1},{8,10},{10,12},{12... | collective-permute-start | bytes 1572872 | tf_op jit(solution)/shard_map/ppermute | solution.py:123
  58.8 14.5 %collective-permute-start.1 = (bf16[1024,256]{1,0:T(8,128)(2,1)S(1)}, bf16[1024,256]{1,0:T(8,128)(2,1)S(1)}, u32[]{:S(2)}, u32[]{:S(2)}) collective-permute-start(bf16[1024,256]{1,0:T(8,128)(2,1)S(1)} %pad_maximum_fusion.4), channel_id=1, source_target_pairs={{0,6},{2,0},{4,2},{6,4},{1,7},{3,1},{5,3},{7,5},{8,14},{10,8},{12,... | collective-permute-start | bytes 1572872 | tf_op jit(solution)/shard_map/ppermute | solution.py:123
  72.2 23.7 %copy-start.1 = (bf16[1024,256]{1,0:T(8,128)(2,1)}, bf16[1024,256]{1,0:T(8,128)(2,1)S(1)}, u32[]{:S(2)}) copy-start(bf16[1024,256]{1,0:T(8,128)(2,1)S(1)} %collective-permute-done.refs_1_) | copy-start | bytes 1572868
  73.3 22.7 %copy-start.4 = (bf16[1024,256]{1,0:T(8,128)(2,1)}, bf16[1024,256]{1,0:T(8,128)(2,1)S(1)}, u32[]{:S(2)}) copy-start(bf16[1024,256]{1,0:T(8,128)(2,1)S(1)} %collective-permute-done.1.refs_3_) | copy-start | bytes 1572868
  73.3 21.6 %all-to-all-start.3 = ((bf16[8,112,256]{2,1,0:T(8,128)(2,1)}), bf16[8,112,256]{2,1,0:T(8,128)(2,1)}, u32[]{:S(2)}, u32[]{:S(2)}) async-start(bf16[8,112,256]{2,1,0:T(8,128)(2,1)} %pad_maximum_fusion.6), calls=%async_computation.3 | async-start | bytes 917504 | tf_op jit(solution)/shard_map/all_to_all | solution.py:30
  83.3 15.3 %collective-permute-start.2 = (bf16[1024,256]{1,0:T(8,128)(2,1)}, bf16[1024,256]{1,0:T(8,128)(2,1)S(1)}, u32[]{:S(2)}, u32[]{:S(2)}) collective-permute-start(bf16[1024,256]{1,0:T(8,128)(2,1)} %get-tuple-element.19), channel_id=1, source_target_pairs={{0,4},{2,6},{4,0},{6,2},{1,5},{3,7},{5,1},{7,3},{8,12},{10,14},{12... | collective-permute-start | bytes 1572872 | tf_op jit(solution)/shard_map/ppermute | solution.py:123
  98.6 0.8 copy-start.7
  99.5 21.6 %copy-start.2 = (bf16[1024,256]{1,0:T(8,128)(2,1)S(1)}, bf16[1024,256]{1,0:T(8,128)(2,1)}, u32[]{:S(2)}) copy-start(bf16[1024,256]{1,0:T(8,128)(2,1)} %copy-done.1) | copy-start | bytes 1572868
  99.5 21.6 %copy-start.5 = (bf16[1024,256]{1,0:T(8,128)(2,1)S(1)}, bf16[1024,256]{1,0:T(8,128)(2,1)}, u32[]{:S(2)}) copy-start(bf16[1024,256]{1,0:T(8,128)(2,1)} %copy-done.4) | copy-start | bytes 1572868
  99.5 21.6 %copy-start.8 = (bf16[1024,256]{1,0:T(8,128)(2,1)S(1)}, bf16[1024,256]{1,0:T(8,128)(2,1)}, u32[]{:S(2)}) copy-start(bf16[1024,256]{1,0:T(8,128)(2,1)} %copy-done.7) | copy-start | bytes 1572868
  124.1 29.1 %collective-permute-start.3 = (bf16[768,512]{1,0:T(8,128)(2,1)}, bf16[768,512]{1,0:T(8,128)(2,1)}, u32[]{:S(2)}, u32[]{:S(2)}) collective-permute-start(bf16[768,512]{1,0:T(8,128)(2,1)} %shard_map.87), channel_id=1, source_target_pairs={{0,1},{1,0},{2,3},{3,2},{4,5},{5,4},{6,7},{7,6},{8,9},{9,8},{10,11... | collective-permute-start | bytes 2359304 | tf_op jit(solution)/shard_map/ppermute | solution.py:24
  129.9 3.1 %collective-permute-start.5 = (f32[8,768]{1,0:T(8,128)S(1)}, f32[8,768]{1,0:T(8,128)S(1)}, u32[]{:S(2)}, u32[]{:S(2)}) collective-permute-start(f32[8,768]{1,0:T(8,128)S(1)} %add.149), channel_id=1, source_target_pairs={{0,1},{1,0},{2,3},{3,2},{4,5},{5,4},{6,7},{7,6},{8,9},{9,8},{10,11... | collective-permute-start | bytes 73736 | tf_op jit(solution)/shard_map/ppermute | solution.py:24
  133.0 6.1 %collective-permute-start.6 = (f32[8,768]{1,0:T(8,128)S(1)}, f32[8,768]{1,0:T(8,128)S(1)}, u32[]{:S(2)}, u32[]{:S(2)}) collective-permute-start(f32[8,768]{1,0:T(8,128)S(1)} %add.150), channel_id=1, source_target_pairs={{0,8},{8,0},{1,9},{9,1},{2,10},{10,2},{3,11},{11,3},{4,12},{12,4},... | collective-permute-start | bytes 73736 | tf_op jit(solution)/shard_map/ppermute | solution.py:24
  139.7 24.6 %all-to-all-start.5 = ((bf16[32,8,384]{2,1,0:T(8,128)(2,1)}), bf16[32,8,384]{2,1,0:T(8,128)(2,1)S(1)}, u32[]{:S(2)}, u32[]{:S(2)}) async-start(bf16[32,8,384]{2,1,0:T(8,128)(2,1)} %broadcast_in_dim.20), calls=%async_computation.5 | async-start | bytes 393216 | tf_op jit(solution)/shard_map/all_to_all | solution.py:30
  147.9 1.0 copy-start.3
  149.0 1.0 copy-start.6
  150.0 1.0 copy-start.9
  155.4 15.5 %collective-permute-start.4 = (bf16[768,256]{1,0:T(8,128)(2,1)}, bf16[768,256]{1,0:T(8,128)(2,1)}, u32[]{:S(2)}, u32[]{:S(2)}) collective-permute-start(bf16[768,256]{1,0:T(8,128)(2,1)} %slice.125), channel_id=1, source_target_pairs={{0,8},{8,0},{1,9},{9,1},{2,10},{10,2},{3,11},{11,3},{4,12},{12,4},... | collective-permute-start | bytes 1179656 | tf_op jit(solution)/shard_map/ppermute | solution.py:24

commit v3 on v2

--- a/solution.py
+++ b/solution.py
@@ -43,28 +43,30 @@
     return lax.dot_general(left, right, (((1,), (1,)), ((), ())), preferred_element_type=F32)
 
 
-def partial_kernel(first, tile, place_ref, queries_ref, *refs):
-    stored, out_ref = refs[:4], refs[4]
-    height, count = out_ref.shape
+def partial_kernel(tile, place_ref, queries_ref, *refs):
+    stored, (away_ref, kept_ref) = refs[:4], refs[4:]
+    height, half = away_ref.shape
     x = place_ref[0]
-    for start in range(0, height, tile):
-        total = None
-        for d in range(4):
-            left = queries_ref[lax.rem(x + 4 - d, 4), pl.ds(start, tile), :]
-            term = dot_t(left, stored[d][pl.ds(first, count), :])
-            total = term if total is None else total + term
-        out_ref[pl.ds(start, tile), :] = total.astype(out_ref.dtype)
+    for first, out_ref in ((0, away_ref), (half, kept_ref)):
+        for start in range(0, height, tile):
+            total = None
+            for d in range(4):
+                left = queries_ref[lax.rem(x + 4 - d, 4), pl.ds(start, tile), :]
+                term = dot_t(left, stored[d][pl.ds(first, half), :])
+                total = term if total is None else total + term
+            out_ref[pl.ds(start, tile), :] = total.astype(out_ref.dtype)
 
 
-def partial(place, queries, stored, height, first, count, dtype):
+def partial(place, queries, stored):
+    height, half = queries.shape[1], stored[0].shape[0] // 2
     vmem = pl.BlockSpec(memory_space=pltpu.VMEM)
     return pl.pallas_call(
-        functools.partial(partial_kernel, first, 128),
-        out_shape=jax.ShapeDtypeStruct((height, count), dtype),
+        functools.partial(partial_kernel, 128),
+        out_shape=(jax.ShapeDtypeStruct((height, half), BF16), jax.ShapeDtypeStruct((height, half), F32)),
         in_specs=[pl.BlockSpec(memory_space=pltpu.SMEM)] + [vmem] * 5,
-        out_specs=vmem,
+        out_specs=(vmem, vmem),
         compiler_params=pltpu.CompilerParams(vmem_limit_bytes=32 * 1024 * 1024),
-        cost_estimate=pl.CostEstimate(flops=2 * height * count * 1024, bytes_accessed=5 << 20, transcendentals=0),
+        cost_estimate=pl.CostEstimate(flops=1024, bytes_accessed=1024, transcendentals=0),
     )(place, queries, *stored)
 
 
@@ -103,10 +105,8 @@
     query_block = (log_sums.reshape(EX_DEV, block_rank * rank) / counts[:, None]).astype(BF16)
 
     doc_hot = (jnp.arange(DOCS, dtype=jnp.int32)[:, None] == all_owners[None, :]).astype(BF16)
-    high, low = split(jnp.dot(doc_hot, train_logs, preferred_element_type=F32))
-    far = jnp.concatenate(
-        [to_all(query_block, 4), high.reshape(4, DOCS // 4, width), low.reshape(4, DOCS // 4, width)], axis=1
-    )
+    doc_sums = jnp.dot(doc_hot, train_logs, preferred_element_type=F32).astype(BF16)
+    far = jnp.concatenate([to_all(query_block, 4), doc_sums.reshape(4, DOCS // 4, width)], axis=1)
 
     blocks = train_logs.reshape(2, 4, 2, logs // 16, width)
 
@@ -123,7 +123,7 @@
         stored.append(lax.ppermute(moving[d - 1], "x", [(i, (i + d) % 4) for i in range(4)]))
 
     docs = jnp.sum(far[:, EX_DEV:].astype(F32), axis=0)
-    high, low = split(docs[: DOCS // 4] + docs[DOCS // 4 :])
+    high, low = split(docs)
     own_docs = DOCS // 32
     near = jnp.concatenate(
         [
@@ -133,7 +133,7 @@
         ],
         axis=1,
     )
-    near, stored[1], stored[3] = lax.optimization_barrier((near, stored[1], stored[3]))
+    near, stored[2] = lax.optimization_barrier((near, stored[2]))
     near = exchange(near, NEAR)
     queries = near[:, : 4 * EX_DEV].reshape(8, 4, EX_DEV, width).transpose(1, 0, 2, 3).reshape(32 * EX_DEV, width)
     docs = jnp.sum(near[:, 4 * EX_DEV :].astype(F32), axis=0)
@@ -141,26 +141,30 @@
     doc_part = dot_t(high, queries) + dot_t(low, queries)
 
     height = queries.shape[0]
-    high, low = split(doc_part)
-    third = jnp.concatenate([queries, high.reshape(-1, width), low.reshape(-1, width)])
-    third, *stored = lax.optimization_barrier((third, *stored))
+    third, doc_part, stored[1], stored[3] = lax.optimization_barrier((queries, doc_part, stored[1], stored[3]))
     third = exchange(to_all(third, 4), "x")
-    doc_part = jnp.sum(third[:, height:].astype(F32), axis=0).reshape(2, own_docs, height)
-    doc_part = doc_part[0] + doc_part[1]
-    doc_part = doc_part + swap(doc_part, "c")
-    doc_part = doc_part + swap(doc_part, "yh")
 
-    place = x.reshape(1)
-    half = logs // 8
-    away = swap(partial(place, third, stored, height, 0, half, BF16), "c")
-    kept = partial(place, third, stored, height, half, half, F32) + away.astype(F32)
-    quarter = half // 2
+    doc_part = doc_part.reshape(own_docs, 2, height // 2)
+    doc_half = lax.dynamic_index_in_dim(doc_part, c, 1, keepdims=False) + swap(
+        lax.dynamic_index_in_dim(doc_part, 1 - c, 1, keepdims=False), "c"
+    )
+    from_left = jnp.stack(
+        [doc_half] + [lax.ppermute(doc_half, "x", [(i, (i + d) % 4) for i in range(4)]) for d in range(1, 4)]
+    )
+    parts = [lax.dynamic_index_in_dim(from_left, (x + 4 - i) % 4, 0, keepdims=False) for i in range(4)]
+    doc_half = (parts[0] + parts[1]) + (parts[2] + parts[3])
+    doc_half = doc_half + swap(doc_half, "yh")
+
+    third, doc_half = lax.optimization_barrier((third, doc_half))
+    away, kept = partial(x.reshape(1), third, stored)
+    kept = kept + swap(away, "c").astype(F32)
+    quarter = kept.shape[1] // 2
     beyond = swap(kept[:, :quarter].astype(BF16), "yh")
     scores = (kept[:, quarter:] + beyond.astype(F32)) * 0.125
 
     scale = 0.125 / math.sqrt(logs * 32 / DOCS)
-    own_half = lax.dynamic_slice_in_dim(doc_part, c * (height // 2), height // 2, 1)
-    final = exchange(to_all((own_half * scale).astype(BF16), 32), DP).reshape(DOCS, height // 2)
+    final = exchange(to_all((doc_half * scale).astype(BF16), 32), DP).reshape(DOCS, height // 2)
+    final, scores = lax.optimization_barrier((final, scores))
     final = lax.all_gather(final, "c", axis=0)
     doc_influence = final.transpose(0, 2, 1).reshape(height, DOCS).astype(F32)
     return (scores, doc_influence)

time: 174 us -> 177 us (1.017)
  blocking collectives: 27 us -> 3.61 us
  starting transfers between devices: 68.7 us -> 85.4 us
  waiting for transfers between devices: 43.3 us -> 51.4 us
  local copies, waits for them, and re-layouts: 11.2 us -> 13.9 us
    all_to_all x1 -> x0, blocking collectives: 21.6 us -> none  [exchange(): return lax.all_to_all(flat, axes, 0, 0, tiled=True).reshape(shape)]
    ppermute x4, waiting for transfers between devices: 4 us -> 16.4 us  [swap(): return lax.ppermute(value, axis, [(0, 1), (1, 0)])]
    all_to_all x5 -> x6, waiting for transfers between devices: 36.6 us -> 24.8 us  [exchange(): return lax.all_to_all(flat, axes, 0, 0, tiled=True).reshape(shape)]
    ppermute x0 -> x3, starting transfers between devices: none -> 11 us  [per_device(): lax.ppermute(doc_half, 'x', [(i, (i + d) % 4) for i in range(4)])]
    ppermute x3, waiting for transfers between devices: 2.75 us -> 8.47 us  [per_device(): lax.ppermute(moving[d - 1], 'x', [(i, (i + d) % 4) for i in range(4)])]
    all_to_all x5 -> x6, starting transfers between devices: 44.7 us -> 47.7 us  [exchange(): return lax.all_to_all(flat, axes, 0, 0, tiled=True).reshape(shape)]
    ppermute x4, starting transfers between devices: 14.3 us -> 17.1 us  [swap(): return lax.ppermute(value, axis, [(0, 1), (1, 0)])]
    all_gather x1, blocking collectives: 5.42 us -> 3.61 us  [per_device(): final = lax.all_gather(final, 'c', axis=0)]
  transfers between devices with their start and end apart: 12 -> 16, of which waited for: 10 -> 13; matrix products, arithmetic and copies ran while one was open for 8% -> 8% of each run, Pallas kernels for 1% -> 0%
where the time goes in v3:
time: 177 us; the launch traced here: 175 us
  starting transfers between devices  85.4 us (48%)
  waiting for transfers between devices  51.4 us (29%)
  local copies, waits for them, and re-layouts  13.9 us (8%)
  other arithmetic  9.55 us (5%)
  matrix products  5.51 us (3%)
  Pallas kernels  4.78 us (3%)
  blocking collectives  3.61 us (2%)
    all_to_all x6, starting transfers between devices, exchange(): return lax.all_to_all(flat, axes, 0, 0, tiled=True).reshape(shape)  47.7 us
    all_to_all x6, waiting for transfers between devices, exchange(): return lax.all_to_all(flat, axes, 0, 0, tiled=True).reshape(shape)  24.8 us
    ppermute x4, starting transfers between devices, swap(): return lax.ppermute(value, axis, [(0, 1), (1, 0)])  17.1 us
    ppermute x4, waiting for transfers between devices, swap(): return lax.ppermute(value, axis, [(0, 1), (1, 0)])  16.4 us
    ppermute x3, starting transfers between devices, per_device(): lax.ppermute(doc_half, 'x', [(i, (i + d) % 4) for i in range(4)])  11 us
    ppermute x3, starting transfers between devices, per_device(): lax.ppermute(moving[d - 1], 'x', [(i, (i + d) % 4) for i in range(4)])  9.52 us
    ppermute x3, waiting for transfers between devices, per_device(): lax.ppermute(moving[d - 1], 'x', [(i, (i + d) % 4) for i in range(4)])  8.47 us
    unnamed x24, local copies, waits for them, and re-layouts  5.54 us
  transfers between devices with their start and end apart: 16, of which 13 were waited for; matrix products, arithmetic and copies ran while one was open for 8% of the time, Pallas kernels for 0%

profile of v3, /device:TPU:1, one launch (start us, length us, event | category | flops | bytes accessed | tf_op | source)
XLA Modules:
  0.0 175.2 jit_solution(13608241473114211282)
XLA Ops:
  0.7 1.2 copy-done
  1.9 1.3 fusion.11
  3.2 1.3 fusion.12
  4.5 0.2 copy.11
  4.7 0.9 pad_maximum_fusion
  5.6 10.3 %all-to-all-start = ((f32[16,72,128]{2,1,0:T(8,128)}), f32[16,72,128]{2,1,0:T(8,128)S(1)}, u32[]{:S(2)}, u32[]{:S(2)}) async-start(f32[16,72,128]{2,1,0:T(8,128)} %pad_maximum_fusion), calls=%async_computation | async-start | bytes 1179648 | tf_op jit(solution)/shard_map/all_to_all | solution.py:30
  15.8 2.6 %dynamic-slice_bitcast_fusion.3 = (bf16[256,256]{1,0:T(8,128)(2,1)S(1)}, bf16[256,256]{1,0:T(8,128)(2,1)S(1)}, bf16[256,256]{1,0:T(8,128)(2,1)}, bf16[256,256]{1...) fusion(bf16[2,4,2,256,256]{4,3,2,1,0:T(8,128)(2,1)} %bitcast.83, ...), kind=kLoop, calls=%fused_computation.25 | loop fusion | bytes 4194336 | tf_op jit(solution)/shard_map/reshape | solution.py:115
  18.4 0.1 convert_reduce_fusion.2
  18.5 2.1 %pad_maximum_fusion.4 = (bf16[1024,256]{1,0:T(8,128)(2,1)}, bf16[1024,256]{1,0:T(8,128)(2,1)S(1)}) fusion(bf16[256,256]{1,0:T(8,128)(2,1)} %get-tuple-element.38, bf16[256,256]{1,0:T(8,128)(2,1)} %get-tuple-element.39, bf16[256,256]{1,0:T(8,128)(2,1)} %get-tuple-element.40, bf16[256,256]{1,0:T(8,128)(2,1)} %get-tuple-element.41, ...), kind=kLoop, calls=%fused_computation.15 | loop fusion | flops 4194304 | bytes 2097152 | tf_op jit(solution)/shard_map/concatenate | solution.py:117
  20.6 1.1 pad_maximum_fusion.2
  21.7 6.4 %all-to-all-done = f32[16,72,128]{2,1,0:T(8,128)S(1)} async-done(((f32[16,72,128]{2,1,0:T(8,128)}), f32[16,72,128]{2,1,0:T(8,128)S(1)}, u32[]{:S(2)}, u32[]{:S(2)}) %all-to-all-start) | async-done | bytes 589856 | tf_op jit(solution)/shard_map/all_to_all | solution.py:30
  28.1 0.8 broadcast_in_dim.15
  28.9 4.3 %all-to-all-start.1 = ((bf16[16,64,128]{2,1,0:T(8,128)(2,1)}), bf16[16,64,128]{2,1,0:T(8,128)(2,1)S(1)}, u32[]{:S(2)}, u32[]{:S(2)}) async-start(bf16[16,64,128]{2,1,0:T(8,128)(2,1)} %broadcast_in_dim.15), calls=%async_computation.1 | async-start | bytes 524288 | tf_op jit(solution)/shard_map/all_to_all | solution.py:30
  33.2 2.3 %fusion.2 = bf16[256,256]{1,0:T(8,128)(2,1)S(1)} fusion(bf16[4096,256]{1,0:T(8,128)(2,1)} %param.12, s32[4096]{0:T(1024)S(1)} %bitcast.94), kind=kOutput, calls=%fused_computation.4 | convolution fusion | flops 537985024 | bytes 2244608 | tf_op jit(solution)/shard_map/dot_general | solution.py:108
  35.5 6.4 %all-to-all-done.1 = bf16[16,64,128]{2,1,0:T(8,128)(2,1)S(1)} async-done(((bf16[16,64,128]{2,1,0:T(8,128)(2,1)}), bf16[16,64,128]{2,1,0:T(8,128)(2,1)S(1)}, u32[]{:S(2)}, u32[]{:S(2)}) %all-to-all-start.1) | async-done | bytes 262176 | tf_op jit(solution)/shard_map/all_to_all | solution.py:30
  42.0 0.1 slice.50
  42.1 0.1 constant_dynamic-slice_fusion
  42.2 0.1 copy.12
  42.4 0.1 broadcast_multiply_fusion
  42.6 0.2 fusion.4
  42.8 0.1 reshape.184
  42.8 0.1 divide_convert_fusion
  42.9 0.7 pad_maximum_fusion.7
  43.6 12.9 %all-to-all-start.2 = ((bf16[4,88,256]{2,1,0:T(8,128)(2,1)}), bf16[4,88,256]{2,1,0:T(8,128)(2,1)S(1)}, u32[]{:S(2)}, u32[]{:S(2)}) async-start(bf16[4,88,256]{2,1,0:T(8,128)(2,1)} %pad_maximum_fusion.7), calls=%async_computation.2 | async-start | bytes 360448 | tf_op jit(solution)/shard_map/all_to_all | solution.py:30
  56.5 3.0 %collective-permute-start = (bf16[1024,256]{1,0:T(8,128)(2,1)S(1)}, bf16[1024,256]{1,0:T(8,128)(2,1)S(1)}, u32[]{:S(2)}, u32[]{:S(2)}) collective-permute-start(bf16[1024,256]{1,0:T(8,128)(2,1)S(1)} %copy-done.9), channel_id=1, source_target_pairs={{0,4},{2,6},{4,0},{6,2},{1,5},{3,7},{5,1},{7,3},{8,12},{10,14},{12... | collective-permute-start | bytes 1572872 | tf_op jit(solution)/shard_map/ppermute | solution.py:123
  59.6 9.4 %all-to-all-done.2 = bf16[4,88,256]{2,1,0:T(8,128)(2,1)S(1)} async-done(((bf16[4,88,256]{2,1,0:T(8,128)(2,1)}), bf16[4,88,256]{2,1,0:T(8,128)(2,1)S(1)}, u32[]{:S(2)}, u32[]{:S(2)}) %all-to-all-start.2) | async-done | bytes 180256 | tf_op jit(solution)/shard_map/all_to_all | solution.py:30
  69.1 0.8 pad_maximum_fusion.6
  69.9 2.3 %collective-permute-done.refs_2_ = bf16[1024,256]{1,0:T(8,128)(2,1)S(1)} collective-permute-done((bf16[1024,256]{1,0:T(8,128)(2,1)S(1)}, bf16[1024,256]{1,0:T(8,128)(2,1)S(1)}, u32[]{:S(2)}, u32[]{:S(2)}) %collective-permute-start) | collective-permute-done | bytes 524320 | tf_op jit(solution)/shard_map/ppermute | solution.py:123
  72.2 4.1 %all-to-all-start.3 = ((bf16[8,112,256]{2,1,0:T(8,128)(2,1)}), bf16[8,112,256]{2,1,0:T(8,128)(2,1)}, u32[]{:S(2)}, u32[]{:S(2)}) async-start(bf16[8,112,256]{2,1,0:T(8,128)(2,1)} %pad_maximum_fusion.6), calls=%async_computation.3 | async-start | bytes 917504 | tf_op jit(solution)/shard_map/all_to_all | solution.py:30
  76.4 3.4 %collective-permute-start.1 = (bf16[1024,256]{1,0:T(8,128)(2,1)}, bf16[1024,256]{1,0:T(8,128)(2,1)S(1)}, u32[]{:S(2)}, u32[]{:S(2)}) collective-permute-start(bf16[1024,256]{1,0:T(8,128)(2,1)} %get-tuple-element.21), channel_id=1, source_target_pairs={{0,2},{2,4},{4,6},{6,0},{1,3},{3,5},{5,7},{7,1},{8,10},{10,12},{12... | collective-permute-start | bytes 1572872 | tf_op jit(solution)/shard_map/ppermute | solution.py:123
  79.8 3.1 %collective-permute-start.2 = (bf16[1024,256]{1,0:T(8,128)(2,1)}, bf16[1024,256]{1,0:T(8,128)(2,1)S(1)}, u32[]{:S(2)}, u32[]{:S(2)}) collective-permute-start(bf16[1024,256]{1,0:T(8,128)(2,1)} %get-tuple-element.22), channel_id=1, source_target_pairs={{0,6},{2,0},{4,2},{6,4},{1,7},{3,1},{5,3},{7,5},{8,14},{10,8},{12,... | collective-permute-start | bytes 1572872 | tf_op jit(solution)/shard_map/ppermute | solution.py:123
  82.9 2.3 %all-to-all-done.3 = bf16[8,112,256]{2,1,0:T(8,128)(2,1)} async-done(((bf16[8,112,256]{2,1,0:T(8,128)(2,1)}), bf16[8,112,256]{2,1,0:T(8,128)(2,1)}, u32[]{:S(2)}, u32[]{:S(2)}) %all-to-all-start.3) | async-done | bytes 458784 | tf_op jit(solution)/shard_map/all_to_all | solution.py:30
  85.2 0.9 convert_reduce_fusion.1
  86.0 1.0 slice.55
  87.1 0.2 fusion.10
  87.3 0.3 convolution_add_fusion
  87.6 2.9 %collective-permute-done.1.refs_1_ = bf16[1024,256]{1,0:T(8,128)(2,1)S(1)} collective-permute-done((bf16[1024,256]{1,0:T(8,128)(2,1)}, bf16[1024,256]{1,0:T(8,128)(2,1)S(1)}, u32[]{:S(2)}, u32[]{:S(2)}) %collective-permute-start.1) | collective-permute-done | bytes 524320 | tf_op jit(solution)/shard_map/ppermute | solution.py:123
  90.5 3.2 %collective-permute-done.2.refs_3_ = bf16[1024,256]{1,0:T(8,128)(2,1)S(1)} collective-permute-done((bf16[1024,256]{1,0:T(8,128)(2,1)}, bf16[1024,256]{1,0:T(8,128)(2,1)S(1)}, u32[]{:S(2)}, u32[]{:S(2)}) %collective-permute-start.2) | collective-permute-done | bytes 524320 | tf_op jit(solution)/shard_map/ppermute | solution.py:123
  93.7 1.3 broadcast_in_dim.19
  95.1 3.6 %all-to-all-start.4 = ((bf16[4,768,256]{2,1,0:T(8,128)(2,1)}), bf16[4,768,256]{2,1,0:T(8,128)(2,1)S(1)}, u32[]{:S(2)}, u32[]{:S(2)}) async-start(bf16[4,768,256]{2,1,0:T(8,128)(2,1)} %broadcast_in_dim.19), calls=%async_computation.4 | async-start | bytes 3145728 | tf_op jit(solution)/shard_map/all_to_all | solution.py:30
  98.7 4.8 %collective-permute-start.3 = (f32[8,384]{1,0:T(8,128)S(1)}, f32[8,384]{1,0:T(8,128)S(1)}, u32[]{:S(2)}, u32[]{:S(2)}) collective-permute-start(f32[8,384]{1,0:T(8,128)S(1)} %dynamic-slice_bitcast_fusion.16), channel_id=1, source_target_pairs={{0,1},{1,0},{2,3},{3,2},{4,5},{5,4},{6,7},{7,6},{8,9},{9,8},{10,11... | collective-permute-start | bytes 36872 | tf_op jit(solution)/shard_map/ppermute | solution.py:24
  103.4 0.8 collective-permute-done.3
  104.3 3.6 %collective-permute-start.4 = (f32[8,384]{1,0:T(8,128)S(1)}, f32[8,384]{1,0:T(8,128)S(1)}, u32[]{:S(2)}, u32[]{:S(2)}) collective-permute-start(f32[8,384]{1,0:T(8,128)S(1)} %bitcast_add_fusion), channel_id=1, source_target_pairs={{0,2},{2,4},{4,6},{6,0},{1,3},{3,5},{5,7},{7,1},{8,10},{10,12},{12... | collective-permute-start | bytes 36872 | tf_op jit(solution)/shard_map/ppermute | solution.py:152
  107.9 4.3 %collective-permute-start.5 = (f32[8,384]{1,0:T(8,128)S(1)}, f32[8,384]{1,0:T(8,128)S(1)}, u32[]{:S(2)}, u32[]{:S(2)}) collective-permute-start(f32[8,384]{1,0:T(8,128)S(1)} %bitcast_add_fusion), channel_id=1, source_target_pairs={{0,4},{2,6},{4,0},{6,2},{1,5},{3,7},{5,1},{7,3},{8,12},{10,14},{12... | collective-permute-start | bytes 36872 | tf_op jit(solution)/shard_map/ppermute | solution.py:152
  112.2 3.1 %collective-permute-start.6 = (f32[8,384]{1,0:T(8,128)S(1)}, f32[8,384]{1,0:T(8,128)S(1)}, u32[]{:S(2)}, u32[]{:S(2)}) collective-permute-start(f32[8,384]{1,0:T(8,128)S(1)} %bitcast_add_fusion), channel_id=1, source_target_pairs={{0,6},{2,0},{4,2},{6,4},{1,7},{3,1},{5,3},{7,5},{8,14},{10,8},{12,... | collective-permute-start | bytes 36872 | tf_op jit(solution)/shard_map/ppermute | solution.py:152
  115.3 1.6 collective-permute-done.5
  117.0 0.2 collective-permute-done.6
  117.2 3.1 %collective-permute-start.7 = (f32[8,384]{1,0:T(8,128)S(1)}, f32[8,384]{1,0:T(8,128)S(1)}, u32[]{:S(2)}, u32[]{:S(2)}) collective-permute-start(f32[8,384]{1,0:T(8,128)S(1)} %add_bitcast_fusion), channel_id=1, source_target_pairs={{0,8},{8,0},{1,9},{9,1},{2,10},{10,2},{3,11},{11,3},{4,12},{12,4},... | collective-permute-start | bytes 36872 | tf_op jit(solution)/shard_map/ppermute | solution.py:24
  120.3 2.8 %collective-permute-done.7 = f32[8,384]{1,0:T(8,128)S(1)} collective-permute-done((f32[8,384]{1,0:T(8,128)S(1)}, f32[8,384]{1,0:T(8,128)S(1)}, u32[]{:S(2)}, u32[]{:S(2)}) %collective-permute-start.7) | collective-permute-done | bytes 12320 | tf_op jit(solution)/shard_map/ppermute | solution.py:24
  123.1 1.0 copy-done.3
  124.2 1.0 copy-done.5
  125.2 1.0 copy-done.7
  126.2 4.8 %shard_map.86 = (bf16[768,512]{1,0:T(8,128)(2,1)}, f32[768,512]{1,0:T(8,128)S(1)}) custom-call(s32[1]{0:T(128)} %bitcast.33.place_ref, bf16[4,768,256]{2,1,0:T(8,128)(2,1)S(1)} %all-to-all-done.4.queries_ref, bf16[1024,256]{1,0:T(8,128)(2,1)S(1)} %get-tuple-element.55.refs_0_, bf16[1024,256]{1,0:T(8,128)(2,1)S(1)} %copy-done.5, ...), custom_call_target="tpu_custom_call" | custom-call | flops 1024 | bytes 1024 | tf_op jit(solution)/shard_map/pallas_call | solution.py:63
  131.0 1.2 copy-done.1
  132.2 6.7 %collective-permute-start.8 = (bf16[768,512]{1,0:T(8,128)(2,1)}, bf16[768,512]{1,0:T(8,128)(2,1)S(1)}, u32[]{:S(2)}, u32[]{:S(2)}) collective-permute-start(bf16[768,512]{1,0:T(8,128)(2,1)} %get-tuple-element.31), channel_id=1, source_target_pairs={{0,1},{1,0},{2,3},{3,2},{4,5},{5,4},{6,7},{7,6},{8,9},{9,8},{10,11... | collective-permute-start | bytes 2359304 | tf_op jit(solution)/shard_map/ppermute | solution.py:24
  138.9 0.7 broadcast_in_dim.20
  139.6 12.5 %all-to-all-start.5 = ((bf16[32,8,384]{2,1,0:T(8,128)(2,1)}), bf16[32,8,384]{2,1,0:T(8,128)(2,1)S(1)}, u32[]{:S(2)}, u32[]{:S(2)}) async-start(bf16[32,8,384]{2,1,0:T(8,128)(2,1)} %broadcast_in_dim.20), calls=%async_computation.5 | async-start | bytes 393216 | tf_op jit(solution)/shard_map/all_to_all | solution.py:30
  152.2 1.6 convert_add_fusion
  153.9 2.5 %collective-permute-start.9 = (bf16[768,256]{1,0:T(8,128)(2,1)S(1)}, bf16[768,256]{1,0:T(8,128)(2,1)S(1)}, u32[]{:S(2)}, u32[]{:S(2)}) collective-permute-start(bf16[768,256]{1,0:T(8,128)(2,1)S(1)} %slice.85), channel_id=1, source_target_pairs={{0,8},{8,0},{1,9},{9,1},{2,10},{10,2},{3,11},{11,3},{4,12},{12,4},... | collective-permute-start | bytes 1179656 | tf_op jit(solution)/shard_map/ppermute | solution.py:24
  156.5 12.7 %collective-permute-done.9 = bf16[768,256]{1,0:T(8,128)(2,1)S(1)} collective-permute-done((bf16[768,256]{1,0:T(8,128)(2,1)S(1)}, bf16[768,256]{1,0:T(8,128)(2,1)S(1)}, u32[]{:S(2)}, u32[]{:S(2)}) %collective-permute-start.9) | collective-permute-done | bytes 393248 | tf_op jit(solution)/shard_map/ppermute | solution.py:24
  169.2 1.0 fusion.3
  170.2 0.2 all-to-all-done.5
  170.4 3.6 %all-gather = bf16[512,384]{1,0:T(8,128)(2,1)S(1)} all-gather(bf16[256,384]{1,0:T(8,128)(2,1)S(1)} %bitcast.88), channel_id=2, replica_groups=mesh['zh'=4,'zl'=4,'yl'=2,'yh'=2,'x'=4,'c'=2] {'c'}, dimensions={0}, use_global_device_ids=true | all-gather | bytes 589824 | tf_op jit(solution)/shard_map/all_gather | solution.py:168
  174.1 1.1 copy.15
  (44 shorter events, 0.5 us)
Async XLA Ops:
  0.6 1.2 copy-start
  0.6 2.5 %copy-start.8 = (bf16[1024,512]{1,0:T(8,128)(2,1)S(1)}, bf16[1024,512]{1,0:T(8,128)(2,1)}, u32[]{:S(2)}) copy-start(bf16[1024,512]{1,0:T(8,128)(2,1)} %param.8) | copy-start | bytes 3145732
  3.1 1.5 copy-start.11
  5.6 22.5 %all-to-all-start = ((f32[16,72,128]{2,1,0:T(8,128)}), f32[16,72,128]{2,1,0:T(8,128)S(1)}, u32[]{:S(2)}, u32[]{:S(2)}) async-start(f32[16,72,128]{2,1,0:T(8,128)} %pad_maximum_fusion), calls=%async_computation | async-start | bytes 1179648 | tf_op jit(solution)/shard_map/all_to_all | solution.py:30
  15.8 2.6 %copy-start.10 = (s32[1,1024]{1,0:T(1,128)S(1)}, s32[1,1024]{1,0:T(1,128)}, u32[]{:S(2)}) copy-start(s32[1,1024]{1,0:T(1,128)} %param.11) | copy-start | bytes 12292
  28.9 13.1 %all-to-all-start.1 = ((bf16[16,64,128]{2,1,0:T(8,128)(2,1)}), bf16[16,64,128]{2,1,0:T(8,128)(2,1)S(1)}, u32[]{:S(2)}, u32[]{:S(2)}) async-start(bf16[16,64,128]{2,1,0:T(8,128)(2,1)} %broadcast_in_dim.15), calls=%async_computation.1 | async-start | bytes 524288 | tf_op jit(solution)/shard_map/all_to_all | solution.py:30
  42.0 14.6 %copy-start.9 = (bf16[1024,256]{1,0:T(8,128)(2,1)S(1)}, bf16[1024,256]{1,0:T(8,128)(2,1)}, u32[]{:S(2)}) copy-start(bf16[1024,256]{1,0:T(8,128)(2,1)} %get-tuple-element.19) | copy-start | bytes 1572868
  43.6 25.4 %all-to-all-start.2 = ((bf16[4,88,256]{2,1,0:T(8,128)(2,1)}), bf16[4,88,256]{2,1,0:T(8,128)(2,1)S(1)}, u32[]{:S(2)}, u32[]{:S(2)}) async-start(bf16[4,88,256]{2,1,0:T(8,128)(2,1)} %pad_maximum_fusion.7), calls=%async_computation.2 | async-start | bytes 360448 | tf_op jit(solution)/shard_map/all_to_all | solution.py:30
  56.5 15.7 %collective-permute-start = (bf16[1024,256]{1,0:T(8,128)(2,1)S(1)}, bf16[1024,256]{1,0:T(8,128)(2,1)S(1)}, u32[]{:S(2)}, u32[]{:S(2)}) collective-permute-start(bf16[1024,256]{1,0:T(8,128)(2,1)S(1)} %copy-done.9), channel_id=1, source_target_pairs={{0,4},{2,6},{4,0},{6,2},{1,5},{3,7},{5,1},{7,3},{8,12},{10,14},{12... | collective-permute-start | bytes 1572872 | tf_op jit(solution)/shard_map/ppermute | solution.py:123
  72.2 15.3 %copy-start.2 = (bf16[1024,256]{1,0:T(8,128)(2,1)}, bf16[1024,256]{1,0:T(8,128)(2,1)S(1)}, u32[]{:S(2)}) copy-start(bf16[1024,256]{1,0:T(8,128)(2,1)S(1)} %collective-permute-done.refs_2_) | copy-start | bytes 1572868
  72.2 13.0 %all-to-all-start.3 = ((bf16[8,112,256]{2,1,0:T(8,128)(2,1)}), bf16[8,112,256]{2,1,0:T(8,128)(2,1)}, u32[]{:S(2)}, u32[]{:S(2)}) async-start(bf16[8,112,256]{2,1,0:T(8,128)(2,1)} %pad_maximum_fusion.6), calls=%async_computation.3 | async-start | bytes 917504 | tf_op jit(solution)/shard_map/all_to_all | solution.py:30
  76.4 14.1 %collective-permute-start.1 = (bf16[1024,256]{1,0:T(8,128)(2,1)}, bf16[1024,256]{1,0:T(8,128)(2,1)S(1)}, u32[]{:S(2)}, u32[]{:S(2)}) collective-permute-start(bf16[1024,256]{1,0:T(8,128)(2,1)} %get-tuple-element.21), channel_id=1, source_target_pairs={{0,2},{2,4},{4,6},{6,0},{1,3},{3,5},{5,7},{7,1},{8,10},{10,12},{12... | collective-permute-start | bytes 1572872 | tf_op jit(solution)/shard_map/ppermute | solution.py:123
  79.8 13.9 %collective-permute-start.2 = (bf16[1024,256]{1,0:T(8,128)(2,1)}, bf16[1024,256]{1,0:T(8,128)(2,1)S(1)}, u32[]{:S(2)}, u32[]{:S(2)}) collective-permute-start(bf16[1024,256]{1,0:T(8,128)(2,1)} %get-tuple-element.22), channel_id=1, source_target_pairs={{0,6},{2,0},{4,2},{6,4},{1,7},{3,1},{5,3},{7,5},{8,14},{10,8},{12,... | collective-permute-start | bytes 1572872 | tf_op jit(solution)/shard_map/ppermute | solution.py:123
  90.5 4.6 %copy-start.4 = (bf16[1024,256]{1,0:T(8,128)(2,1)}, bf16[1024,256]{1,0:T(8,128)(2,1)S(1)}, u32[]{:S(2)}) copy-start(bf16[1024,256]{1,0:T(8,128)(2,1)S(1)} %collective-permute-done.1.refs_1_) | copy-start | bytes 1572868
  93.7 1.4 copy-start.6
  95.1 28.0 %all-to-all-start.4 = ((bf16[4,768,256]{2,1,0:T(8,128)(2,1)}), bf16[4,768,256]{2,1,0:T(8,128)(2,1)S(1)}, u32[]{:S(2)}, u32[]{:S(2)}) async-start(bf16[4,768,256]{2,1,0:T(8,128)(2,1)} %broadcast_in_dim.19), calls=%async_computation.4 | async-start | bytes 3145728 | tf_op jit(solution)/shard_map/all_to_all | solution.py:30
  98.7 5.6 %collective-permute-start.3 = (f32[8,384]{1,0:T(8,128)S(1)}, f32[8,384]{1,0:T(8,128)S(1)}, u32[]{:S(2)}, u32[]{:S(2)}) collective-permute-start(f32[8,384]{1,0:T(8,128)S(1)} %dynamic-slice_bitcast_fusion.16), channel_id=1, source_target_pairs={{0,1},{1,0},{2,3},{3,2},{4,5},{5,4},{6,7},{7,6},{8,9},{9,8},{10,11... | collective-permute-start | bytes 36872 | tf_op jit(solution)/shard_map/ppermute | solution.py:24
  104.3 11.1 %collective-permute-start.4 = (f32[8,384]{1,0:T(8,128)S(1)}, f32[8,384]{1,0:T(8,128)S(1)}, u32[]{:S(2)}, u32[]{:S(2)}) collective-permute-start(f32[8,384]{1,0:T(8,128)S(1)} %bitcast_add_fusion), channel_id=1, source_target_pairs={{0,2},{2,4},{4,6},{6,0},{1,3},{3,5},{5,7},{7,1},{8,10},{10,12},{12... | collective-permute-start | bytes 36872 | tf_op jit(solution)/shard_map/ppermute | solution.py:152
  107.9 9.0 %collective-permute-start.5 = (f32[8,384]{1,0:T(8,128)S(1)}, f32[8,384]{1,0:T(8,128)S(1)}, u32[]{:S(2)}, u32[]{:S(2)}) collective-permute-start(f32[8,384]{1,0:T(8,128)S(1)} %bitcast_add_fusion), channel_id=1, source_target_pairs={{0,4},{2,6},{4,0},{6,2},{1,5},{3,7},{5,1},{7,3},{8,12},{10,14},{12... | collective-permute-start | bytes 36872 | tf_op jit(solution)/shard_map/ppermute | solution.py:152
  112.2 4.9 %collective-permute-start.6 = (f32[8,384]{1,0:T(8,128)S(1)}, f32[8,384]{1,0:T(8,128)S(1)}, u32[]{:S(2)}, u32[]{:S(2)}) collective-permute-start(f32[8,384]{1,0:T(8,128)S(1)} %bitcast_add_fusion), channel_id=1, source_target_pairs={{0,6},{2,0},{4,2},{6,4},{1,7},{3,1},{5,3},{7,5},{8,14},{10,8},{12,... | collective-permute-start | bytes 36872 | tf_op jit(solution)/shard_map/ppermute | solution.py:152
  117.2 5.9 %collective-permute-start.7 = (f32[8,384]{1,0:T(8,128)S(1)}, f32[8,384]{1,0:T(8,128)S(1)}, u32[]{:S(2)}, u32[]{:S(2)}) collective-permute-start(f32[8,384]{1,0:T(8,128)S(1)} %add_bitcast_fusion), channel_id=1, source_target_pairs={{0,8},{8,0},{1,9},{9,1},{2,10},{10,2},{3,11},{11,3},{4,12},{12,4},... | collective-permute-start | bytes 36872 | tf_op jit(solution)/shard_map/ppermute | solution.py:24
  123.1 1.0 copy-start.3
  124.2 1.0 copy-start.5
  125.2 1.0 copy-start.7
  131.0 1.2 copy-start.1
  132.2 20.0 %collective-permute-start.8 = (bf16[768,512]{1,0:T(8,128)(2,1)}, bf16[768,512]{1,0:T(8,128)(2,1)S(1)}, u32[]{:S(2)}, u32[]{:S(2)}) collective-permute-start(bf16[768,512]{1,0:T(8,128)(2,1)} %get-tuple-element.31), channel_id=1, source_target_pairs={{0,1},{1,0},{2,3},{3,2},{4,5},{5,4},{6,7},{7,6},{8,9},{9,8},{10,11... | collective-permute-start | bytes 2359304 | tf_op jit(solution)/shard_map/ppermute | solution.py:24
  139.6 30.7 %all-to-all-start.5 = ((bf16[32,8,384]{2,1,0:T(8,128)(2,1)}), bf16[32,8,384]{2,1,0:T(8,128)(2,1)S(1)}, u32[]{:S(2)}, u32[]{:S(2)}) async-start(bf16[32,8,384]{2,1,0:T(8,128)(2,1)} %broadcast_in_dim.20), calls=%async_computation.5 | async-start | bytes 393216 | tf_op jit(solution)/shard_map/all_to_all | solution.py:30
  153.9 15.3 %collective-permute-start.9 = (bf16[768,256]{1,0:T(8,128)(2,1)S(1)}, bf16[768,256]{1,0:T(8,128)(2,1)S(1)}, u32[]{:S(2)}, u32[]{:S(2)}) collective-permute-start(bf16[768,256]{1,0:T(8,128)(2,1)S(1)} %slice.85), channel_id=1, source_target_pairs={{0,8},{8,0},{1,9},{9,1},{2,10},{10,2},{3,11},{11,3},{4,12},{12,4},... | collective-permute-start | bytes 1179656 | tf_op jit(solution)/shard_map/ppermute | solution.py:24

commit v4 on v3

--- a/solution.py
+++ b/solution.py
@@ -1,11 +1,9 @@
-import functools
 import math
 
 import jax
 import jax.numpy as jnp
 from jax import lax
 from jax.experimental import pallas as pl
-from jax.experimental.pallas import tpu as pltpu
 from jax.sharding import Mesh
 from jax.sharding import PartitionSpec as P
 
@@ -22,6 +20,10 @@
 
 def swap(value, axis):
     return lax.ppermute(value, axis, [(0, 1), (1, 0)])
+
+
+def along_x(value, distance):
+    return lax.ppermute(value, "x", [(i, (i + distance) % 4) for i in range(4)]) if distance else value
 
 
 def exchange(value, axes):
@@ -43,31 +45,34 @@
     return lax.dot_general(left, right, (((1,), (1,)), ((), ())), preferred_element_type=F32)
 
 
-def partial_kernel(tile, place_ref, queries_ref, *refs):
+def partial_kernel(own, left, upper, lower, right, *refs):
     stored, (away_ref, kept_ref) = refs[:4], refs[4:]
-    height, half = away_ref.shape
-    x = place_ref[0]
+    half = away_ref.shape[1]
+    first_half = pl.program_id(0) < pl.num_programs(0) // 2
+    across = jnp.where(first_half, upper[...], lower[...])
+    queries = (own[...], left[...], across, right[...])
     for first, out_ref in ((0, away_ref), (half, kept_ref)):
-        for start in range(0, height, tile):
-            total = None
-            for d in range(4):
-                left = queries_ref[lax.rem(x + 4 - d, 4), pl.ds(start, tile), :]
-                term = dot_t(left, stored[d][pl.ds(first, half), :])
-                total = term if total is None else total + term
-            out_ref[pl.ds(start, tile), :] = total.astype(out_ref.dtype)
+        terms = [dot_t(q, t[pl.ds(first, half), :]) for q, t in zip(queries, stored)]
+        out_ref[...] = ((terms[0] + terms[1]) + (terms[2] + terms[3])).astype(out_ref.dtype)
 
 
-def partial(place, queries, stored):
-    height, half = queries.shape[1], stored[0].shape[0] // 2
-    vmem = pl.BlockSpec(memory_space=pltpu.VMEM)
+def partial(queries, stored):
+    (height, width), count = queries[0].shape, stored[0].shape[0]
+    tile, half = 128, count // 2
+    steps = height // tile
+    rows = pl.BlockSpec((tile, width), lambda i: (i, 0))
+    upper = pl.BlockSpec((tile, width), lambda i: (jnp.minimum(i, steps // 2 - 1), 0))
+    lower = pl.BlockSpec((tile, width), lambda i: (jnp.maximum(i - steps // 2, 0), 0))
+    whole = pl.BlockSpec((count, width), lambda i: (0, 0))
+    out = pl.BlockSpec((tile, half), lambda i: (i, 0))
     return pl.pallas_call(
-        functools.partial(partial_kernel, 128),
+        partial_kernel,
+        grid=(steps,),
         out_shape=(jax.ShapeDtypeStruct((height, half), BF16), jax.ShapeDtypeStruct((height, half), F32)),
-        in_specs=[pl.BlockSpec(memory_space=pltpu.SMEM)] + [vmem] * 5,
-        out_specs=(vmem, vmem),
-        compiler_params=pltpu.CompilerParams(vmem_limit_bytes=32 * 1024 * 1024),
-        cost_estimate=pl.CostEstimate(flops=1024, bytes_accessed=1024, transcendentals=0),
-    )(place, queries, *stored)
+        in_specs=[rows, rows, upper, lower, rows] + [whole] * 4,
+        out_specs=(out, out),
+        cost_estimate=pl.CostEstimate(flops=8 * height * count * width, bytes_accessed=6 << 20, transcendentals=0),
+    )(*queries, *stored)
 
 
 def per_device(activations, out_grads, proj_in, proj_out, segment_ids, train_logs, doc_ids):
@@ -116,11 +121,9 @@
 
         return jnp.concatenate([block(1 - yh, 1 - c), block(yh, 1 - c), block(1 - yh, c), block(yh, c)])
 
-    far, *moving = lax.optimization_barrier((far, *(rows_for((x + d) % 4) for d in range(1, 4))))
+    stored = [along_x(rows_for((x + d) % 4), d) for d in range(4)]
+    far, stored[1], stored[3] = lax.optimization_barrier((far, stored[1], stored[3]))
     far = exchange(far, "zh")
-    stored = [rows_for(x)]
-    for d in range(1, 4):
-        stored.append(lax.ppermute(moving[d - 1], "x", [(i, (i + d) % 4) for i in range(4)]))
 
     docs = jnp.sum(far[:, EX_DEV:].astype(F32), axis=0)
     high, low = split(docs)
@@ -141,32 +144,23 @@
     doc_part = dot_t(high, queries) + dot_t(low, queries)
 
     height = queries.shape[0]
-    third, doc_part, stored[1], stored[3] = lax.optimization_barrier((queries, doc_part, stored[1], stored[3]))
-    third = exchange(to_all(third, 4), "x")
+    share = height // 16
+    left, right = along_x(queries, 1), along_x(queries, 3)
+    doc_part = jnp.pad(doc_part.reshape(own_docs, 16, share), ((0, 0), (0, 0), (0, 128 - share))).transpose(1, 0, 2)
+    doc_part = jnp.sum(exchange(doc_part, TENSOR), axis=0)
+    scale = 0.125 / math.sqrt(logs * 32 / DOCS)
+    doc_part = to_all((doc_part * scale).astype(BF16), 32)
+    doc_part, left, right = lax.optimization_barrier((doc_part, left, right))
+    influence = exchange(doc_part, DP).reshape(DOCS, 128)[:, :share].T
+    across = [along_x(left[: height // 2], 1), along_x(right[height // 2 :], 3)]
+    *across, influence = lax.optimization_barrier((*across, influence))
 
-    doc_part = doc_part.reshape(own_docs, 2, height // 2)
-    doc_half = lax.dynamic_index_in_dim(doc_part, c, 1, keepdims=False) + swap(
-        lax.dynamic_index_in_dim(doc_part, 1 - c, 1, keepdims=False), "c"
-    )
-    from_left = jnp.stack(
-        [doc_half] + [lax.ppermute(doc_half, "x", [(i, (i + d) % 4) for i in range(4)]) for d in range(1, 4)]
-    )
-    parts = [lax.dynamic_index_in_dim(from_left, (x + 4 - i) % 4, 0, keepdims=False) for i in range(4)]
-    doc_half = (parts[0] + parts[1]) + (parts[2] + parts[3])
-    doc_half = doc_half + swap(doc_half, "yh")
-
-    third, doc_half = lax.optimization_barrier((third, doc_half))
-    away, kept = partial(x.reshape(1), third, stored)
+    away, kept = partial([queries, left, *across, right], stored)
     kept = kept + swap(away, "c").astype(F32)
     quarter = kept.shape[1] // 2
     beyond = swap(kept[:, :quarter].astype(BF16), "yh")
     scores = (kept[:, quarter:] + beyond.astype(F32)) * 0.125
-
-    scale = 0.125 / math.sqrt(logs * 32 / DOCS)
-    final = exchange(to_all((doc_half * scale).astype(BF16), 32), DP).reshape(DOCS, height // 2)
-    final, scores = lax.optimization_barrier((final, scores))
-    final = lax.all_gather(final, "c", axis=0)
-    doc_influence = final.transpose(0, 2, 1).reshape(height, DOCS).astype(F32)
+    doc_influence = exchange(to_all(influence, 16), TENSOR).reshape(height, DOCS).astype(F32)
     return (scores, doc_influence)
 
 

time: 177 us -> 177 us (level)
  blocking collectives: 3.61 us -> 29.5 us
  waiting for transfers between devices: 51.4 us -> 36.8 us
  starting transfers between devices: 85.4 us -> 74.4 us
  local copies, waits for them, and re-layouts: 13.9 us -> 8.59 us
  Pallas kernels: 4.78 us -> 7.86 us
    all_to_all x0 -> x2, blocking collectives: none -> 29.5 us  [exchange(): return lax.all_to_all(flat, axes, 0, 0, tiled=True).reshape(shape)]
    ppermute x4 -> x2, waiting for transfers between devices: 16.4 us -> 7.42 us  [swap(): return lax.ppermute(value, axis, [(0, 1), (1, 0)])]
    ppermute x4 -> x2, starting transfers between devices: 17.1 us -> 8.71 us  [swap(): return lax.ppermute(value, axis, [(0, 1), (1, 0)])]
    ppermute x6 -> x7, waiting for transfers between devices: 10.3 us -> 4.41 us  [along_x(): lax.ppermute(value, 'x', [(i, (i + distance) % 4) for i in range(4)])]
    all_to_all x6 -> x5, starting transfers between devices: 47.7 us -> 42.9 us  [exchange(): return lax.all_to_all(flat, axes, 0, 0, tiled=True).reshape(shape)]
    all_gather x1 -> x0, blocking collectives: 3.61 us -> none  [per_device(): final = lax.all_gather(final, 'c', axis=0)]
    pallas_call x1, Pallas kernels: 4.78 us -> 7.86 us  [partial(): pl.pallas_call(partial_kernel, grid=(steps,), out_shape=(jax.ShapeDtypeSt...]
    unnamed x24 -> x18, local copies, waits for them, and re-layouts: 5.54 us -> 2.7 us
  transfers between devices with their start and end apart: 16 -> 14, of which waited for: 13 -> 7; matrix products, arithmetic and copies ran while one was open for 8% -> 9% of each run, Pallas kernels for 0% -> 0%
where the time goes in v4:
time: 177 us; the launch traced here: 175 us
  starting transfers between devices  74.4 us (42%)
  waiting for transfers between devices  36.8 us (21%)
  blocking collectives  29.5 us (17%)
  other arithmetic  10.6 us (6%)
  local copies, waits for them, and re-layouts  8.59 us (5%)
  Pallas kernels  7.86 us (4%)
  matrix products  6.56 us (4%)
    all_to_all x5, starting transfers between devices, exchange(): return lax.all_to_all(flat, axes, 0, 0, tiled=True).reshape(shape)  42.9 us
    all_to_all x2, blocking collectives, exchange(): return lax.all_to_all(flat, axes, 0, 0, tiled=True).reshape(shape)  29.5 us
    all_to_all x5, waiting for transfers between devices, exchange(): return lax.all_to_all(flat, axes, 0, 0, tiled=True).reshape(shape)  25 us
    ppermute x7, starting transfers between devices, along_x(): lax.ppermute(value, 'x', [(i, (i + distance) % 4) for i in range(4)])  22.8 us
    ppermute x2, starting transfers between devices, swap(): return lax.ppermute(value, axis, [(0, 1), (1, 0)])  8.71 us
    pallas_call x1, Pallas kernels, partial(): pl.pallas_call(partial_kernel, grid=(steps,), out_shape=(jax.ShapeDtypeSt...  7.86 us
    ppermute x2, waiting for transfers between devices, swap(): return lax.ppermute(value, axis, [(0, 1), (1, 0)])  7.42 us
    ppermute x7, waiting for transfers between devices, along_x(): lax.ppermute(value, 'x', [(i, (i + distance) % 4) for i in range(4)])  4.41 us
  transfers between devices with their start and end apart: 14, of which 7 were waited for; matrix products, arithmetic and copies ran while one was open for 9% of the time, Pallas kernels for 0%

profile of v4, /device:TPU:1, one launch (start us, length us, event | category | flops | bytes accessed | tf_op | source)
XLA Modules:
  0.0 175.4 jit_solution(17195293360767217665)
XLA Ops:
  0.6 0.0 copy-start
  0.6 0.8 convert_bitcast_fusion
  1.4 0.5 copy-done
  1.9 1.3 fusion.11
  3.1 1.7 fusion.12
  4.9 0.2 copy.18
  5.1 0.9 pad_maximum_fusion
  6.0 10.3 %all-to-all-start = ((f32[16,72,128]{2,1,0:T(8,128)}), f32[16,72,128]{2,1,0:T(8,128)S(1)}, u32[]{:S(2)}, u32[]{:S(2)}) async-start(f32[16,72,128]{2,1,0:T(8,128)} %pad_maximum_fusion), calls=%async_computation | async-start | bytes 1179648 | tf_op jit(solution)/shard_map/all_to_all | solution.py:32
  16.2 2.5 %dynamic-slice_bitcast_fusion.3 = (bf16[256,256]{1,0:T(8,128)(2,1)S(1)}, bf16[256,256]{1,0:T(8,128)(2,1)S(1)}, bf16[256,256]{1,0:T(8,128)(2,1)S(1)}, bf16[256,25...) fusion(bf16[2,4,2,256,256]{4,3,2,1,0:T(8,128)(2,1)} %bitcast.73, ...), kind=kLoop, calls=%fused_computation.25 | loop fusion | bytes 4194336 | tf_op jit(solution)/shard_map/reshape | solution.py:120
  18.8 3.3 %collective-permute-start = (bf16[1024,256]{1,0:T(8,128)(2,1)S(1)}, bf16[1024,256]{1,0:T(8,128)(2,1)}, u32[]{:S(2)}, u32[]{:S(2)}) collective-permute-start(bf16[1024,256]{1,0:T(8,128)(2,1)S(1)} %pad_maximum_fusion.2), channel_id=1, source_target_pairs={{0,2},{2,4},{4,6},{6,0},{1,3},{3,5},{5,7},{7,1},{8,10},{10,12},{12... | collective-permute-start | bytes 1572872 | tf_op jit(solution)/shard_map/ppermute | solution.py:26
  22.1 3.2 %collective-permute-start.1 = (bf16[1024,256]{1,0:T(8,128)(2,1)S(1)}, bf16[1024,256]{1,0:T(8,128)(2,1)}, u32[]{:S(2)}, u32[]{:S(2)}) collective-permute-start(bf16[1024,256]{1,0:T(8,128)(2,1)S(1)} %pad_maximum_fusion.3), channel_id=1, source_target_pairs={{0,6},{2,0},{4,2},{6,4},{1,7},{3,1},{5,3},{7,5},{8,14},{10,8},{12,... | collective-permute-start | bytes 1572872 | tf_op jit(solution)/shard_map/ppermute | solution.py:26
  25.3 0.1 convert_reduce_fusion.2
  25.5 3.0 %all-to-all-done = f32[16,72,128]{2,1,0:T(8,128)S(1)} async-done(((f32[16,72,128]{2,1,0:T(8,128)}), f32[16,72,128]{2,1,0:T(8,128)S(1)}, u32[]{:S(2)}, u32[]{:S(2)}) %all-to-all-start) | async-done | bytes 589856 | tf_op jit(solution)/shard_map/all_to_all | solution.py:32
  28.5 0.8 broadcast_in_dim.15
  29.3 4.6 %all-to-all-start.1 = ((bf16[16,64,128]{2,1,0:T(8,128)(2,1)}), bf16[16,64,128]{2,1,0:T(8,128)(2,1)S(1)}, u32[]{:S(2)}, u32[]{:S(2)}) async-start(bf16[16,64,128]{2,1,0:T(8,128)(2,1)} %broadcast_in_dim.15), calls=%async_computation.1 | async-start | bytes 524288 | tf_op jit(solution)/shard_map/all_to_all | solution.py:32
  33.9 3.0 %fusion.2 = bf16[256,256]{1,0:T(8,128)(2,1)} fusion(bf16[4096,256]{1,0:T(8,128)(2,1)} %param.12, s32[4096]{0:T(1024)S(1)} %bitcast.79), kind=kOutput, calls=%fused_computation.4 | convolution fusion | flops 537985024 | bytes 2244608 | tf_op jit(solution)/shard_map/dot_general | solution.py:113
  36.8 6.0 %all-to-all-done.1 = bf16[16,64,128]{2,1,0:T(8,128)(2,1)S(1)} async-done(((bf16[16,64,128]{2,1,0:T(8,128)(2,1)}), bf16[16,64,128]{2,1,0:T(8,128)(2,1)S(1)}, u32[]{:S(2)}, u32[]{:S(2)}) %all-to-all-start.1) | async-done | bytes 262176 | tf_op jit(solution)/shard_map/all_to_all | solution.py:32
  42.9 0.1 slice.62
  43.0 0.1 constant_dynamic-slice_fusion
  43.2 0.1 copy.19
  43.3 0.1 broadcast_multiply_fusion
  43.4 0.1 mul.48
  43.5 0.2 fusion.4
  43.7 0.1 reshape.184
  43.8 0.1 divide_convert_fusion
  43.8 1.6 pad_maximum_fusion.7
  45.4 0.0 collective-permute-done.refs_1_
  45.4 12.9 %all-to-all-start.2 = ((bf16[4,88,256]{2,1,0:T(8,128)(2,1)}), bf16[4,88,256]{2,1,0:T(8,128)(2,1)S(1)}, u32[]{:S(2)}, u32[]{:S(2)}) async-start(bf16[4,88,256]{2,1,0:T(8,128)(2,1)} %pad_maximum_fusion.7), calls=%async_computation.2 | async-start | bytes 360448 | tf_op jit(solution)/shard_map/all_to_all | solution.py:32
  58.4 1.1 pad_maximum_fusion.4
  59.5 4.0 %collective-permute-start.2 = (bf16[1024,256]{1,0:T(8,128)(2,1)S(1)}, bf16[1024,256]{1,0:T(8,128)(2,1)S(1)}, u32[]{:S(2)}, u32[]{:S(2)}) collective-permute-start(bf16[1024,256]{1,0:T(8,128)(2,1)S(1)} %pad_maximum_fusion.4), channel_id=1, source_target_pairs={{0,4},{2,6},{4,0},{6,2},{1,5},{3,7},{5,1},{7,3},{8,12},{10,14},{12... | collective-permute-start | bytes 1572872 | tf_op jit(solution)/shard_map/ppermute | solution.py:26
  63.5 7.3 %all-to-all-done.2 = bf16[4,88,256]{2,1,0:T(8,128)(2,1)S(1)} async-done(((bf16[4,88,256]{2,1,0:T(8,128)(2,1)}), bf16[4,88,256]{2,1,0:T(8,128)(2,1)S(1)}, u32[]{:S(2)}, u32[]{:S(2)}) %all-to-all-start.2) | async-done | bytes 180256 | tf_op jit(solution)/shard_map/all_to_all | solution.py:32
  71.0 4.4 %collective-permute-done.2.refs_2_ = bf16[1024,256]{1,0:T(8,128)(2,1)S(1)} collective-permute-done((bf16[1024,256]{1,0:T(8,128)(2,1)S(1)}, bf16[1024,256]{1,0:T(8,128)(2,1)S(1)}, u32[]{:S(2)}, u32[]{:S(2)}) %collective-permute-start.2) | collective-permute-done | bytes 524320 | tf_op jit(solution)/shard_map/ppermute | solution.py:26
  75.4 14.0 %all_to_all.48 = bf16[8,112,256]{2,1,0:T(8,128)(2,1)S(1)} all-to-all(bf16[8,112,256]{2,1,0:T(8,128)(2,1)S(1)} %pad_maximum_fusion.6), channel_id=1, replica_groups=mesh['zh'=4,'zl'=4,'yl'=2,'yh'=2,'x'=4,'c'=2] {'zl','yl'}, dimensions={0} | all-to-all | bytes 917504 | tf_op jit(solution)/shard_map/all_to_all | solution.py:32
  89.5 5.0 %collective-permute-start.4 = (bf16[768,256]{1,0:T(8,128)(2,1)S(1)}, bf16[768,256]{1,0:T(8,128)(2,1)S(1)}, u32[]{:S(2)}, u32[]{:S(2)}) collective-permute-start(bf16[768,256]{1,0:T(8,128)(2,1)S(1)} %bitcast.66), channel_id=1, source_target_pairs={{0,6},{2,0},{4,2},{6,4},{1,7},{3,1},{5,3},{7,5},{8,14},{10,8},{12,... | collective-permute-start | bytes 1179656 | tf_op jit(solution)/shard_map/ppermute | solution.py:26
  94.5 2.0 %collective-permute-start.3 = (bf16[768,256]{1,0:T(8,128)(2,1)S(1)}, bf16[768,256]{1,0:T(8,128)(2,1)S(1)}, u32[]{:S(2)}, u32[]{:S(2)}) collective-permute-start(bf16[768,256]{1,0:T(8,128)(2,1)S(1)} %bitcast.67), channel_id=1, source_target_pairs={{0,2},{2,4},{4,6},{6,0},{1,3},{3,5},{5,7},{7,1},{8,10},{10,12},{12... | collective-permute-start | bytes 1179656 | tf_op jit(solution)/shard_map/ppermute | solution.py:26
  96.5 0.2 fusion.10
  96.7 0.3 convolution_add_fusion
  97.0 0.1 reshape.201
  97.2 15.5 %all_to_all.49 = f32[16,8,128]{2,1,0:T(8,128)S(1)} all-to-all(f32[16,8,128]{2,1,0:T(8,128)S(1)} %pad_bitcast_fusion), channel_id=1, replica_groups=mesh['zh'=4,'zl'=4,'yl'=2,'yh'=2,'x'=4,'c'=2] {'yh','x','c'}, dimensions={0} | all-to-all | bytes 131072 | tf_op jit(solution)/shard_map/all_to_all | solution.py:32
  112.7 0.0 collective-permute-done.4.right
  112.7 0.0 collective-permute-done.3.left
  112.8 0.7 broadcast_in_dim.19
  113.5 11.7 %all-to-all-start.5 = ((bf16[32,8,128]{2,1,0:T(8,128)(2,1)}), bf16[32,8,128]{2,1,0:T(8,128)(2,1)S(1)}, u32[]{:S(2)}, u32[]{:S(2)}) async-start(bf16[32,8,128]{2,1,0:T(8,128)(2,1)} %broadcast_in_dim.19), calls=%async_computation.5 | async-start | bytes 131072 | tf_op jit(solution)/shard_map/all_to_all | solution.py:32
  125.1 0.8 pad_maximum_fusion.5.refs_0_
  126.0 2.9 %collective-permute-start.6 = (bf16[384,256]{1,0:T(8,128)(2,1)S(1)}, bf16[384,256]{1,0:T(8,128)(2,1)S(1)}, u32[]{:S(2)}, u32[]{:S(2)}) collective-permute-start(bf16[384,256]{1,0:T(8,128)(2,1)S(1)} %slice.57), channel_id=1, source_target_pairs={{0,6},{2,0},{4,2},{6,4},{1,7},{3,1},{5,3},{7,5},{8,14},{10,8},{12,... | collective-permute-start | bytes 589832 | tf_op jit(solution)/shard_map/ppermute | solution.py:26
  128.9 2.4 %collective-permute-start.5 = (bf16[384,256]{1,0:T(8,128)(2,1)S(1)}, bf16[384,256]{1,0:T(8,128)(2,1)S(1)}, u32[]{:S(2)}, u32[]{:S(2)}) collective-permute-start(bf16[384,256]{1,0:T(8,128)(2,1)S(1)} %slice.56), channel_id=1, source_target_pairs={{0,2},{2,4},{4,6},{6,0},{1,3},{3,5},{5,7},{7,1},{8,10},{10,12},{12... | collective-permute-start | bytes 589832 | tf_op jit(solution)/shard_map/ppermute | solution.py:26
  131.3 6.4 %all-to-all-done.5 = bf16[32,8,128]{2,1,0:T(8,128)(2,1)S(1)} async-done(((bf16[32,8,128]{2,1,0:T(8,128)(2,1)}), bf16[32,8,128]{2,1,0:T(8,128)(2,1)S(1)}, u32[]{:S(2)}, u32[]{:S(2)}) %all-to-all-start.5) | async-done | bytes 65568 | tf_op jit(solution)/shard_map/all_to_all | solution.py:32
  137.7 0.0 collective-permute-done.6.lower
  137.7 0.6 copy-done.7
  138.4 0.7 copy-done.8
  139.1 7.9 %shard_map.86 = (bf16[768,512]{1,0:T(8,128)(2,1)}, f32[768,512]{1,0:T(8,128)}) custom-call(bf16[768,256]{1,0:T(8,128)(2,1)} %bitcast.70, bf16[768,256]{1,0:T(8,128)(2,1)} %copy-done.4, bf16[384,256]{1,0:T(8,128)(2,1)} %copy-done.8, bf16[384,256]{1,0:T(8,128)(2,1)} %copy-done.7, bf16[768,256]{1,0:T(8,128)(2,1)} %copy-done.3, ...), custom_call_target="tpu_custom_call" | custom-call | flops 1610612736 | bytes 6291456 | tf_op jit(solution)/shard_map/pallas_call | solution.py:68
  146.9 4.0 %collective-permute-start.7 = (bf16[768,512]{1,0:T(8,128)(2,1)}, bf16[768,512]{1,0:T(8,128)(2,1)S(1)}, u32[]{:S(2)}, u32[]{:S(2)}) collective-permute-start(bf16[768,512]{1,0:T(8,128)(2,1)} %get-tuple-element.26), channel_id=1, source_target_pairs={{0,1},{1,0},{2,3},{3,2},{4,5},{5,4},{6,7},{7,6},{8,9},{9,8},{10,11... | collective-permute-start | bytes 2359304 | tf_op jit(solution)/shard_map/ppermute | solution.py:22
  150.9 0.1 copy.23
  151.0 0.8 broadcast_in_dim.20
  151.8 3.5 %all-to-all-start.6 = ((bf16[16,48,256]{2,1,0:T(8,128)(2,1)}), bf16[16,48,256]{2,1,0:T(8,128)(2,1)S(1)}, u32[]{:S(2)}, u32[]{:S(2)}) async-start(bf16[16,48,256]{2,1,0:T(8,128)(2,1)} %broadcast_in_dim.20), calls=%async_computation.6 | async-start | bytes 786432 | tf_op jit(solution)/shard_map/all_to_all | solution.py:32
  155.3 0.0 copy-start.2
  155.3 0.9 copy-done.2
  156.1 1.8 %convert_add_fusion = f32[768,512]{1,0:T(8,128)S(1)} fusion(f32[768,512]{1,0:T(8,128)} %get-tuple-element.25, bf16[768,512]{1,0:T(8,128)(2,1)} %copy-done.2), kind=kLoop, calls=%fused_computation.3 | loop fusion | flops 786432 | bytes 3932160 | tf_op jit(solution)/shard_map/add | solution.py:159
  158.0 0.1 slice.99
  158.0 4.7 %collective-permute-start.8 = (bf16[768,256]{1,0:T(8,128)(2,1)S(1)}, bf16[768,256]{1,0:T(8,128)(2,1)}, u32[]{:S(2)}, u32[]{:S(2)}) collective-permute-start(bf16[768,256]{1,0:T(8,128)(2,1)S(1)} %slice.99), channel_id=1, source_target_pairs={{0,8},{8,0},{1,9},{9,1},{2,10},{10,2},{3,11},{11,3},{4,12},{12,4},... | collective-permute-start | bytes 1179656 | tf_op jit(solution)/shard_map/ppermute | solution.py:22
  162.8 2.2 %all-to-all-done.6 = bf16[16,48,256]{2,1,0:T(8,128)(2,1)S(1)} async-done(((bf16[16,48,256]{2,1,0:T(8,128)(2,1)}), bf16[16,48,256]{2,1,0:T(8,128)(2,1)S(1)}, u32[]{:S(2)}, u32[]{:S(2)}) %all-to-all-start.6) | async-done | bytes 393248 | tf_op jit(solution)/shard_map/all_to_all | solution.py:32
  165.0 1.0 bitcast_convert_fusion
  166.0 7.4 %collective-permute-done.8 = bf16[768,256]{1,0:T(8,128)(2,1)} collective-permute-done((bf16[768,256]{1,0:T(8,128)(2,1)S(1)}, bf16[768,256]{1,0:T(8,128)(2,1)}, u32[]{:S(2)}, u32[]{:S(2)}) %collective-permute-start.8) | collective-permute-done | bytes 393248 | tf_op jit(solution)/shard_map/ppermute | solution.py:22
  173.4 2.0 %fusion.3 = f32[768,256]{1,0:T(8,128)} fusion(f32[768,512]{1,0:T(8,128)S(1)} %convert_add_fusion, bf16[768,256]{1,0:T(8,128)(2,1)} %collective-permute-done.8), kind=kLoop, calls=%fused_computation.8 | loop fusion | flops 589824 | bytes 1966080 | tf_op jit(solution)/shard_map/mul | solution.py:162
  (39 shorter events, 0.5 us)
Async XLA Ops:
  0.6 1.2 copy-start
  6.0 22.5 %all-to-all-start = ((f32[16,72,128]{2,1,0:T(8,128)}), f32[16,72,128]{2,1,0:T(8,128)S(1)}, u32[]{:S(2)}, u32[]{:S(2)}) async-start(f32[16,72,128]{2,1,0:T(8,128)} %pad_maximum_fusion), calls=%async_computation | async-start | bytes 1179648 | tf_op jit(solution)/shard_map/all_to_all | solution.py:32
  18.7 6.6 %copy-start.5 = (s32[1,1024]{1,0:T(1,128)S(1)}, s32[1,1024]{1,0:T(1,128)}, u32[]{:S(2)}) copy-start(s32[1,1024]{1,0:T(1,128)} %param.11) | copy-start | bytes 12292
  18.8 26.7 %collective-permute-start = (bf16[1024,256]{1,0:T(8,128)(2,1)S(1)}, bf16[1024,256]{1,0:T(8,128)(2,1)}, u32[]{:S(2)}, u32[]{:S(2)}) collective-permute-start(bf16[1024,256]{1,0:T(8,128)(2,1)S(1)} %pad_maximum_fusion.2), channel_id=1, source_target_pairs={{0,2},{2,4},{4,6},{6,0},{1,3},{3,5},{5,7},{7,1},{8,10},{10,12},{12... | collective-permute-start | bytes 1572872 | tf_op jit(solution)/shard_map/ppermute | solution.py:26
  22.1 23.3 %collective-permute-start.1 = (bf16[1024,256]{1,0:T(8,128)(2,1)S(1)}, bf16[1024,256]{1,0:T(8,128)(2,1)}, u32[]{:S(2)}, u32[]{:S(2)}) collective-permute-start(bf16[1024,256]{1,0:T(8,128)(2,1)S(1)} %pad_maximum_fusion.3), channel_id=1, source_target_pairs={{0,6},{2,0},{4,2},{6,4},{1,7},{3,1},{5,3},{7,5},{8,14},{10,8},{12,... | collective-permute-start | bytes 1572872 | tf_op jit(solution)/shard_map/ppermute | solution.py:26
  29.3 13.6 %all-to-all-start.1 = ((bf16[16,64,128]{2,1,0:T(8,128)(2,1)}), bf16[16,64,128]{2,1,0:T(8,128)(2,1)S(1)}, u32[]{:S(2)}, u32[]{:S(2)}) async-start(bf16[16,64,128]{2,1,0:T(8,128)(2,1)} %broadcast_in_dim.15), calls=%async_computation.1 | async-start | bytes 524288 | tf_op jit(solution)/shard_map/all_to_all | solution.py:32
  45.4 25.4 %all-to-all-start.2 = ((bf16[4,88,256]{2,1,0:T(8,128)(2,1)}), bf16[4,88,256]{2,1,0:T(8,128)(2,1)S(1)}, u32[]{:S(2)}, u32[]{:S(2)}) async-start(bf16[4,88,256]{2,1,0:T(8,128)(2,1)} %pad_maximum_fusion.7), calls=%async_computation.2 | async-start | bytes 360448 | tf_op jit(solution)/shard_map/all_to_all | solution.py:32
  59.5 15.9 %collective-permute-start.2 = (bf16[1024,256]{1,0:T(8,128)(2,1)S(1)}, bf16[1024,256]{1,0:T(8,128)(2,1)S(1)}, u32[]{:S(2)}, u32[]{:S(2)}) collective-permute-start(bf16[1024,256]{1,0:T(8,128)(2,1)S(1)} %pad_maximum_fusion.4), channel_id=1, source_target_pairs={{0,4},{2,6},{4,0},{6,2},{1,5},{3,7},{5,1},{7,3},{8,12},{10,14},{12... | collective-permute-start | bytes 1572872 | tf_op jit(solution)/shard_map/ppermute | solution.py:26
  75.4 14.1 %copy-start.6 = (bf16[1024,256]{1,0:T(8,128)(2,1)}, bf16[1024,256]{1,0:T(8,128)(2,1)S(1)}, u32[]{:S(2)}) copy-start(bf16[1024,256]{1,0:T(8,128)(2,1)S(1)} %collective-permute-done.2.refs_2_) | copy-start | bytes 1572868
  89.5 48.3 %copy-start.1 = (bf16[4,8,24,256]{3,2,1,0:T(8,128)(2,1)}, bf16[4,8,24,256]{3,2,1,0:T(8,128)(2,1)S(1)}, u32[]{:S(2)}) copy-start(bf16[4,8,24,256]{3,2,1,0:T(8,128)(2,1)S(1)} %copy.21) | copy-start | bytes 1179652
  89.5 23.2 %collective-permute-start.4 = (bf16[768,256]{1,0:T(8,128)(2,1)S(1)}, bf16[768,256]{1,0:T(8,128)(2,1)S(1)}, u32[]{:S(2)}, u32[]{:S(2)}) collective-permute-start(bf16[768,256]{1,0:T(8,128)(2,1)S(1)} %bitcast.66), channel_id=1, source_target_pairs={{0,6},{2,0},{4,2},{6,4},{1,7},{3,1},{5,3},{7,5},{8,14},{10,8},{12,... | collective-permute-start | bytes 1179656 | tf_op jit(solution)/shard_map/ppermute | solution.py:26
  94.5 18.2 %collective-permute-start.3 = (bf16[768,256]{1,0:T(8,128)(2,1)S(1)}, bf16[768,256]{1,0:T(8,128)(2,1)S(1)}, u32[]{:S(2)}, u32[]{:S(2)}) collective-permute-start(bf16[768,256]{1,0:T(8,128)(2,1)S(1)} %bitcast.67), channel_id=1, source_target_pairs={{0,2},{2,4},{4,6},{6,0},{1,3},{3,5},{5,7},{7,1},{8,10},{10,12},{12... | collective-permute-start | bytes 1179656 | tf_op jit(solution)/shard_map/ppermute | solution.py:26
  112.7 25.0 %copy-start.3 = (bf16[768,256]{1,0:T(8,128)(2,1)}, bf16[768,256]{1,0:T(8,128)(2,1)S(1)}, u32[]{:S(2)}) copy-start(bf16[768,256]{1,0:T(8,128)(2,1)S(1)} %collective-permute-done.4.right) | copy-start | bytes 1179652
  112.8 13.2 %copy-start.4 = (bf16[768,256]{1,0:T(8,128)(2,1)}, bf16[768,256]{1,0:T(8,128)(2,1)S(1)}, u32[]{:S(2)}) copy-start(bf16[768,256]{1,0:T(8,128)(2,1)S(1)} %collective-permute-done.3.left) | copy-start | bytes 1179652
  113.5 24.2 %all-to-all-start.5 = ((bf16[32,8,128]{2,1,0:T(8,128)(2,1)}), bf16[32,8,128]{2,1,0:T(8,128)(2,1)S(1)}, u32[]{:S(2)}, u32[]{:S(2)}) async-start(bf16[32,8,128]{2,1,0:T(8,128)(2,1)} %broadcast_in_dim.19), calls=%async_computation.5 | async-start | bytes 131072 | tf_op jit(solution)/shard_map/all_to_all | solution.py:32
  126.0 11.7 %collective-permute-start.6 = (bf16[384,256]{1,0:T(8,128)(2,1)S(1)}, bf16[384,256]{1,0:T(8,128)(2,1)S(1)}, u32[]{:S(2)}, u32[]{:S(2)}) collective-permute-start(bf16[384,256]{1,0:T(8,128)(2,1)S(1)} %slice.57), channel_id=1, source_target_pairs={{0,6},{2,0},{4,2},{6,4},{1,7},{3,1},{5,3},{7,5},{8,14},{10,8},{12,... | collective-permute-start | bytes 589832 | tf_op jit(solution)/shard_map/ppermute | solution.py:26
  128.9 8.8 %collective-permute-start.5 = (bf16[384,256]{1,0:T(8,128)(2,1)S(1)}, bf16[384,256]{1,0:T(8,128)(2,1)S(1)}, u32[]{:S(2)}, u32[]{:S(2)}) collective-permute-start(bf16[384,256]{1,0:T(8,128)(2,1)S(1)} %slice.56), channel_id=1, source_target_pairs={{0,2},{2,4},{4,6},{6,0},{1,3},{3,5},{5,7},{7,1},{8,10},{10,12},{12... | collective-permute-start | bytes 589832 | tf_op jit(solution)/shard_map/ppermute | solution.py:26
  137.7 0.7 copy-start.7
  138.4 0.7 copy-start.8
  146.9 8.3 %collective-permute-start.7 = (bf16[768,512]{1,0:T(8,128)(2,1)}, bf16[768,512]{1,0:T(8,128)(2,1)S(1)}, u32[]{:S(2)}, u32[]{:S(2)}) collective-permute-start(bf16[768,512]{1,0:T(8,128)(2,1)} %get-tuple-element.26), channel_id=1, source_target_pairs={{0,1},{1,0},{2,3},{3,2},{4,5},{5,4},{6,7},{7,6},{8,9},{9,8},{10,11... | collective-permute-start | bytes 2359304 | tf_op jit(solution)/shard_map/ppermute | solution.py:22
  151.8 13.2 %all-to-all-start.6 = ((bf16[16,48,256]{2,1,0:T(8,128)(2,1)}), bf16[16,48,256]{2,1,0:T(8,128)(2,1)S(1)}, u32[]{:S(2)}, u32[]{:S(2)}) async-start(bf16[16,48,256]{2,1,0:T(8,128)(2,1)} %broadcast_in_dim.20), calls=%async_computation.6 | async-start | bytes 786432 | tf_op jit(solution)/shard_map/all_to_all | solution.py:32
  155.3 0.9 copy-start.2
  158.0 15.3 %collective-permute-start.8 = (bf16[768,256]{1,0:T(8,128)(2,1)S(1)}, bf16[768,256]{1,0:T(8,128)(2,1)}, u32[]{:S(2)}, u32[]{:S(2)}) collective-permute-start(bf16[768,256]{1,0:T(8,128)(2,1)S(1)} %slice.99), channel_id=1, source_target_pairs={{0,8},{8,0},{1,9},{9,1},{2,10},{10,2},{3,11},{11,3},{4,12},{12,4},... | collective-permute-start | bytes 1179656 | tf_op jit(solution)/shard_map/ppermute | solution.py:22

commit v5 on v4

--- a/solution.py
+++ b/solution.py
@@ -9,10 +9,9 @@
 
 EX_DEV = 24
 DOCS = 256
-AXES = ("zh", "zl", "yl", "yh", "x", "c")
-SIZES = (4, 4, 2, 2, 4, 2)
-DP = ("zh", "zl", "yl")
-NEAR = ("zl", "yl")
+AXES = ("z", "yl", "yh", "x", "c")
+SIZES = (16, 2, 2, 4, 2)
+DP = ("z", "yl")
 TENSOR = ("yh", "x", "c")
 BF16 = jnp.bfloat16
 F32 = jnp.float32
@@ -58,7 +57,7 @@
 
 def partial(queries, stored):
     (height, width), count = queries[0].shape, stored[0].shape[0]
-    tile, half = 128, count // 2
+    tile, half = height // 2, count // 2
     steps = height // tile
     rows = pl.BlockSpec((tile, width), lambda i: (i, 0))
     upper = pl.BlockSpec((tile, width), lambda i: (jnp.minimum(i, steps // 2 - 1), 0))
@@ -111,7 +110,8 @@
 
     doc_hot = (jnp.arange(DOCS, dtype=jnp.int32)[:, None] == all_owners[None, :]).astype(BF16)
     doc_sums = jnp.dot(doc_hot, train_logs, preferred_element_type=F32).astype(BF16)
-    far = jnp.concatenate([to_all(query_block, 4), doc_sums.reshape(4, DOCS // 4, width)], axis=1)
+    own_docs = DOCS // 32
+    second = jnp.concatenate([to_all(query_block, 32), doc_sums.reshape(32, own_docs, width)], axis=1)
 
     blocks = train_logs.reshape(2, 4, 2, logs // 16, width)
 
@@ -122,45 +122,28 @@
         return jnp.concatenate([block(1 - yh, 1 - c), block(yh, 1 - c), block(1 - yh, c), block(yh, c)])
 
     stored = [along_x(rows_for((x + d) % 4), d) for d in range(4)]
-    far, stored[1], stored[3] = lax.optimization_barrier((far, stored[1], stored[3]))
-    far = exchange(far, "zh")
+    second, stored[1], stored[3] = lax.optimization_barrier((second, stored[1], stored[3]))
+    second = exchange(second, DP)
+    second, stored[2] = lax.optimization_barrier((second, stored[2]))
+    queries = second[:, :EX_DEV].reshape(32 * EX_DEV, width)
+    height = queries.shape[0]
 
-    docs = jnp.sum(far[:, EX_DEV:].astype(F32), axis=0)
-    high, low = split(docs)
-    own_docs = DOCS // 32
-    near = jnp.concatenate(
-        [
-            to_all(far[:, :EX_DEV].reshape(4 * EX_DEV, width), 8),
-            high.reshape(8, own_docs, width),
-            low.reshape(8, own_docs, width),
-        ],
-        axis=1,
-    )
-    near, stored[2] = lax.optimization_barrier((near, stored[2]))
-    near = exchange(near, NEAR)
-    queries = near[:, : 4 * EX_DEV].reshape(8, 4, EX_DEV, width).transpose(1, 0, 2, 3).reshape(32 * EX_DEV, width)
-    docs = jnp.sum(near[:, 4 * EX_DEV :].astype(F32), axis=0)
-    high, low = split(docs[:own_docs] + docs[own_docs:])
+    left, right = along_x(queries, 1), along_x(queries, 3)
+
+    high, low = split(jnp.sum(second[:, EX_DEV:].astype(F32), axis=0))
     doc_part = dot_t(high, queries) + dot_t(low, queries)
+    doc_part = jnp.sum(exchange(to_all(doc_part, 16), TENSOR), axis=0)
+    doc_part = (doc_part * (0.125 / math.sqrt(logs * 32 / DOCS))).astype(BF16)
+    doc_part, left, right = lax.optimization_barrier((doc_part, left, right))
+    doc_influence = exchange(to_all(doc_part, 32), DP).reshape(DOCS, height).T.astype(F32)
 
-    height = queries.shape[0]
-    share = height // 16
-    left, right = along_x(queries, 1), along_x(queries, 3)
-    doc_part = jnp.pad(doc_part.reshape(own_docs, 16, share), ((0, 0), (0, 0), (0, 128 - share))).transpose(1, 0, 2)
-    doc_part = jnp.sum(exchange(doc_part, TENSOR), axis=0)
-    scale = 0.125 / math.sqrt(logs * 32 / DOCS)
-    doc_part = to_all((doc_part * scale).astype(BF16), 32)
-    doc_part, left, right = lax.optimization_barrier((doc_part, left, right))
-    influence = exchange(doc_part, DP).reshape(DOCS, 128)[:, :share].T
     across = [along_x(left[: height // 2], 1), along_x(right[height // 2 :], 3)]
-    *across, influence = lax.optimization_barrier((*across, influence))
 
     away, kept = partial([queries, left, *across, right], stored)
     kept = kept + swap(away, "c").astype(F32)
     quarter = kept.shape[1] // 2
     beyond = swap(kept[:, :quarter].astype(BF16), "yh")
     scores = (kept[:, quarter:] + beyond.astype(F32)) * 0.125
-    doc_influence = exchange(to_all(influence, 16), TENSOR).reshape(height, DOCS).astype(F32)
     return (scores, doc_influence)
 
 

time: 177 us -> 171 us (0.966)
  waiting for transfers between devices: 36.8 us -> 69.5 us
  blocking collectives: 29.5 us -> 0 us
  starting transfers between devices: 74.4 us -> 71 us
  Pallas kernels: 7.86 us -> 5.02 us
  other arithmetic: 10.6 us -> 8.62 us
    all_to_all x2 -> x0, blocking collectives: 29.5 us -> none  [exchange(): return lax.all_to_all(flat, axes, 0, 0, tiled=True).reshape(shape)]
    ppermute x7, waiting for transfers between devices: 4.41 us -> 23.6 us  [along_x(): lax.ppermute(value, 'x', [(i, (i + distance) % 4) for i in range(4)])]
    all_to_all x5, waiting for transfers between devices: 25 us -> 34.7 us  [exchange(): return lax.all_to_all(flat, axes, 0, 0, tiled=True).reshape(shape)]
    ppermute x2, waiting for transfers between devices: 7.42 us -> 11.3 us  [swap(): return lax.ppermute(value, axis, [(0, 1), (1, 0)])]
    all_to_all x5, starting transfers between devices: 42.9 us -> 39.9 us  [exchange(): return lax.all_to_all(flat, axes, 0, 0, tiled=True).reshape(shape)]
    pallas_call x1, Pallas kernels: 7.86 us -> 5.02 us  [partial(): pl.pallas_call(partial_kernel, grid=(steps,), out_shape=(jax.ShapeDtypeSt...]
  transfers between devices with their start and end apart: 14 -> 14, of which waited for: 7 -> 11; matrix products, arithmetic and copies ran while one was open for 9% -> 9% of each run, Pallas kernels for 0% -> 0%
where the time goes in v5:
time: 171 us; the launch traced here: 170 us
  starting transfers between devices  71 us (42%)
  waiting for transfers between devices  69.5 us (41%)
  other arithmetic  8.62 us (5%)
  local copies, waits for them, and re-layouts  8.08 us (5%)
  matrix products  6.56 us (4%)
  Pallas kernels  5.02 us (3%)
    all_to_all x5, starting transfers between devices, exchange(): return lax.all_to_all(flat, axes, 0, 0, tiled=True).reshape(shape)  39.9 us
    all_to_all x5, waiting for transfers between devices, exchange(): return lax.all_to_all(flat, axes, 0, 0, tiled=True).reshape(shape)  34.7 us
    ppermute x7, waiting for transfers between devices, along_x(): lax.ppermute(value, 'x', [(i, (i + distance) % 4) for i in range(4)])  23.6 us
    ppermute x7, starting transfers between devices, along_x(): lax.ppermute(value, 'x', [(i, (i + distance) % 4) for i in range(4)])  22.2 us
    ppermute x2, waiting for transfers between devices, swap(): return lax.ppermute(value, axis, [(0, 1), (1, 0)])  11.3 us
    ppermute x2, starting transfers between devices, swap(): return lax.ppermute(value, axis, [(0, 1), (1, 0)])  8.91 us
    pallas_call x1, Pallas kernels, partial(): pl.pallas_call(partial_kernel, grid=(steps,), out_shape=(jax.ShapeDtypeSt...  5.02 us
  transfers between devices with their start and end apart: 14, of which 11 were waited for; matrix products, arithmetic and copies ran while one was open for 9% of the time, Pallas kernels for 0%

profile of v5, /device:TPU:1, one launch (start us, length us, event | category | flops | bytes accessed | tf_op | source)
XLA Modules:
  0.0 169.8 jit_solution(9345791987009702864)
XLA Ops:
  0.6 0.0 copy-start
  0.6 0.8 convert_bitcast_fusion.1
  1.4 0.5 copy-done
  1.9 1.3 fusion.11
  3.1 1.7 fusion.12
  4.9 0.2 copy.16
  5.1 0.9 pad_maximum_fusion
  5.9 10.3 %all-to-all-start = ((f32[16,72,128]{2,1,0:T(8,128)}), f32[16,72,128]{2,1,0:T(8,128)S(1)}, u32[]{:S(2)}, u32[]{:S(2)}) async-start(f32[16,72,128]{2,1,0:T(8,128)} %pad_maximum_fusion), calls=%async_computation | async-start | bytes 1179648 | tf_op jit(solution)/shard_map/all_to_all | solution.py:31
  16.2 2.5 %dynamic-slice_bitcast_fusion.3 = (bf16[256,256]{1,0:T(8,128)(2,1)S(1)}, bf16[256,256]{1,0:T(8,128)(2,1)S(1)}, bf16[256,256]{1,0:T(8,128)(2,1)S(1)}, bf16[256,25...) fusion(bf16[2,4,2,256,256]{4,3,2,1,0:T(8,128)(2,1)} %bitcast.64, ...), kind=kLoop, calls=%fused_computation.25 | loop fusion | bytes 4194336 | tf_op jit(solution)/shard_map/reshape | solution.py:120
  18.8 3.3 %collective-permute-start = (bf16[1024,256]{1,0:T(8,128)(2,1)S(1)}, bf16[1024,256]{1,0:T(8,128)(2,1)}, u32[]{:S(2)}, u32[]{:S(2)}) collective-permute-start(bf16[1024,256]{1,0:T(8,128)(2,1)S(1)} %pad_maximum_fusion.3), channel_id=1, source_target_pairs={{0,2},{2,4},{4,6},{6,0},{1,3},{3,5},{5,7},{7,1},{8,10},{10,12},{12... | collective-permute-start | bytes 1572872 | tf_op jit(solution)/shard_map/ppermute | solution.py:25
  22.1 3.2 %collective-permute-start.1 = (bf16[1024,256]{1,0:T(8,128)(2,1)S(1)}, bf16[1024,256]{1,0:T(8,128)(2,1)}, u32[]{:S(2)}, u32[]{:S(2)}) collective-permute-start(bf16[1024,256]{1,0:T(8,128)(2,1)S(1)} %pad_maximum_fusion.4), channel_id=1, source_target_pairs={{0,6},{2,0},{4,2},{6,4},{1,7},{3,1},{5,3},{7,5},{8,14},{10,8},{12,... | collective-permute-start | bytes 1572872 | tf_op jit(solution)/shard_map/ppermute | solution.py:25
  25.3 0.0 copy-done.4
  25.3 0.1 convert_reduce_fusion.1
  25.5 3.0 %all-to-all-done = f32[16,72,128]{2,1,0:T(8,128)S(1)} async-done(((f32[16,72,128]{2,1,0:T(8,128)}), f32[16,72,128]{2,1,0:T(8,128)S(1)}, u32[]{:S(2)}, u32[]{:S(2)}) %all-to-all-start) | async-done | bytes 589856 | tf_op jit(solution)/shard_map/all_to_all | solution.py:31
  28.5 0.8 broadcast_in_dim.11
  29.3 4.6 %all-to-all-start.1 = ((bf16[16,64,128]{2,1,0:T(8,128)(2,1)}), bf16[16,64,128]{2,1,0:T(8,128)(2,1)S(1)}, u32[]{:S(2)}, u32[]{:S(2)}) async-start(bf16[16,64,128]{2,1,0:T(8,128)(2,1)} %broadcast_in_dim.11), calls=%async_computation.1 | async-start | bytes 524288 | tf_op jit(solution)/shard_map/all_to_all | solution.py:31
  33.9 3.0 %fusion.3 = bf16[32,8,256]{2,1,0:T(8,128)(2,1)} fusion(bf16[4096,256]{1,0:T(8,128)(2,1)} %param.12, s32[4096]{0:T(1024)S(1)} %bitcast.66), kind=kOutput, calls=%fused_computation.5 | convolution fusion | flops 537985024 | bytes 2244608 | tf_op jit(solution)/shard_map/dot_general | solution.py:112
  36.8 6.0 %all-to-all-done.1 = bf16[16,64,128]{2,1,0:T(8,128)(2,1)S(1)} async-done(((bf16[16,64,128]{2,1,0:T(8,128)(2,1)}), bf16[16,64,128]{2,1,0:T(8,128)(2,1)S(1)}, u32[]{:S(2)}, u32[]{:S(2)}) %all-to-all-start.1) | async-done | bytes 262176 | tf_op jit(solution)/shard_map/all_to_all | solution.py:31
  42.9 0.1 slice.42
  43.0 0.1 constant_dynamic-slice_fusion
  43.2 0.1 copy.17
  43.3 0.1 broadcast_multiply_fusion
  43.4 0.1 mul.44
  43.5 0.2 fusion.5
  43.7 0.1 reshape.160
  43.8 0.1 divide_convert_fusion
  43.9 1.8 %pad_maximum_fusion.2 = bf16[32,32,256]{2,1,0:T(8,128)(2,1)} fusion(bf16[32,8,256]{2,1,0:T(8,128)(2,1)} %fusion.3, bf16[32,24,256]{2,1,0:T(8,128)(2,1)S(1)} %broadcast_in_dim.12), kind=kLoop, calls=%fused_computation.14 | loop fusion | flops 1048576 | bytes 1048576 | tf_op jit(solution)/shard_map/concatenate | solution.py:114
  45.6 0.0 collective-permute-done.refs_1_
  45.6 0.0 collective-permute-done.1.refs_3_
  45.6 13.5 %all-to-all-start.2 = ((bf16[32,32,256]{2,1,0:T(8,128)(2,1)}), bf16[32,32,256]{2,1,0:T(8,128)(2,1)S(1)}, u32[]{:S(2)}, u32[]{:S(2)}) async-start(bf16[32,32,256]{2,1,0:T(8,128)(2,1)} %pad_maximum_fusion.2), calls=%async_computation.2 | async-start | bytes 1048576 | tf_op jit(solution)/shard_map/all_to_all | solution.py:31
  59.1 1.1 pad_maximum_fusion.5
  60.2 4.0 %collective-permute-start.2 = (bf16[1024,256]{1,0:T(8,128)(2,1)S(1)}, bf16[1024,256]{1,0:T(8,128)(2,1)}, u32[]{:S(2)}, u32[]{:S(2)}) collective-permute-start(bf16[1024,256]{1,0:T(8,128)(2,1)S(1)} %pad_maximum_fusion.5), channel_id=1, source_target_pairs={{0,4},{2,6},{4,0},{6,2},{1,5},{3,7},{5,1},{7,3},{8,12},{10,14},{12... | collective-permute-start | bytes 1572872 | tf_op jit(solution)/shard_map/ppermute | solution.py:25
  64.3 12.0 %collective-permute-done.2.refs_2_ = bf16[1024,256]{1,0:T(8,128)(2,1)} collective-permute-done((bf16[1024,256]{1,0:T(8,128)(2,1)S(1)}, bf16[1024,256]{1,0:T(8,128)(2,1)}, u32[]{:S(2)}, u32[]{:S(2)}) %collective-permute-start.2) | collective-permute-done | bytes 524320 | tf_op jit(solution)/shard_map/ppermute | solution.py:25
  76.2 13.9 %all-to-all-done.2 = bf16[32,32,256]{2,1,0:T(8,128)(2,1)S(1)} async-done(((bf16[32,32,256]{2,1,0:T(8,128)(2,1)}), bf16[32,32,256]{2,1,0:T(8,128)(2,1)S(1)}, u32[]{:S(2)}, u32[]{:S(2)}) %all-to-all-start.2) | async-done | bytes 524320 | tf_op jit(solution)/shard_map/all_to_all | solution.py:31
  90.2 0.2 fusion.10
  90.4 0.3 convolution_add_fusion
  90.6 0.8 broadcast_in_dim.13
  91.5 7.7 %all-to-all-start.3 = ((f32[16,8,768]{2,1,0:T(8,128)}), f32[16,8,768]{2,1,0:T(8,128)S(1)}, u32[]{:S(2)}, u32[]{:S(2)}) async-start(f32[16,8,768]{2,1,0:T(8,128)} %broadcast_in_dim.13), calls=%async_computation.3 | async-start | bytes 786432 | tf_op jit(solution)/shard_map/all_to_all | solution.py:31
  99.1 4.5 %collective-permute-start.4 = (bf16[768,256]{1,0:T(8,128)(2,1)S(1)}, bf16[768,256]{1,0:T(8,128)(2,1)S(1)}, u32[]{:S(2)}, u32[]{:S(2)}) collective-permute-start(bf16[768,256]{1,0:T(8,128)(2,1)S(1)} %bitcast.59), channel_id=1, source_target_pairs={{0,6},{2,0},{4,2},{6,4},{1,7},{3,1},{5,3},{7,5},{8,14},{10,8},{12,... | collective-permute-start | bytes 1179656 | tf_op jit(solution)/shard_map/ppermute | solution.py:25
  103.6 1.9 %collective-permute-start.3 = (bf16[768,256]{1,0:T(8,128)(2,1)S(1)}, bf16[768,256]{1,0:T(8,128)(2,1)S(1)}, u32[]{:S(2)}, u32[]{:S(2)}) collective-permute-start(bf16[768,256]{1,0:T(8,128)(2,1)S(1)} %bitcast.60), channel_id=1, source_target_pairs={{0,2},{2,4},{4,6},{6,0},{1,3},{3,5},{5,7},{7,1},{8,10},{10,12},{12... | collective-permute-start | bytes 1179656 | tf_op jit(solution)/shard_map/ppermute | solution.py:25
  105.6 3.3 %all-to-all-done.3 = f32[16,8,768]{2,1,0:T(8,128)S(1)} async-done(((f32[16,8,768]{2,1,0:T(8,128)}), f32[16,8,768]{2,1,0:T(8,128)S(1)}, u32[]{:S(2)}, u32[]{:S(2)}) %all-to-all-start.3) | async-done | bytes 393248 | tf_op jit(solution)/shard_map/all_to_all | solution.py:31
  109.0 5.2 %collective-permute-done.4.right = bf16[768,256]{1,0:T(8,128)(2,1)S(1)} collective-permute-done((bf16[768,256]{1,0:T(8,128)(2,1)S(1)}, bf16[768,256]{1,0:T(8,128)(2,1)S(1)}, u32[]{:S(2)}, u32[]{:S(2)}) %collective-permute-start.4) | collective-permute-done | bytes 393248 | tf_op jit(solution)/shard_map/ppermute | solution.py:25
  114.1 2.6 %collective-permute-done.3.left = bf16[768,256]{1,0:T(8,128)(2,1)S(1)} collective-permute-done((bf16[768,256]{1,0:T(8,128)(2,1)S(1)}, bf16[768,256]{1,0:T(8,128)(2,1)S(1)}, u32[]{:S(2)}, u32[]{:S(2)}) %collective-permute-start.3) | collective-permute-done | bytes 393248 | tf_op jit(solution)/shard_map/ppermute | solution.py:25
  116.8 1.9 %collective-permute-start.6 = (bf16[384,256]{1,0:T(8,128)(2,1)S(1)}, bf16[384,256]{1,0:T(8,128)(2,1)S(1)}, u32[]{:S(2)}, u32[]{:S(2)}) collective-permute-start(bf16[384,256]{1,0:T(8,128)(2,1)S(1)} %slice.38), channel_id=1, source_target_pairs={{0,6},{2,0},{4,2},{6,4},{1,7},{3,1},{5,3},{7,5},{8,14},{10,8},{12,... | collective-permute-start | bytes 589832 | tf_op jit(solution)/shard_map/ppermute | solution.py:25
  118.7 3.4 %collective-permute-start.5 = (bf16[384,256]{1,0:T(8,128)(2,1)S(1)}, bf16[384,256]{1,0:T(8,128)(2,1)S(1)}, u32[]{:S(2)}, u32[]{:S(2)}) collective-permute-start(bf16[384,256]{1,0:T(8,128)(2,1)S(1)} %slice.37), channel_id=1, source_target_pairs={{0,2},{2,4},{4,6},{6,0},{1,3},{3,5},{5,7},{7,1},{8,10},{10,12},{12... | collective-permute-start | bytes 589832 | tf_op jit(solution)/shard_map/ppermute | solution.py:25
  122.1 0.8 pad_maximum_fusion.6.refs_0_
  122.9 0.7 collective-permute-done.6.lower
  123.6 3.1 %collective-permute-done.5.upper = bf16[384,256]{1,0:T(8,128)(2,1)S(1)} collective-permute-done((bf16[384,256]{1,0:T(8,128)(2,1)S(1)}, bf16[384,256]{1,0:T(8,128)(2,1)S(1)}, u32[]{:S(2)}, u32[]{:S(2)}) %collective-permute-start.5) | collective-permute-done | bytes 196640 | tf_op jit(solution)/shard_map/ppermute | solution.py:25
  126.7 0.0 copy-done.2
  126.7 0.0 copy-done.5
  126.7 0.7 copy-done.6
  127.4 5.0 %shard_map.86 = (bf16[768,512]{1,0:T(8,128)(2,1)}, f32[768,512]{1,0:T(8,128)}) custom-call(bf16[768,256]{1,0:T(8,128)(2,1)} %bitcast.61, bf16[768,256]{1,0:T(8,128)(2,1)} %copy-done.3, bf16[384,256]{1,0:T(8,128)(2,1)} %copy-done.6, bf16[384,256]{1,0:T(8,128)(2,1)} %copy-done.5, bf16[768,256]{1,0:T(8,128)(2,1)} %copy-done.2, ...), custom_call_target="tpu_custom_call" | custom-call | flops 1610612736 | bytes 6291456 | tf_op jit(solution)/shard_map/pallas_call | solution.py:67
  132.5 4.3 %collective-permute-start.7 = (bf16[768,512]{1,0:T(8,128)(2,1)}, bf16[768,512]{1,0:T(8,128)(2,1)S(1)}, u32[]{:S(2)}, u32[]{:S(2)}) collective-permute-start(bf16[768,512]{1,0:T(8,128)(2,1)} %get-tuple-element.20), channel_id=1, source_target_pairs={{0,1},{1,0},{2,3},{3,2},{4,5},{5,4},{6,7},{7,6},{8,9},{9,8},{10,11... | collective-permute-start | bytes 2359304 | tf_op jit(solution)/shard_map/ppermute | solution.py:21
  136.8 0.8 broadcast_in_dim.14
  137.6 3.9 %all-to-all-start.4 = ((bf16[32,8,768]{2,1,0:T(8,128)(2,1)}), bf16[32,8,768]{2,1,0:T(8,128)(2,1)S(1)}, u32[]{:S(2)}, u32[]{:S(2)}) async-start(bf16[32,8,768]{2,1,0:T(8,128)(2,1)} %broadcast_in_dim.14), calls=%async_computation.4 | async-start | bytes 786432 | tf_op jit(solution)/shard_map/all_to_all | solution.py:31
  141.4 0.0 collective-permute-done.7
  141.5 1.6 convert_add_fusion
  143.1 0.1 slice.56
  143.2 4.6 %collective-permute-start.8 = (bf16[768,256]{1,0:T(8,128)(2,1)S(1)}, bf16[768,256]{1,0:T(8,128)(2,1)S(1)}, u32[]{:S(2)}, u32[]{:S(2)}) collective-permute-start(bf16[768,256]{1,0:T(8,128)(2,1)S(1)} %slice.56), channel_id=1, source_target_pairs={{0,8},{8,0},{1,9},{9,1},{2,10},{10,2},{3,11},{11,3},{4,12},{12,4},... | collective-permute-start | bytes 1179656 | tf_op jit(solution)/shard_map/ppermute | solution.py:21
  147.8 11.3 %collective-permute-done.8 = bf16[768,256]{1,0:T(8,128)(2,1)S(1)} collective-permute-done((bf16[768,256]{1,0:T(8,128)(2,1)S(1)}, bf16[768,256]{1,0:T(8,128)(2,1)S(1)}, u32[]{:S(2)}, u32[]{:S(2)}) %collective-permute-start.8) | collective-permute-done | bytes 393248 | tf_op jit(solution)/shard_map/ppermute | solution.py:21
  159.1 1.0 fusion.4
  160.1 8.5 %all-to-all-done.4 = bf16[32,8,768]{2,1,0:T(8,128)(2,1)S(1)} async-done(((bf16[32,8,768]{2,1,0:T(8,128)(2,1)}), bf16[32,8,768]{2,1,0:T(8,128)(2,1)S(1)}, u32[]{:S(2)}, u32[]{:S(2)}) %all-to-all-start.4) | async-done | bytes 393248 | tf_op jit(solution)/shard_map/all_to_all | solution.py:31
  168.6 0.1 convert_bitcast_fusion
  168.6 1.1 copy.19
  (23 shorter events, 0.4 us)
Async XLA Ops:
  0.6 1.2 copy-start
  5.9 22.5 %all-to-all-start = ((f32[16,72,128]{2,1,0:T(8,128)}), f32[16,72,128]{2,1,0:T(8,128)S(1)}, u32[]{:S(2)}, u32[]{:S(2)}) async-start(f32[16,72,128]{2,1,0:T(8,128)} %pad_maximum_fusion), calls=%async_computation | async-start | bytes 1179648 | tf_op jit(solution)/shard_map/all_to_all | solution.py:31
  18.7 6.6 %copy-start.4 = (s32[1,1024]{1,0:T(1,128)S(1)}, s32[1,1024]{1,0:T(1,128)}, u32[]{:S(2)}) copy-start(s32[1,1024]{1,0:T(1,128)} %param.11) | copy-start | bytes 12292
  18.8 26.9 %collective-permute-start = (bf16[1024,256]{1,0:T(8,128)(2,1)S(1)}, bf16[1024,256]{1,0:T(8,128)(2,1)}, u32[]{:S(2)}, u32[]{:S(2)}) collective-permute-start(bf16[1024,256]{1,0:T(8,128)(2,1)S(1)} %pad_maximum_fusion.3), channel_id=1, source_target_pairs={{0,2},{2,4},{4,6},{6,0},{1,3},{3,5},{5,7},{7,1},{8,10},{10,12},{12... | collective-permute-start | bytes 1572872 | tf_op jit(solution)/shard_map/ppermute | solution.py:25
  22.1 23.5 %collective-permute-start.1 = (bf16[1024,256]{1,0:T(8,128)(2,1)S(1)}, bf16[1024,256]{1,0:T(8,128)(2,1)}, u32[]{:S(2)}, u32[]{:S(2)}) collective-permute-start(bf16[1024,256]{1,0:T(8,128)(2,1)S(1)} %pad_maximum_fusion.4), channel_id=1, source_target_pairs={{0,6},{2,0},{4,2},{6,4},{1,7},{3,1},{5,3},{7,5},{8,14},{10,8},{12,... | collective-permute-start | bytes 1572872 | tf_op jit(solution)/shard_map/ppermute | solution.py:25
  29.3 13.6 %all-to-all-start.1 = ((bf16[16,64,128]{2,1,0:T(8,128)(2,1)}), bf16[16,64,128]{2,1,0:T(8,128)(2,1)S(1)}, u32[]{:S(2)}, u32[]{:S(2)}) async-start(bf16[16,64,128]{2,1,0:T(8,128)(2,1)} %broadcast_in_dim.11), calls=%async_computation.1 | async-start | bytes 524288 | tf_op jit(solution)/shard_map/all_to_all | solution.py:31
  45.6 44.4 %all-to-all-start.2 = ((bf16[32,32,256]{2,1,0:T(8,128)(2,1)}), bf16[32,32,256]{2,1,0:T(8,128)(2,1)S(1)}, u32[]{:S(2)}, u32[]{:S(2)}) async-start(bf16[32,32,256]{2,1,0:T(8,128)(2,1)} %pad_maximum_fusion.2), calls=%async_computation.2 | async-start | bytes 1048576 | tf_op jit(solution)/shard_map/all_to_all | solution.py:31
  60.2 16.0 %collective-permute-start.2 = (bf16[1024,256]{1,0:T(8,128)(2,1)S(1)}, bf16[1024,256]{1,0:T(8,128)(2,1)}, u32[]{:S(2)}, u32[]{:S(2)}) collective-permute-start(bf16[1024,256]{1,0:T(8,128)(2,1)S(1)} %pad_maximum_fusion.5), channel_id=1, source_target_pairs={{0,4},{2,6},{4,0},{6,2},{1,5},{3,7},{5,1},{7,3},{8,12},{10,14},{12... | collective-permute-start | bytes 1572872 | tf_op jit(solution)/shard_map/ppermute | solution.py:25
  90.2 32.8 %copy-start.1 = (bf16[32,24,256]{2,1,0:T(8,128)(2,1)}, bf16[32,24,256]{2,1,0:T(8,128)(2,1)S(1)}, u32[]{:S(2)}) copy-start(bf16[32,24,256]{2,1,0:T(8,128)(2,1)S(1)} %slice.35) | copy-start | bytes 1179652
  91.5 17.5 %all-to-all-start.3 = ((f32[16,8,768]{2,1,0:T(8,128)}), f32[16,8,768]{2,1,0:T(8,128)S(1)}, u32[]{:S(2)}, u32[]{:S(2)}) async-start(f32[16,8,768]{2,1,0:T(8,128)} %broadcast_in_dim.13), calls=%async_computation.3 | async-start | bytes 786432 | tf_op jit(solution)/shard_map/all_to_all | solution.py:31
  99.1 15.0 %collective-permute-start.4 = (bf16[768,256]{1,0:T(8,128)(2,1)S(1)}, bf16[768,256]{1,0:T(8,128)(2,1)S(1)}, u32[]{:S(2)}, u32[]{:S(2)}) collective-permute-start(bf16[768,256]{1,0:T(8,128)(2,1)S(1)} %bitcast.59), channel_id=1, source_target_pairs={{0,6},{2,0},{4,2},{6,4},{1,7},{3,1},{5,3},{7,5},{8,14},{10,8},{12,... | collective-permute-start | bytes 1179656 | tf_op jit(solution)/shard_map/ppermute | solution.py:25
  103.6 13.1 %collective-permute-start.3 = (bf16[768,256]{1,0:T(8,128)(2,1)S(1)}, bf16[768,256]{1,0:T(8,128)(2,1)S(1)}, u32[]{:S(2)}, u32[]{:S(2)}) collective-permute-start(bf16[768,256]{1,0:T(8,128)(2,1)S(1)} %bitcast.60), channel_id=1, source_target_pairs={{0,2},{2,4},{4,6},{6,0},{1,3},{3,5},{5,7},{7,1},{8,10},{10,12},{12... | collective-permute-start | bytes 1179656 | tf_op jit(solution)/shard_map/ppermute | solution.py:25
  114.1 12.6 %copy-start.2 = (bf16[768,256]{1,0:T(8,128)(2,1)}, bf16[768,256]{1,0:T(8,128)(2,1)S(1)}, u32[]{:S(2)}) copy-start(bf16[768,256]{1,0:T(8,128)(2,1)S(1)} %collective-permute-done.4.right) | copy-start | bytes 1179652
  116.8 10.0 %copy-start.3 = (bf16[768,256]{1,0:T(8,128)(2,1)}, bf16[768,256]{1,0:T(8,128)(2,1)S(1)}, u32[]{:S(2)}) copy-start(bf16[768,256]{1,0:T(8,128)(2,1)S(1)} %collective-permute-done.3.left) | copy-start | bytes 1179652
  116.8 6.8 %collective-permute-start.6 = (bf16[384,256]{1,0:T(8,128)(2,1)S(1)}, bf16[384,256]{1,0:T(8,128)(2,1)S(1)}, u32[]{:S(2)}, u32[]{:S(2)}) collective-permute-start(bf16[384,256]{1,0:T(8,128)(2,1)S(1)} %slice.38), channel_id=1, source_target_pairs={{0,6},{2,0},{4,2},{6,4},{1,7},{3,1},{5,3},{7,5},{8,14},{10,8},{12,... | collective-permute-start | bytes 589832 | tf_op jit(solution)/shard_map/ppermute | solution.py:25
  118.7 8.0 %collective-permute-start.5 = (bf16[384,256]{1,0:T(8,128)(2,1)S(1)}, bf16[384,256]{1,0:T(8,128)(2,1)S(1)}, u32[]{:S(2)}, u32[]{:S(2)}) collective-permute-start(bf16[384,256]{1,0:T(8,128)(2,1)S(1)} %slice.37), channel_id=1, source_target_pairs={{0,2},{2,4},{4,6},{6,0},{1,3},{3,5},{5,7},{7,1},{8,10},{10,12},{12... | collective-permute-start | bytes 589832 | tf_op jit(solution)/shard_map/ppermute | solution.py:25
  123.6 3.1 %copy-start.5 = (bf16[384,256]{1,0:T(8,128)(2,1)}, bf16[384,256]{1,0:T(8,128)(2,1)S(1)}, u32[]{:S(2)}) copy-start(bf16[384,256]{1,0:T(8,128)(2,1)S(1)} %collective-permute-done.6.lower) | copy-start | bytes 589828
  126.7 0.7 copy-start.6
  132.5 9.0 %collective-permute-start.7 = (bf16[768,512]{1,0:T(8,128)(2,1)}, bf16[768,512]{1,0:T(8,128)(2,1)S(1)}, u32[]{:S(2)}, u32[]{:S(2)}) collective-permute-start(bf16[768,512]{1,0:T(8,128)(2,1)} %get-tuple-element.20), channel_id=1, source_target_pairs={{0,1},{1,0},{2,3},{3,2},{4,5},{5,4},{6,7},{7,6},{8,9},{9,8},{10,11... | collective-permute-start | bytes 2359304 | tf_op jit(solution)/shard_map/ppermute | solution.py:21
  137.6 31.0 %all-to-all-start.4 = ((bf16[32,8,768]{2,1,0:T(8,128)(2,1)}), bf16[32,8,768]{2,1,0:T(8,128)(2,1)S(1)}, u32[]{:S(2)}, u32[]{:S(2)}) async-start(bf16[32,8,768]{2,1,0:T(8,128)(2,1)} %broadcast_in_dim.14), calls=%async_computation.4 | async-start | bytes 786432 | tf_op jit(solution)/shard_map/all_to_all | solution.py:31
  143.2 15.9 %collective-permute-start.8 = (bf16[768,256]{1,0:T(8,128)(2,1)S(1)}, bf16[768,256]{1,0:T(8,128)(2,1)S(1)}, u32[]{:S(2)}, u32[]{:S(2)}) collective-permute-start(bf16[768,256]{1,0:T(8,128)(2,1)S(1)} %slice.56), channel_id=1, source_target_pairs={{0,8},{8,0},{1,9},{9,1},{2,10},{10,2},{3,11},{11,3},{4,12},{12,4},... | collective-permute-start | bytes 1179656 | tf_op jit(solution)/shard_map/ppermute | solution.py:21

commit v6 on v5

--- a/solution.py
+++ b/solution.py
@@ -132,17 +132,21 @@
 
     high, low = split(jnp.sum(second[:, EX_DEV:].astype(F32), axis=0))
     doc_part = dot_t(high, queries) + dot_t(low, queries)
-    doc_part = jnp.sum(exchange(to_all(doc_part, 16), TENSOR), axis=0)
-    doc_part = (doc_part * (0.125 / math.sqrt(logs * 32 / DOCS))).astype(BF16)
-    doc_part, left, right = lax.optimization_barrier((doc_part, left, right))
-    doc_influence = exchange(to_all(doc_part, 32), DP).reshape(DOCS, height).T.astype(F32)
+    halves = doc_part.reshape(own_docs, 2, height // 2).transpose(1, 0, 2)
+    halves = jnp.broadcast_to(halves[None], (8, *halves.shape)).reshape(16, own_docs, height // 2)
+    halves = jnp.sum(exchange(halves, TENSOR), axis=0)
+    halves = (halves * (0.125 / math.sqrt(logs * 32 / DOCS))).astype(BF16)
+    halves, left, right = lax.optimization_barrier((halves, left, right))
+    halves = exchange(to_all(halves, 32), DP).reshape(DOCS, height // 2)
 
     across = [along_x(left[: height // 2], 1), along_x(right[height // 2 :], 3)]
 
+    *across, halves = lax.optimization_barrier((*across, halves))
     away, kept = partial([queries, left, *across, right], stored)
     kept = kept + swap(away, "c").astype(F32)
     quarter = kept.shape[1] // 2
     beyond = swap(kept[:, :quarter].astype(BF16), "yh")
+    doc_influence = lax.all_gather(halves, "c", axis=0).transpose(0, 2, 1).reshape(height, DOCS).astype(F32)
     scores = (kept[:, quarter:] + beyond.astype(F32)) * 0.125
     return (scores, doc_influence)
 

time: 171 us -> 170 us (level)
  waiting for transfers between devices: 69.5 us -> 63.3 us
  blocking collectives: 0 us -> 2.37 us
    all_to_all x5, waiting for transfers between devices: 34.7 us -> 30.8 us  [exchange(): return lax.all_to_all(flat, axes, 0, 0, tiled=True).reshape(shape)]
    ppermute x2, waiting for transfers between devices: 11.3 us -> 7.96 us  [swap(): return lax.ppermute(value, axis, [(0, 1), (1, 0)])]
    all_gather x0 -> x1, blocking collectives: none -> 2.37 us  [per_device(): lax.all_gather(halves, 'c', axis=0).transpose(0, 2, 1).reshape(height, DOCS)]
  transfers between devices with their start and end apart: 14 -> 14, of which waited for: 11 -> 12; matrix products, arithmetic and copies ran while one was open for 9% -> 7% of each run, Pallas kernels for 0% -> 0%
where the time goes in v6:
time: 170 us; the launch traced here: 169 us
  starting transfers between devices  71.7 us (42%)
  waiting for transfers between devices  63.3 us (37%)
  other arithmetic  9.63 us (6%)
  local copies, waits for them, and re-layouts  9.49 us (6%)
  matrix products  6.56 us (4%)
  Pallas kernels  5.05 us (3%)
  blocking collectives  2.37 us (1%)
    all_to_all x5, starting transfers between devices, exchange(): return lax.all_to_all(flat, axes, 0, 0, tiled=True).reshape(shape)  39.9 us
    all_to_all x5, waiting for transfers between devices, exchange(): return lax.all_to_all(flat, axes, 0, 0, tiled=True).reshape(shape)  30.8 us
    ppermute x7, waiting for transfers between devices, along_x(): lax.ppermute(value, 'x', [(i, (i + distance) % 4) for i in range(4)])  24.5 us
    ppermute x7, starting transfers between devices, along_x(): lax.ppermute(value, 'x', [(i, (i + distance) % 4) for i in range(4)])  22.2 us
    ppermute x2, starting transfers between devices, swap(): return lax.ppermute(value, axis, [(0, 1), (1, 0)])  9.57 us
    ppermute x2, waiting for transfers between devices, swap(): return lax.ppermute(value, axis, [(0, 1), (1, 0)])  7.96 us
    pallas_call x1, Pallas kernels, partial(): pl.pallas_call(partial_kernel, grid=(steps,), out_shape=(jax.ShapeDtypeSt...  5.05 us
  transfers between devices with their start and end apart: 14, of which 12 were waited for; matrix products, arithmetic and copies ran while one was open for 7% of the time, Pallas kernels for 0%

profile of v6, /device:TPU:1, one launch (start us, length us, event | category | flops | bytes accessed | tf_op | source)
XLA Modules:
  0.0 169.0 jit_solution(7436974654287977799)
XLA Ops:
  0.6 0.0 copy-start
  0.6 0.8 convert_bitcast_fusion.1
  1.4 0.5 copy-done
  1.9 1.3 fusion.11
  3.1 1.7 fusion.12
  4.9 0.2 copy.15
  5.1 0.9 pad_maximum_fusion
  6.0 10.3 %all-to-all-start = ((f32[16,72,128]{2,1,0:T(8,128)}), f32[16,72,128]{2,1,0:T(8,128)S(1)}, u32[]{:S(2)}, u32[]{:S(2)}) async-start(f32[16,72,128]{2,1,0:T(8,128)} %pad_maximum_fusion), calls=%async_computation | async-start | bytes 1179648 | tf_op jit(solution)/shard_map/all_to_all | solution.py:31
  16.2 2.5 %dynamic-slice_bitcast_fusion.3 = (bf16[256,256]{1,0:T(8,128)(2,1)S(1)}, bf16[256,256]{1,0:T(8,128)(2,1)S(1)}, bf16[256,256]{1,0:T(8,128)(2,1)S(1)}, bf16[256,25...) fusion(bf16[2,4,2,256,256]{4,3,2,1,0:T(8,128)(2,1)} %bitcast.69, ...), kind=kLoop, calls=%fused_computation.25 | loop fusion | bytes 4194336 | tf_op jit(solution)/shard_map/reshape | solution.py:120
  18.8 3.3 %collective-permute-start = (bf16[1024,256]{1,0:T(8,128)(2,1)S(1)}, bf16[1024,256]{1,0:T(8,128)(2,1)}, u32[]{:S(2)}, u32[]{:S(2)}) collective-permute-start(bf16[1024,256]{1,0:T(8,128)(2,1)S(1)} %pad_maximum_fusion.3), channel_id=1, source_target_pairs={{0,2},{2,4},{4,6},{6,0},{1,3},{3,5},{5,7},{7,1},{8,10},{10,12},{12... | collective-permute-start | bytes 1572872 | tf_op jit(solution)/shard_map/ppermute | solution.py:25
  22.1 3.2 %collective-permute-start.1 = (bf16[1024,256]{1,0:T(8,128)(2,1)S(1)}, bf16[1024,256]{1,0:T(8,128)(2,1)}, u32[]{:S(2)}, u32[]{:S(2)}) collective-permute-start(bf16[1024,256]{1,0:T(8,128)(2,1)S(1)} %pad_maximum_fusion.4), channel_id=1, source_target_pairs={{0,6},{2,0},{4,2},{6,4},{1,7},{3,1},{5,3},{7,5},{8,14},{10,8},{12,... | collective-permute-start | bytes 1572872 | tf_op jit(solution)/shard_map/ppermute | solution.py:25
  25.3 0.1 convert_reduce_fusion.1
  25.5 3.0 %all-to-all-done = f32[16,72,128]{2,1,0:T(8,128)S(1)} async-done(((f32[16,72,128]{2,1,0:T(8,128)}), f32[16,72,128]{2,1,0:T(8,128)S(1)}, u32[]{:S(2)}, u32[]{:S(2)}) %all-to-all-start) | async-done | bytes 589856 | tf_op jit(solution)/shard_map/all_to_all | solution.py:31
  28.5 0.8 broadcast_in_dim.11
  29.3 4.6 %all-to-all-start.1 = ((bf16[16,64,128]{2,1,0:T(8,128)(2,1)}), bf16[16,64,128]{2,1,0:T(8,128)(2,1)S(1)}, u32[]{:S(2)}, u32[]{:S(2)}) async-start(bf16[16,64,128]{2,1,0:T(8,128)(2,1)} %broadcast_in_dim.11), calls=%async_computation.1 | async-start | bytes 524288 | tf_op jit(solution)/shard_map/all_to_all | solution.py:31
  33.9 3.0 %fusion.3 = bf16[32,8,256]{2,1,0:T(8,128)(2,1)} fusion(bf16[4096,256]{1,0:T(8,128)(2,1)} %param.12, s32[4096]{0:T(1024)S(1)} %bitcast.75), kind=kOutput, calls=%fused_computation.5 | convolution fusion | flops 537985024 | bytes 2244608 | tf_op jit(solution)/shard_map/dot_general | solution.py:112
  36.8 6.0 %all-to-all-done.1 = bf16[16,64,128]{2,1,0:T(8,128)(2,1)S(1)} async-done(((bf16[16,64,128]{2,1,0:T(8,128)(2,1)}), bf16[16,64,128]{2,1,0:T(8,128)(2,1)S(1)}, u32[]{:S(2)}, u32[]{:S(2)}) %all-to-all-start.1) | async-done | bytes 262176 | tf_op jit(solution)/shard_map/all_to_all | solution.py:31
  42.9 0.1 slice.42
  43.0 0.1 constant_dynamic-slice_fusion
  43.2 0.1 copy.16
  43.3 0.1 broadcast_multiply_fusion
  43.4 0.1 mul.44
  43.5 0.2 fusion.5
  43.7 0.1 reshape.163
  43.8 0.1 divide_convert_fusion
  43.9 1.8 %pad_maximum_fusion.2 = bf16[32,32,256]{2,1,0:T(8,128)(2,1)} fusion(bf16[32,8,256]{2,1,0:T(8,128)(2,1)} %fusion.3, bf16[32,24,256]{2,1,0:T(8,128)(2,1)S(1)} %broadcast_in_dim.12), kind=kLoop, calls=%fused_computation.14 | loop fusion | flops 1048576 | bytes 1048576 | tf_op jit(solution)/shard_map/concatenate | solution.py:114
  45.6 0.0 collective-permute-done.refs_1_
  45.6 0.0 collective-permute-done.1.refs_3_
  45.6 13.5 %all-to-all-start.2 = ((bf16[32,32,256]{2,1,0:T(8,128)(2,1)}), bf16[32,32,256]{2,1,0:T(8,128)(2,1)S(1)}, u32[]{:S(2)}, u32[]{:S(2)}) async-start(bf16[32,32,256]{2,1,0:T(8,128)(2,1)} %pad_maximum_fusion.2), calls=%async_computation.2 | async-start | bytes 1048576 | tf_op jit(solution)/shard_map/all_to_all | solution.py:31
  59.1 1.1 pad_maximum_fusion.5
  60.2 4.0 %collective-permute-start.2 = (bf16[1024,256]{1,0:T(8,128)(2,1)S(1)}, bf16[1024,256]{1,0:T(8,128)(2,1)S(1)}, u32[]{:S(2)}, u32[]{:S(2)}) collective-permute-start(bf16[1024,256]{1,0:T(8,128)(2,1)S(1)} %pad_maximum_fusion.5), channel_id=1, source_target_pairs={{0,4},{2,6},{4,0},{6,2},{1,5},{3,7},{5,1},{7,3},{8,12},{10,14},{12... | collective-permute-start | bytes 1572872 | tf_op jit(solution)/shard_map/ppermute | solution.py:25
  64.3 11.8 %collective-permute-done.2.refs_2_ = bf16[1024,256]{1,0:T(8,128)(2,1)S(1)} collective-permute-done((bf16[1024,256]{1,0:T(8,128)(2,1)S(1)}, bf16[1024,256]{1,0:T(8,128)(2,1)S(1)}, u32[]{:S(2)}, u32[]{:S(2)}) %collective-permute-start.2) | collective-permute-done | bytes 524320 | tf_op jit(solution)/shard_map/ppermute | solution.py:25
  76.1 0.8 copy-done.5
  76.9 13.2 %all-to-all-done.2 = bf16[32,32,256]{2,1,0:T(8,128)(2,1)S(1)} async-done(((bf16[32,32,256]{2,1,0:T(8,128)(2,1)}), bf16[32,32,256]{2,1,0:T(8,128)(2,1)S(1)}, u32[]{:S(2)}, u32[]{:S(2)}) %all-to-all-start.2) | async-done | bytes 524320 | tf_op jit(solution)/shard_map/all_to_all | solution.py:31
  90.1 0.0 copy-start.1
  90.2 0.2 fusion.10
  90.4 0.3 convolution_add_fusion
  90.6 0.7 broadcast_in_dim.13
  91.4 7.7 %all-to-all-start.3 = ((f32[16,8,384]{2,1,0:T(8,128)}), f32[16,8,384]{2,1,0:T(8,128)S(1)}, u32[]{:S(2)}, u32[]{:S(2)}) async-start(f32[16,8,384]{2,1,0:T(8,128)} %bitcast.22), calls=%async_computation.3 | async-start | bytes 393216 | tf_op jit(solution)/shard_map/all_to_all | solution.py:31
  99.0 4.5 %collective-permute-start.4 = (bf16[768,256]{1,0:T(8,128)(2,1)S(1)}, bf16[768,256]{1,0:T(8,128)(2,1)S(1)}, u32[]{:S(2)}, u32[]{:S(2)}) collective-permute-start(bf16[768,256]{1,0:T(8,128)(2,1)S(1)} %bitcast.64), channel_id=1, source_target_pairs={{0,6},{2,0},{4,2},{6,4},{1,7},{3,1},{5,3},{7,5},{8,14},{10,8},{12,... | collective-permute-start | bytes 1179656 | tf_op jit(solution)/shard_map/ppermute | solution.py:25
  103.6 1.9 %collective-permute-start.3 = (bf16[768,256]{1,0:T(8,128)(2,1)S(1)}, bf16[768,256]{1,0:T(8,128)(2,1)S(1)}, u32[]{:S(2)}, u32[]{:S(2)}) collective-permute-start(bf16[768,256]{1,0:T(8,128)(2,1)S(1)} %bitcast.65), channel_id=1, source_target_pairs={{0,2},{2,4},{4,6},{6,0},{1,3},{3,5},{5,7},{7,1},{8,10},{10,12},{12... | collective-permute-start | bytes 1179656 | tf_op jit(solution)/shard_map/ppermute | solution.py:25
  105.5 1.7 %all-to-all-done.3 = f32[16,8,384]{2,1,0:T(8,128)S(1)} async-done(((f32[16,8,384]{2,1,0:T(8,128)}), f32[16,8,384]{2,1,0:T(8,128)S(1)}, u32[]{:S(2)}, u32[]{:S(2)}) %all-to-all-start.3) | async-done | bytes 196640 | tf_op jit(solution)/shard_map/all_to_all | solution.py:31
  107.2 4.9 %collective-permute-done.4.right = bf16[768,256]{1,0:T(8,128)(2,1)S(1)} collective-permute-done((bf16[768,256]{1,0:T(8,128)(2,1)S(1)}, bf16[768,256]{1,0:T(8,128)(2,1)S(1)}, u32[]{:S(2)}, u32[]{:S(2)}) %collective-permute-start.4) | collective-permute-done | bytes 393248 | tf_op jit(solution)/shard_map/ppermute | solution.py:25
  112.1 4.5 %collective-permute-done.3.left = bf16[768,256]{1,0:T(8,128)(2,1)S(1)} collective-permute-done((bf16[768,256]{1,0:T(8,128)(2,1)S(1)}, bf16[768,256]{1,0:T(8,128)(2,1)S(1)}, u32[]{:S(2)}, u32[]{:S(2)}) %collective-permute-start.3) | collective-permute-done | bytes 393248 | tf_op jit(solution)/shard_map/ppermute | solution.py:25
  116.7 0.7 broadcast_in_dim.14
  117.4 3.9 %all-to-all-start.4 = ((bf16[32,8,384]{2,1,0:T(8,128)(2,1)}), bf16[32,8,384]{2,1,0:T(8,128)(2,1)S(1)}, u32[]{:S(2)}, u32[]{:S(2)}) async-start(bf16[32,8,384]{2,1,0:T(8,128)(2,1)} %broadcast_in_dim.14), calls=%async_computation.4 | async-start | bytes 393216 | tf_op jit(solution)/shard_map/all_to_all | solution.py:31
  121.3 1.9 %collective-permute-start.6 = (bf16[384,256]{1,0:T(8,128)(2,1)S(1)}, bf16[384,256]{1,0:T(8,128)(2,1)S(1)}, u32[]{:S(2)}, u32[]{:S(2)}) collective-permute-start(bf16[384,256]{1,0:T(8,128)(2,1)S(1)} %slice.38), channel_id=1, source_target_pairs={{0,6},{2,0},{4,2},{6,4},{1,7},{3,1},{5,3},{7,5},{8,14},{10,8},{12,... | collective-permute-start | bytes 589832 | tf_op jit(solution)/shard_map/ppermute | solution.py:25
  123.3 3.4 %collective-permute-start.5 = (bf16[384,256]{1,0:T(8,128)(2,1)S(1)}, bf16[384,256]{1,0:T(8,128)(2,1)}, u32[]{:S(2)}, u32[]{:S(2)}) collective-permute-start(bf16[384,256]{1,0:T(8,128)(2,1)S(1)} %slice.37), channel_id=1, source_target_pairs={{0,2},{2,4},{4,6},{6,0},{1,3},{3,5},{5,7},{7,1},{8,10},{10,12},{12... | collective-permute-start | bytes 589832 | tf_op jit(solution)/shard_map/ppermute | solution.py:25
  126.6 0.8 pad_maximum_fusion.6.refs_0_
  127.5 0.7 collective-permute-done.6.lower
  128.1 0.7 copy-done.6
  128.8 2.6 %collective-permute-done.5.upper = bf16[384,256]{1,0:T(8,128)(2,1)} collective-permute-done((bf16[384,256]{1,0:T(8,128)(2,1)S(1)}, bf16[384,256]{1,0:T(8,128)(2,1)}, u32[]{:S(2)}, u32[]{:S(2)}) %collective-permute-start.5) | collective-permute-done | bytes 196640 | tf_op jit(solution)/shard_map/ppermute | solution.py:25
  131.4 6.9 %all-to-all-done.4 = bf16[32,8,384]{2,1,0:T(8,128)(2,1)S(1)} async-done(((bf16[32,8,384]{2,1,0:T(8,128)(2,1)}), bf16[32,8,384]{2,1,0:T(8,128)(2,1)S(1)}, u32[]{:S(2)}, u32[]{:S(2)}) %all-to-all-start.4) | async-done | bytes 196640 | tf_op jit(solution)/shard_map/all_to_all | solution.py:31
  138.3 5.1 %shard_map.86 = (bf16[768,512]{1,0:T(8,128)(2,1)}, f32[768,512]{1,0:T(8,128)}) custom-call(bf16[768,256]{1,0:T(8,128)(2,1)} %bitcast.66, bf16[768,256]{1,0:T(8,128)(2,1)} %copy-done.3, bf16[384,256]{1,0:T(8,128)(2,1)} %collective-permute-done.5.upper, bf16[384,256]{1,0:T(8,128)(2,1)} %copy-done.6, bf16[768,256]{1,0:T(8,128)(2,1)} %copy-done.2, ...), custom_call_target="tpu_custom_call" | custom-call | flops 1610612736 | bytes 6291456 | tf_op jit(solution)/shard_map/pallas_call | solution.py:67
  143.3 5.0 %collective-permute-start.7 = (bf16[768,512]{1,0:T(8,128)(2,1)}, bf16[768,512]{1,0:T(8,128)(2,1)S(1)}, u32[]{:S(2)}, u32[]{:S(2)}) collective-permute-start(bf16[768,512]{1,0:T(8,128)(2,1)} %get-tuple-element.26), channel_id=1, source_target_pairs={{0,1},{1,0},{2,3},{3,2},{4,5},{5,4},{6,7},{7,6},{8,9},{9,8},{10,11... | collective-permute-start | bytes 2359304 | tf_op jit(solution)/shard_map/ppermute | solution.py:21
  148.3 2.1 %collective-permute-done.7 = bf16[768,512]{1,0:T(8,128)(2,1)S(1)} collective-permute-done((bf16[768,512]{1,0:T(8,128)(2,1)}, bf16[768,512]{1,0:T(8,128)(2,1)S(1)}, u32[]{:S(2)}, u32[]{:S(2)}) %collective-permute-start.7) | collective-permute-done | bytes 786464 | tf_op jit(solution)/shard_map/ppermute | solution.py:21
  150.4 1.7 convert_add_fusion
  152.1 0.8 slice.56
  152.9 4.6 %collective-permute-start.8 = (bf16[768,256]{1,0:T(8,128)(2,1)}, bf16[768,256]{1,0:T(8,128)(2,1)}, u32[]{:S(2)}, u32[]{:S(2)}) collective-permute-start(bf16[768,256]{1,0:T(8,128)(2,1)} %slice.56), channel_id=1, source_target_pairs={{0,8},{8,0},{1,9},{9,1},{2,10},{10,2},{3,11},{11,3},{4,12},{12,4},... | collective-permute-start | bytes 1179656 | tf_op jit(solution)/shard_map/ppermute | solution.py:21
  157.5 2.4 %all-gather = bf16[512,384]{1,0:T(8,128)(2,1)S(1)} all-gather(bf16[256,384]{1,0:T(8,128)(2,1)S(1)} %bitcast.73), channel_id=2, replica_groups=mesh['z'=16,'yl'=2,'yh'=2,'x'=4,'c'=2] {'c'}, dimensions={0}, use_global_device_ids=true | all-gather | bytes 589824 | tf_op jit(solution)/shard_map/all_gather | solution.py:149
  159.9 0.1 convert_bitcast_fusion
  160.0 1.1 copy.18
  161.1 5.9 %collective-permute-done.8 = bf16[768,256]{1,0:T(8,128)(2,1)} collective-permute-done((bf16[768,256]{1,0:T(8,128)(2,1)}, bf16[768,256]{1,0:T(8,128)(2,1)}, u32[]{:S(2)}, u32[]{:S(2)}) %collective-permute-start.8) | collective-permute-done | bytes 393248 | tf_op jit(solution)/shard_map/ppermute | solution.py:21
  167.0 2.0 %fusion.4 = f32[768,256]{1,0:T(8,128)} fusion(f32[768,512]{1,0:T(8,128)S(1)} %convert_add_fusion, bf16[768,256]{1,0:T(8,128)(2,1)} %collective-permute-done.8), kind=kLoop, calls=%fused_computation.9 | loop fusion | flops 589824 | bytes 1966080 | tf_op jit(solution)/shard_map/mul | solution.py:150
  (24 shorter events, 0.4 us)
Async XLA Ops:
  0.6 1.2 copy-start
  6.0 22.5 %all-to-all-start = ((f32[16,72,128]{2,1,0:T(8,128)}), f32[16,72,128]{2,1,0:T(8,128)S(1)}, u32[]{:S(2)}, u32[]{:S(2)}) async-start(f32[16,72,128]{2,1,0:T(8,128)} %pad_maximum_fusion), calls=%async_computation | async-start | bytes 1179648 | tf_op jit(solution)/shard_map/all_to_all | solution.py:31
  18.7 6.6 %copy-start.4 = (s32[1,1024]{1,0:T(1,128)S(1)}, s32[1,1024]{1,0:T(1,128)}, u32[]{:S(2)}) copy-start(s32[1,1024]{1,0:T(1,128)} %param.11) | copy-start | bytes 12292
  18.8 26.9 %collective-permute-start = (bf16[1024,256]{1,0:T(8,128)(2,1)S(1)}, bf16[1024,256]{1,0:T(8,128)(2,1)}, u32[]{:S(2)}, u32[]{:S(2)}) collective-permute-start(bf16[1024,256]{1,0:T(8,128)(2,1)S(1)} %pad_maximum_fusion.3), channel_id=1, source_target_pairs={{0,2},{2,4},{4,6},{6,0},{1,3},{3,5},{5,7},{7,1},{8,10},{10,12},{12... | collective-permute-start | bytes 1572872 | tf_op jit(solution)/shard_map/ppermute | solution.py:25
  22.1 23.5 %collective-permute-start.1 = (bf16[1024,256]{1,0:T(8,128)(2,1)S(1)}, bf16[1024,256]{1,0:T(8,128)(2,1)}, u32[]{:S(2)}, u32[]{:S(2)}) collective-permute-start(bf16[1024,256]{1,0:T(8,128)(2,1)S(1)} %pad_maximum_fusion.4), channel_id=1, source_target_pairs={{0,6},{2,0},{4,2},{6,4},{1,7},{3,1},{5,3},{7,5},{8,14},{10,8},{12,... | collective-permute-start | bytes 1572872 | tf_op jit(solution)/shard_map/ppermute | solution.py:25
  29.3 13.6 %all-to-all-start.1 = ((bf16[16,64,128]{2,1,0:T(8,128)(2,1)}), bf16[16,64,128]{2,1,0:T(8,128)(2,1)S(1)}, u32[]{:S(2)}, u32[]{:S(2)}) async-start(bf16[16,64,128]{2,1,0:T(8,128)(2,1)} %broadcast_in_dim.11), calls=%async_computation.1 | async-start | bytes 524288 | tf_op jit(solution)/shard_map/all_to_all | solution.py:31
  45.6 44.4 %all-to-all-start.2 = ((bf16[32,32,256]{2,1,0:T(8,128)(2,1)}), bf16[32,32,256]{2,1,0:T(8,128)(2,1)S(1)}, u32[]{:S(2)}, u32[]{:S(2)}) async-start(bf16[32,32,256]{2,1,0:T(8,128)(2,1)} %pad_maximum_fusion.2), calls=%async_computation.2 | async-start | bytes 1048576 | tf_op jit(solution)/shard_map/all_to_all | solution.py:31
  60.2 15.9 %collective-permute-start.2 = (bf16[1024,256]{1,0:T(8,128)(2,1)S(1)}, bf16[1024,256]{1,0:T(8,128)(2,1)S(1)}, u32[]{:S(2)}, u32[]{:S(2)}) collective-permute-start(bf16[1024,256]{1,0:T(8,128)(2,1)S(1)} %pad_maximum_fusion.5), channel_id=1, source_target_pairs={{0,4},{2,6},{4,0},{6,2},{1,5},{3,7},{5,1},{7,3},{8,12},{10,14},{12... | collective-permute-start | bytes 1572872 | tf_op jit(solution)/shard_map/ppermute | solution.py:25
  76.1 0.8 copy-start.5
  90.1 48.1 %copy-start.1 = (bf16[32,24,256]{2,1,0:T(8,128)(2,1)}, bf16[32,24,256]{2,1,0:T(8,128)(2,1)S(1)}, u32[]{:S(2)}) copy-start(bf16[32,24,256]{2,1,0:T(8,128)(2,1)S(1)} %slice.35) | copy-start | bytes 1179652
  91.4 15.9 %all-to-all-start.3 = ((f32[16,8,384]{2,1,0:T(8,128)}), f32[16,8,384]{2,1,0:T(8,128)S(1)}, u32[]{:S(2)}, u32[]{:S(2)}) async-start(f32[16,8,384]{2,1,0:T(8,128)} %bitcast.22), calls=%async_computation.3 | async-start | bytes 393216 | tf_op jit(solution)/shard_map/all_to_all | solution.py:31
  99.0 13.1 %collective-permute-start.4 = (bf16[768,256]{1,0:T(8,128)(2,1)S(1)}, bf16[768,256]{1,0:T(8,128)(2,1)S(1)}, u32[]{:S(2)}, u32[]{:S(2)}) collective-permute-start(bf16[768,256]{1,0:T(8,128)(2,1)S(1)} %bitcast.64), channel_id=1, source_target_pairs={{0,6},{2,0},{4,2},{6,4},{1,7},{3,1},{5,3},{7,5},{8,14},{10,8},{12,... | collective-permute-start | bytes 1179656 | tf_op jit(solution)/shard_map/ppermute | solution.py:25
  103.6 13.1 %collective-permute-start.3 = (bf16[768,256]{1,0:T(8,128)(2,1)S(1)}, bf16[768,256]{1,0:T(8,128)(2,1)S(1)}, u32[]{:S(2)}, u32[]{:S(2)}) collective-permute-start(bf16[768,256]{1,0:T(8,128)(2,1)S(1)} %bitcast.65), channel_id=1, source_target_pairs={{0,2},{2,4},{4,6},{6,0},{1,3},{3,5},{5,7},{7,1},{8,10},{10,12},{12... | collective-permute-start | bytes 1179656 | tf_op jit(solution)/shard_map/ppermute | solution.py:25
  112.1 26.2 %copy-start.2 = (bf16[768,256]{1,0:T(8,128)(2,1)}, bf16[768,256]{1,0:T(8,128)(2,1)S(1)}, u32[]{:S(2)}) copy-start(bf16[768,256]{1,0:T(8,128)(2,1)S(1)} %collective-permute-done.4.right) | copy-start | bytes 1179652
  116.7 21.6 %copy-start.3 = (bf16[768,256]{1,0:T(8,128)(2,1)}, bf16[768,256]{1,0:T(8,128)(2,1)S(1)}, u32[]{:S(2)}) copy-start(bf16[768,256]{1,0:T(8,128)(2,1)S(1)} %collective-permute-done.3.left) | copy-start | bytes 1179652
  117.4 20.9 %all-to-all-start.4 = ((bf16[32,8,384]{2,1,0:T(8,128)(2,1)}), bf16[32,8,384]{2,1,0:T(8,128)(2,1)S(1)}, u32[]{:S(2)}, u32[]{:S(2)}) async-start(bf16[32,8,384]{2,1,0:T(8,128)(2,1)} %broadcast_in_dim.14), calls=%async_computation.4 | async-start | bytes 393216 | tf_op jit(solution)/shard_map/all_to_all | solution.py:31
  121.3 6.8 %collective-permute-start.6 = (bf16[384,256]{1,0:T(8,128)(2,1)S(1)}, bf16[384,256]{1,0:T(8,128)(2,1)S(1)}, u32[]{:S(2)}, u32[]{:S(2)}) collective-permute-start(bf16[384,256]{1,0:T(8,128)(2,1)S(1)} %slice.38), channel_id=1, source_target_pairs={{0,6},{2,0},{4,2},{6,4},{1,7},{3,1},{5,3},{7,5},{8,14},{10,8},{12,... | collective-permute-start | bytes 589832 | tf_op jit(solution)/shard_map/ppermute | solution.py:25
  123.3 8.1 %collective-permute-start.5 = (bf16[384,256]{1,0:T(8,128)(2,1)S(1)}, bf16[384,256]{1,0:T(8,128)(2,1)}, u32[]{:S(2)}, u32[]{:S(2)}) collective-permute-start(bf16[384,256]{1,0:T(8,128)(2,1)S(1)} %slice.37), channel_id=1, source_target_pairs={{0,2},{2,4},{4,6},{6,0},{1,3},{3,5},{5,7},{7,1},{8,10},{10,12},{12... | collective-permute-start | bytes 589832 | tf_op jit(solution)/shard_map/ppermute | solution.py:25
  128.1 0.7 copy-start.6
  143.3 7.1 %collective-permute-start.7 = (bf16[768,512]{1,0:T(8,128)(2,1)}, bf16[768,512]{1,0:T(8,128)(2,1)S(1)}, u32[]{:S(2)}, u32[]{:S(2)}) collective-permute-start(bf16[768,512]{1,0:T(8,128)(2,1)} %get-tuple-element.26), channel_id=1, source_target_pairs={{0,1},{1,0},{2,3},{3,2},{4,5},{5,4},{6,7},{7,6},{8,9},{9,8},{10,11... | collective-permute-start | bytes 2359304 | tf_op jit(solution)/shard_map/ppermute | solution.py:21
  152.9 14.0 %collective-permute-start.8 = (bf16[768,256]{1,0:T(8,128)(2,1)}, bf16[768,256]{1,0:T(8,128)(2,1)}, u32[]{:S(2)}, u32[]{:S(2)}) collective-permute-start(bf16[768,256]{1,0:T(8,128)(2,1)} %slice.56), channel_id=1, source_target_pairs={{0,8},{8,0},{1,9},{9,1},{2,10},{10,2},{3,11},{11,3},{4,12},{12,4},... | collective-permute-start | bytes 1179656 | tf_op jit(solution)/shard_map/ppermute | solution.py:21

commit v7 on v6

--- a/solution.py
+++ b/solution.py
@@ -141,13 +141,13 @@
 
     across = [along_x(left[: height // 2], 1), along_x(right[height // 2 :], 3)]
 
-    *across, halves = lax.optimization_barrier((*across, halves))
     away, kept = partial([queries, left, *across, right], stored)
-    kept = kept + swap(away, "c").astype(F32)
+    away, halves = lax.optimization_barrier((away, halves))
+    away = swap(away, "c")
     quarter = kept.shape[1] // 2
-    beyond = swap(kept[:, :quarter].astype(BF16), "yh")
+    beyond = swap((kept[:, :quarter] + away[:, :quarter].astype(F32)).astype(BF16), "yh")
     doc_influence = lax.all_gather(halves, "c", axis=0).transpose(0, 2, 1).reshape(height, DOCS).astype(F32)
-    scores = (kept[:, quarter:] + beyond.astype(F32)) * 0.125
+    scores = (kept[:, quarter:] + away[:, quarter:].astype(F32) + beyond.astype(F32)) * 0.125
     return (scores, doc_influence)
 
 

time: 170 us -> 163 us (0.959)
  waiting for transfers between devices: 63.3 us -> 58.8 us
    ppermute x7, waiting for transfers between devices: 24.5 us -> 21.8 us  [along_x(): lax.ppermute(value, 'x', [(i, (i + distance) % 4) for i in range(4)])]
    convert_element_type x0 -> x1, other arithmetic: none -> 1.97 us  [per_device(): (kept[:, :quarter] + away[:, :quarter].astype(F32)).astype(BF16)]
    all_to_all x5, waiting for transfers between devices: 30.8 us -> 29 us  [exchange(): return lax.all_to_all(flat, axes, 0, 0, tiled=True).reshape(shape)]
  transfers between devices with their start and end apart: 14 -> 14, of which waited for: 12 -> 12; matrix products, arithmetic and copies ran while one was open for 7% -> 8% of each run, Pallas kernels for 0% -> 3%
where the time goes in v7:
time: 163 us; the launch traced here: 162 us
  starting transfers between devices  70.3 us (43%)
  waiting for transfers between devices  58.8 us (36%)
  other arithmetic  9.42 us (6%)
  local copies, waits for them, and re-layouts  8.65 us (5%)
  matrix products  6.57 us (4%)
  Pallas kernels  5.03 us (3%)
  blocking collectives  2.37 us (1%)
    all_to_all x5, starting transfers between devices, exchange(): return lax.all_to_all(flat, axes, 0, 0, tiled=True).reshape(shape)  38.8 us
    all_to_all x5, waiting for transfers between devices, exchange(): return lax.all_to_all(flat, axes, 0, 0, tiled=True).reshape(shape)  29 us
    ppermute x7, waiting for transfers between devices, along_x(): lax.ppermute(value, 'x', [(i, (i + distance) % 4) for i in range(4)])  21.8 us
    ppermute x7, starting transfers between devices, along_x(): lax.ppermute(value, 'x', [(i, (i + distance) % 4) for i in range(4)])  21.8 us
    ppermute x2, starting transfers between devices, swap(): return lax.ppermute(value, axis, [(0, 1), (1, 0)])  9.63 us
    ppermute x2, waiting for transfers between devices, swap(): return lax.ppermute(value, axis, [(0, 1), (1, 0)])  7.91 us
    pallas_call x1, Pallas kernels, partial(): pl.pallas_call(partial_kernel, grid=(steps,), out_shape=(jax.ShapeDtypeSt...  5.03 us
  transfers between devices with their start and end apart: 14, of which 12 were waited for; matrix products, arithmetic and copies ran while one was open for 8% of the time, Pallas kernels for 3%

profile of v7, /device:TPU:1, one launch (start us, length us, event | category | flops | bytes accessed | tf_op | source)
XLA Modules:
  0.0 162.0 jit_solution(9498924285866553090)
XLA Ops:
  0.6 0.0 copy-start
  0.6 0.0 copy-start.5
  0.7 1.2 copy-done
  1.9 1.3 fusion.10
  3.1 1.7 %fusion.11 = f32[1024,64]{0,1:T(8,128)S(1)} fusion(bf16[1024,512]{1,0:T(8,128)(2,1)} %param.8, bf16[512,64]{0,1:T(8,128)(2,1)} %param.10), kind=kOutput, calls=%fused_computation.50 | convolution fusion | flops 67108864 | bytes 1376256 | tf_op jit(solution)/shard_map/dot_general | solution.py:87
  4.8 0.2 copy.15
  5.0 0.0 copy-done.5
  5.1 0.9 pad_maximum_fusion
  6.0 10.3 %all-to-all-start = ((f32[16,72,128]{2,1,0:T(8,128)}), f32[16,72,128]{2,1,0:T(8,128)S(1)}, u32[]{:S(2)}, u32[]{:S(2)}) async-start(f32[16,72,128]{2,1,0:T(8,128)} %pad_maximum_fusion), calls=%async_computation | async-start | bytes 1179648 | tf_op jit(solution)/shard_map/all_to_all | solution.py:31
  16.2 2.5 %dynamic-slice_bitcast_fusion.3 = (bf16[256,256]{1,0:T(8,128)(2,1)S(1)}, bf16[256,256]{1,0:T(8,128)(2,1)S(1)}, bf16[256,256]{1,0:T(8,128)(2,1)S(1)}, bf16[256,25...) fusion(bf16[2,4,2,256,256]{4,3,2,1,0:T(8,128)(2,1)} %bitcast.69, ...), kind=kLoop, calls=%fused_computation.23 | loop fusion | bytes 4194336 | tf_op jit(solution)/shard_map/reshape | solution.py:120
  18.8 4.5 %collective-permute-start.1 = (bf16[1024,256]{1,0:T(8,128)(2,1)S(1)}, bf16[1024,256]{1,0:T(8,128)(2,1)}, u32[]{:S(2)}, u32[]{:S(2)}) collective-permute-start(bf16[1024,256]{1,0:T(8,128)(2,1)S(1)} %pad_maximum_fusion.4), channel_id=1, source_target_pairs={{0,6},{2,0},{4,2},{6,4},{1,7},{3,1},{5,3},{7,5},{8,14},{10,8},{12,... | collective-permute-start | bytes 1572872 | tf_op jit(solution)/shard_map/ppermute | solution.py:25
  23.4 1.9 %collective-permute-start = (bf16[1024,256]{1,0:T(8,128)(2,1)S(1)}, bf16[1024,256]{1,0:T(8,128)(2,1)}, u32[]{:S(2)}, u32[]{:S(2)}) collective-permute-start(bf16[1024,256]{1,0:T(8,128)(2,1)S(1)} %pad_maximum_fusion.3), channel_id=1, source_target_pairs={{0,2},{2,4},{4,6},{6,0},{1,3},{3,5},{5,7},{7,1},{8,10},{10,12},{12... | collective-permute-start | bytes 1572872 | tf_op jit(solution)/shard_map/ppermute | solution.py:25
  25.3 0.0 copy-done.4
  25.3 0.1 convert_reduce_fusion.1
  25.4 3.0 %all-to-all-done = f32[16,72,128]{2,1,0:T(8,128)S(1)} async-done(((f32[16,72,128]{2,1,0:T(8,128)}), f32[16,72,128]{2,1,0:T(8,128)S(1)}, u32[]{:S(2)}, u32[]{:S(2)}) %all-to-all-start) | async-done | bytes 589856 | tf_op jit(solution)/shard_map/all_to_all | solution.py:31
  28.5 0.8 broadcast_in_dim.11
  29.3 4.6 %all-to-all-start.1 = ((bf16[16,64,128]{2,1,0:T(8,128)(2,1)}), bf16[16,64,128]{2,1,0:T(8,128)(2,1)S(1)}, u32[]{:S(2)}, u32[]{:S(2)}) async-start(bf16[16,64,128]{2,1,0:T(8,128)(2,1)} %broadcast_in_dim.11), calls=%async_computation.1 | async-start | bytes 524288 | tf_op jit(solution)/shard_map/all_to_all | solution.py:31
  33.9 3.0 %fusion.3 = bf16[32,8,256]{2,1,0:T(8,128)(2,1)} fusion(bf16[4096,256]{1,0:T(8,128)(2,1)} %param.12, s32[4096]{0:T(1024)S(1)} %bitcast.75), kind=kOutput, calls=%fused_computation.4 | convolution fusion | flops 537985024 | bytes 2244608 | tf_op jit(solution)/shard_map/dot_general | solution.py:112
  36.8 8.2 %all-to-all-done.1 = bf16[16,64,128]{2,1,0:T(8,128)(2,1)S(1)} async-done(((bf16[16,64,128]{2,1,0:T(8,128)(2,1)}), bf16[16,64,128]{2,1,0:T(8,128)(2,1)S(1)}, u32[]{:S(2)}, u32[]{:S(2)}) %all-to-all-start.1) | async-done | bytes 262176 | tf_op jit(solution)/shard_map/all_to_all | solution.py:31
  45.0 0.1 slice.49
  45.2 0.1 constant_dynamic-slice_fusion
  45.3 0.1 copy.16
  45.4 0.1 broadcast_multiply_fusion
  45.6 0.1 mul.44
  45.6 0.2 fusion.4
  45.8 0.1 reshape.163
  45.9 0.1 divide_convert_fusion
  46.0 1.8 %pad_maximum_fusion.2 = bf16[32,32,256]{2,1,0:T(8,128)(2,1)} fusion(bf16[32,8,256]{2,1,0:T(8,128)(2,1)} %fusion.3, bf16[32,24,256]{2,1,0:T(8,128)(2,1)S(1)} %broadcast_in_dim.12), kind=kLoop, calls=%fused_computation.12 | loop fusion | flops 1048576 | bytes 1048576 | tf_op jit(solution)/shard_map/concatenate | solution.py:114
  47.8 0.0 collective-permute-done.1.refs_3_
  47.8 0.0 collective-permute-done.refs_1_
  47.8 13.4 %all-to-all-start.2 = ((bf16[32,32,256]{2,1,0:T(8,128)(2,1)}), bf16[32,32,256]{2,1,0:T(8,128)(2,1)S(1)}, u32[]{:S(2)}, u32[]{:S(2)}) async-start(bf16[32,32,256]{2,1,0:T(8,128)(2,1)} %pad_maximum_fusion.2), calls=%async_computation.2 | async-start | bytes 1048576 | tf_op jit(solution)/shard_map/all_to_all | solution.py:31
  61.2 1.1 pad_maximum_fusion.5
  62.4 2.4 %collective-permute-start.2 = (bf16[1024,256]{1,0:T(8,128)(2,1)S(1)}, bf16[1024,256]{1,0:T(8,128)(2,1)S(1)}, u32[]{:S(2)}, u32[]{:S(2)}) collective-permute-start(bf16[1024,256]{1,0:T(8,128)(2,1)S(1)} %pad_maximum_fusion.5), channel_id=1, source_target_pairs={{0,4},{2,6},{4,0},{6,2},{1,5},{3,7},{5,1},{7,3},{8,12},{10,14},{12... | collective-permute-start | bytes 1572872 | tf_op jit(solution)/shard_map/ppermute | solution.py:25
  64.8 13.1 %collective-permute-done.2.refs_2_ = bf16[1024,256]{1,0:T(8,128)(2,1)S(1)} collective-permute-done((bf16[1024,256]{1,0:T(8,128)(2,1)S(1)}, bf16[1024,256]{1,0:T(8,128)(2,1)S(1)}, u32[]{:S(2)}, u32[]{:S(2)}) %collective-permute-start.2) | collective-permute-done | bytes 524320 | tf_op jit(solution)/shard_map/ppermute | solution.py:25
  77.9 14.0 %all-to-all-done.2 = bf16[32,32,256]{2,1,0:T(8,128)(2,1)S(1)} async-done(((bf16[32,32,256]{2,1,0:T(8,128)(2,1)}), bf16[32,32,256]{2,1,0:T(8,128)(2,1)S(1)}, u32[]{:S(2)}, u32[]{:S(2)}) %all-to-all-start.2) | async-done | bytes 524320 | tf_op jit(solution)/shard_map/all_to_all | solution.py:31
  91.9 0.2 fusion.9
  92.2 0.3 convolution_add_fusion
  92.4 0.7 broadcast_in_dim.13
  93.1 6.7 %all-to-all-start.3 = ((f32[16,8,384]{2,1,0:T(8,128)}), f32[16,8,384]{2,1,0:T(8,128)S(1)}, u32[]{:S(2)}, u32[]{:S(2)}) async-start(f32[16,8,384]{2,1,0:T(8,128)} %bitcast.22), calls=%async_computation.3 | async-start | bytes 393216 | tf_op jit(solution)/shard_map/all_to_all | solution.py:31
  99.8 3.3 %collective-permute-start.3 = (bf16[768,256]{1,0:T(8,128)(2,1)S(1)}, bf16[768,256]{1,0:T(8,128)(2,1)S(1)}, u32[]{:S(2)}, u32[]{:S(2)}) collective-permute-start(bf16[768,256]{1,0:T(8,128)(2,1)S(1)} %bitcast.64), channel_id=1, source_target_pairs={{0,2},{2,4},{4,6},{6,0},{1,3},{3,5},{5,7},{7,1},{8,10},{10,12},{12... | collective-permute-start | bytes 1179656 | tf_op jit(solution)/shard_map/ppermute | solution.py:25
  103.1 3.2 %collective-permute-start.4 = (bf16[768,256]{1,0:T(8,128)(2,1)S(1)}, bf16[768,256]{1,0:T(8,128)(2,1)S(1)}, u32[]{:S(2)}, u32[]{:S(2)}) collective-permute-start(bf16[768,256]{1,0:T(8,128)(2,1)S(1)} %bitcast.65), channel_id=1, source_target_pairs={{0,6},{2,0},{4,2},{6,4},{1,7},{3,1},{5,3},{7,5},{8,14},{10,8},{12,... | collective-permute-start | bytes 1179656 | tf_op jit(solution)/shard_map/ppermute | solution.py:25
  106.3 1.7 %all-to-all-done.3 = f32[16,8,384]{2,1,0:T(8,128)S(1)} async-done(((f32[16,8,384]{2,1,0:T(8,128)}), f32[16,8,384]{2,1,0:T(8,128)S(1)}, u32[]{:S(2)}, u32[]{:S(2)}) %all-to-all-start.3) | async-done | bytes 196640 | tf_op jit(solution)/shard_map/all_to_all | solution.py:31
  108.1 6.0 %collective-permute-done.3.left = bf16[768,256]{1,0:T(8,128)(2,1)S(1)} collective-permute-done((bf16[768,256]{1,0:T(8,128)(2,1)S(1)}, bf16[768,256]{1,0:T(8,128)(2,1)S(1)}, u32[]{:S(2)}, u32[]{:S(2)}) %collective-permute-start.3) | collective-permute-done | bytes 393248 | tf_op jit(solution)/shard_map/ppermute | solution.py:25
  114.1 0.9 collective-permute-done.4.right
  115.0 0.8 broadcast_in_dim.14
  115.8 3.9 %all-to-all-start.4 = ((bf16[32,8,384]{2,1,0:T(8,128)(2,1)}), bf16[32,8,384]{2,1,0:T(8,128)(2,1)S(1)}, u32[]{:S(2)}, u32[]{:S(2)}) async-start(bf16[32,8,384]{2,1,0:T(8,128)(2,1)} %broadcast_in_dim.14), calls=%async_computation.4 | async-start | bytes 393216 | tf_op jit(solution)/shard_map/all_to_all | solution.py:31
  119.7 3.1 %collective-permute-start.5 = (bf16[384,256]{1,0:T(8,128)(2,1)S(1)}, bf16[384,256]{1,0:T(8,128)(2,1)S(1)}, u32[]{:S(2)}, u32[]{:S(2)}) collective-permute-start(bf16[384,256]{1,0:T(8,128)(2,1)S(1)} %slice.42), channel_id=1, source_target_pairs={{0,2},{2,4},{4,6},{6,0},{1,3},{3,5},{5,7},{7,1},{8,10},{10,12},{12... | collective-permute-start | bytes 589832 | tf_op jit(solution)/shard_map/ppermute | solution.py:25
  122.8 3.4 %collective-permute-start.6 = (bf16[384,256]{1,0:T(8,128)(2,1)S(1)}, bf16[384,256]{1,0:T(8,128)(2,1)}, u32[]{:S(2)}, u32[]{:S(2)}) collective-permute-start(bf16[384,256]{1,0:T(8,128)(2,1)S(1)} %slice.43), channel_id=1, source_target_pairs={{0,6},{2,0},{4,2},{6,4},{1,7},{3,1},{5,3},{7,5},{8,14},{10,8},{12,... | collective-permute-start | bytes 589832 | tf_op jit(solution)/shard_map/ppermute | solution.py:25
  126.2 0.8 pad_maximum_fusion.6.refs_0_
  127.0 0.0 copy-done.6
  127.0 0.6 collective-permute-done.5.upper
  127.7 0.7 copy-done.7
  128.3 1.2 collective-permute-done.6.lower
  129.5 5.0 %shard_map.86 = (bf16[768,512]{1,0:T(8,128)(2,1)}, f32[768,512]{1,0:T(8,128)}) custom-call(bf16[768,256]{1,0:T(8,128)(2,1)} %bitcast.66, bf16[768,256]{1,0:T(8,128)(2,1)} %copy-done.2, bf16[384,256]{1,0:T(8,128)(2,1)} %copy-done.7, bf16[384,256]{1,0:T(8,128)(2,1)} %collective-permute-done.6.lower, bf16[768,256]{1,0:T(8,128)(2,1)} %copy-done.3, ...), custom_call_target="tpu_custom_call" | custom-call | flops 1610612736 | bytes 6291456 | tf_op jit(solution)/shard_map/pallas_call | solution.py:67
  134.6 2.1 %all-to-all-done.4 = bf16[32,8,384]{2,1,0:T(8,128)(2,1)S(1)} async-done(((bf16[32,8,384]{2,1,0:T(8,128)(2,1)}), bf16[32,8,384]{2,1,0:T(8,128)(2,1)S(1)}, u32[]{:S(2)}, u32[]{:S(2)}) %all-to-all-start.4) | async-done | bytes 196640 | tf_op jit(solution)/shard_map/all_to_all | solution.py:31
  136.6 5.0 %collective-permute-start.7 = (bf16[768,512]{1,0:T(8,128)(2,1)}, bf16[768,512]{1,0:T(8,128)(2,1)S(1)}, u32[]{:S(2)}, u32[]{:S(2)}) collective-permute-start(bf16[768,512]{1,0:T(8,128)(2,1)} %get-tuple-element.24), channel_id=1, source_target_pairs={{0,1},{1,0},{2,3},{3,2},{4,5},{5,4},{6,7},{7,6},{8,9},{9,8},{10,11... | collective-permute-start | bytes 2359304 | tf_op jit(solution)/shard_map/ppermute | solution.py:21
  141.6 2.1 %collective-permute-done.7 = bf16[768,512]{1,0:T(8,128)(2,1)S(1)} collective-permute-done((bf16[768,512]{1,0:T(8,128)(2,1)}, bf16[768,512]{1,0:T(8,128)(2,1)S(1)}, u32[]{:S(2)}, u32[]{:S(2)}) %collective-permute-start.7) | collective-permute-done | bytes 786464 | tf_op jit(solution)/shard_map/ppermute | solution.py:21
  143.7 2.0 %add_convert_fusion = bf16[768,256]{1,0:T(8,128)(2,1)} fusion(f32[768,512]{1,0:T(8,128)} %get-tuple-element.21, bf16[768,512]{1,0:T(8,128)(2,1)S(1)} %collective-permute-done.7), kind=kLoop, calls=%fused_computation.8 | loop fusion | flops 589824 | bytes 1572864 | tf_op jit(solution)/shard_map/convert_element_type | solution.py:148
  145.7 4.6 %collective-permute-start.8 = (bf16[768,256]{1,0:T(8,128)(2,1)}, bf16[768,256]{1,0:T(8,128)(2,1)}, u32[]{:S(2)}, u32[]{:S(2)}) collective-permute-start(bf16[768,256]{1,0:T(8,128)(2,1)} %add_convert_fusion), channel_id=1, source_target_pairs={{0,8},{8,0},{1,9},{9,1},{2,10},{10,2},{3,11},{11,3},{4,12},{12,4},... | collective-permute-start | bytes 1179656 | tf_op jit(solution)/shard_map/ppermute | solution.py:21
  150.4 2.4 %all-gather = bf16[512,384]{1,0:T(8,128)(2,1)S(1)} all-gather(bf16[256,384]{1,0:T(8,128)(2,1)S(1)} %bitcast.73), channel_id=2, replica_groups=mesh['z'=16,'yl'=2,'yh'=2,'x'=4,'c'=2] {'c'}, dimensions={0}, use_global_device_ids=true | all-gather | bytes 589824 | tf_op jit(solution)/shard_map/all_gather | solution.py:149
  152.7 0.1 convert_bitcast_fusion
  152.8 1.1 copy.18
  153.9 5.8 %collective-permute-done.8 = bf16[768,256]{1,0:T(8,128)(2,1)} collective-permute-done((bf16[768,256]{1,0:T(8,128)(2,1)}, bf16[768,256]{1,0:T(8,128)(2,1)}, u32[]{:S(2)}, u32[]{:S(2)}) %collective-permute-start.8) | collective-permute-done | bytes 393248 | tf_op jit(solution)/shard_map/ppermute | solution.py:21
  159.7 2.3 %add_multiply_fusion = f32[768,256]{1,0:T(8,128)} fusion(bf16[768,256]{1,0:T(8,128)(2,1)} %collective-permute-done.8, f32[768,512]{1,0:T(8,128)} %get-tuple-element.21, bf16[768,512]{1,0:T(8,128)(2,1)S(1)} %collective-permute-done.7), kind=kLoop, calls=%fused_computation.7 | loop fusion | flops 983040 | bytes 2359296 | tf_op jit(solution)/shard_map/mul | solution.py:150
  (25 shorter events, 0.4 us)
Async XLA Ops:
  0.6 1.2 copy-start
  0.6 4.4 %copy-start.5 = (s32[256]{0:T(256)S(1)}, s32[256]{0:T(256)}, u32[]{:S(2)}) copy-start(s32[256]{0:T(256)} %param.13) | copy-start | bytes 3076
  6.0 22.5 %all-to-all-start = ((f32[16,72,128]{2,1,0:T(8,128)}), f32[16,72,128]{2,1,0:T(8,128)S(1)}, u32[]{:S(2)}, u32[]{:S(2)}) async-start(f32[16,72,128]{2,1,0:T(8,128)} %pad_maximum_fusion), calls=%async_computation | async-start | bytes 1179648 | tf_op jit(solution)/shard_map/all_to_all | solution.py:31
  18.7 6.6 %copy-start.4 = (s32[1,1024]{1,0:T(1,128)S(1)}, s32[1,1024]{1,0:T(1,128)}, u32[]{:S(2)}) copy-start(s32[1,1024]{1,0:T(1,128)} %param.11) | copy-start | bytes 12292
  18.8 29.0 %collective-permute-start.1 = (bf16[1024,256]{1,0:T(8,128)(2,1)S(1)}, bf16[1024,256]{1,0:T(8,128)(2,1)}, u32[]{:S(2)}, u32[]{:S(2)}) collective-permute-start(bf16[1024,256]{1,0:T(8,128)(2,1)S(1)} %pad_maximum_fusion.4), channel_id=1, source_target_pairs={{0,6},{2,0},{4,2},{6,4},{1,7},{3,1},{5,3},{7,5},{8,14},{10,8},{12,... | collective-permute-start | bytes 1572872 | tf_op jit(solution)/shard_map/ppermute | solution.py:25
  23.4 24.4 %collective-permute-start = (bf16[1024,256]{1,0:T(8,128)(2,1)S(1)}, bf16[1024,256]{1,0:T(8,128)(2,1)}, u32[]{:S(2)}, u32[]{:S(2)}) collective-permute-start(bf16[1024,256]{1,0:T(8,128)(2,1)S(1)} %pad_maximum_fusion.3), channel_id=1, source_target_pairs={{0,2},{2,4},{4,6},{6,0},{1,3},{3,5},{5,7},{7,1},{8,10},{10,12},{12... | collective-permute-start | bytes 1572872 | tf_op jit(solution)/shard_map/ppermute | solution.py:25
  29.3 15.8 %all-to-all-start.1 = ((bf16[16,64,128]{2,1,0:T(8,128)(2,1)}), bf16[16,64,128]{2,1,0:T(8,128)(2,1)S(1)}, u32[]{:S(2)}, u32[]{:S(2)}) async-start(bf16[16,64,128]{2,1,0:T(8,128)(2,1)} %broadcast_in_dim.11), calls=%async_computation.1 | async-start | bytes 524288 | tf_op jit(solution)/shard_map/all_to_all | solution.py:31
  47.8 44.1 %all-to-all-start.2 = ((bf16[32,32,256]{2,1,0:T(8,128)(2,1)}), bf16[32,32,256]{2,1,0:T(8,128)(2,1)S(1)}, u32[]{:S(2)}, u32[]{:S(2)}) async-start(bf16[32,32,256]{2,1,0:T(8,128)(2,1)} %pad_maximum_fusion.2), calls=%async_computation.2 | async-start | bytes 1048576 | tf_op jit(solution)/shard_map/all_to_all | solution.py:31
  62.4 15.5 %collective-permute-start.2 = (bf16[1024,256]{1,0:T(8,128)(2,1)S(1)}, bf16[1024,256]{1,0:T(8,128)(2,1)S(1)}, u32[]{:S(2)}, u32[]{:S(2)}) collective-permute-start(bf16[1024,256]{1,0:T(8,128)(2,1)S(1)} %pad_maximum_fusion.5), channel_id=1, source_target_pairs={{0,4},{2,6},{4,0},{6,2},{1,5},{3,7},{5,1},{7,3},{8,12},{10,14},{12... | collective-permute-start | bytes 1572872 | tf_op jit(solution)/shard_map/ppermute | solution.py:25
  77.9 49.2 %copy-start.6 = (bf16[1024,256]{1,0:T(8,128)(2,1)}, bf16[1024,256]{1,0:T(8,128)(2,1)S(1)}, u32[]{:S(2)}) copy-start(bf16[1024,256]{1,0:T(8,128)(2,1)S(1)} %collective-permute-done.2.refs_2_) | copy-start | bytes 1572868
  91.9 35.1 %copy-start.1 = (bf16[32,24,256]{2,1,0:T(8,128)(2,1)}, bf16[32,24,256]{2,1,0:T(8,128)(2,1)S(1)}, u32[]{:S(2)}) copy-start(bf16[32,24,256]{2,1,0:T(8,128)(2,1)S(1)} %slice.40) | copy-start | bytes 1179652
  93.1 14.9 %all-to-all-start.3 = ((f32[16,8,384]{2,1,0:T(8,128)}), f32[16,8,384]{2,1,0:T(8,128)S(1)}, u32[]{:S(2)}, u32[]{:S(2)}) async-start(f32[16,8,384]{2,1,0:T(8,128)} %bitcast.22), calls=%async_computation.3 | async-start | bytes 393216 | tf_op jit(solution)/shard_map/all_to_all | solution.py:31
  99.8 14.3 %collective-permute-start.3 = (bf16[768,256]{1,0:T(8,128)(2,1)S(1)}, bf16[768,256]{1,0:T(8,128)(2,1)S(1)}, u32[]{:S(2)}, u32[]{:S(2)}) collective-permute-start(bf16[768,256]{1,0:T(8,128)(2,1)S(1)} %bitcast.64), channel_id=1, source_target_pairs={{0,2},{2,4},{4,6},{6,0},{1,3},{3,5},{5,7},{7,1},{8,10},{10,12},{12... | collective-permute-start | bytes 1179656 | tf_op jit(solution)/shard_map/ppermute | solution.py:25
  103.1 11.9 %collective-permute-start.4 = (bf16[768,256]{1,0:T(8,128)(2,1)S(1)}, bf16[768,256]{1,0:T(8,128)(2,1)S(1)}, u32[]{:S(2)}, u32[]{:S(2)}) collective-permute-start(bf16[768,256]{1,0:T(8,128)(2,1)S(1)} %bitcast.65), channel_id=1, source_target_pairs={{0,6},{2,0},{4,2},{6,4},{1,7},{3,1},{5,3},{7,5},{8,14},{10,8},{12,... | collective-permute-start | bytes 1179656 | tf_op jit(solution)/shard_map/ppermute | solution.py:25
  114.1 15.4 %copy-start.2 = (bf16[768,256]{1,0:T(8,128)(2,1)}, bf16[768,256]{1,0:T(8,128)(2,1)S(1)}, u32[]{:S(2)}) copy-start(bf16[768,256]{1,0:T(8,128)(2,1)S(1)} %collective-permute-done.3.left) | copy-start | bytes 1179652
  115.0 14.5 %copy-start.3 = (bf16[768,256]{1,0:T(8,128)(2,1)}, bf16[768,256]{1,0:T(8,128)(2,1)S(1)}, u32[]{:S(2)}) copy-start(bf16[768,256]{1,0:T(8,128)(2,1)S(1)} %collective-permute-done.4.right) | copy-start | bytes 1179652
  115.8 20.9 %all-to-all-start.4 = ((bf16[32,8,384]{2,1,0:T(8,128)(2,1)}), bf16[32,8,384]{2,1,0:T(8,128)(2,1)S(1)}, u32[]{:S(2)}, u32[]{:S(2)}) async-start(bf16[32,8,384]{2,1,0:T(8,128)(2,1)} %broadcast_in_dim.14), calls=%async_computation.4 | async-start | bytes 393216 | tf_op jit(solution)/shard_map/all_to_all | solution.py:31
  119.7 8.0 %collective-permute-start.5 = (bf16[384,256]{1,0:T(8,128)(2,1)S(1)}, bf16[384,256]{1,0:T(8,128)(2,1)S(1)}, u32[]{:S(2)}, u32[]{:S(2)}) collective-permute-start(bf16[384,256]{1,0:T(8,128)(2,1)S(1)} %slice.42), channel_id=1, source_target_pairs={{0,2},{2,4},{4,6},{6,0},{1,3},{3,5},{5,7},{7,1},{8,10},{10,12},{12... | collective-permute-start | bytes 589832 | tf_op jit(solution)/shard_map/ppermute | solution.py:25
  122.8 6.7 %collective-permute-start.6 = (bf16[384,256]{1,0:T(8,128)(2,1)S(1)}, bf16[384,256]{1,0:T(8,128)(2,1)}, u32[]{:S(2)}, u32[]{:S(2)}) collective-permute-start(bf16[384,256]{1,0:T(8,128)(2,1)S(1)} %slice.43), channel_id=1, source_target_pairs={{0,6},{2,0},{4,2},{6,4},{1,7},{3,1},{5,3},{7,5},{8,14},{10,8},{12,... | collective-permute-start | bytes 589832 | tf_op jit(solution)/shard_map/ppermute | solution.py:25
  127.7 0.7 copy-start.7
  136.6 7.1 %collective-permute-start.7 = (bf16[768,512]{1,0:T(8,128)(2,1)}, bf16[768,512]{1,0:T(8,128)(2,1)S(1)}, u32[]{:S(2)}, u32[]{:S(2)}) collective-permute-start(bf16[768,512]{1,0:T(8,128)(2,1)} %get-tuple-element.24), channel_id=1, source_target_pairs={{0,1},{1,0},{2,3},{3,2},{4,5},{5,4},{6,7},{7,6},{8,9},{9,8},{10,11... | collective-permute-start | bytes 2359304 | tf_op jit(solution)/shard_map/ppermute | solution.py:21
  145.7 14.0 %collective-permute-start.8 = (bf16[768,256]{1,0:T(8,128)(2,1)}, bf16[768,256]{1,0:T(8,128)(2,1)}, u32[]{:S(2)}, u32[]{:S(2)}) collective-permute-start(bf16[768,256]{1,0:T(8,128)(2,1)} %add_convert_fusion), channel_id=1, source_target_pairs={{0,8},{8,0},{1,9},{9,1},{2,10},{10,2},{3,11},{11,3},{4,12},{12,4},... | collective-permute-start | bytes 1179656 | tf_op jit(solution)/shard_map/ppermute | solution.py:21

commit v8 on v7

--- a/solution.py
+++ b/solution.py
@@ -122,9 +122,9 @@
         return jnp.concatenate([block(1 - yh, 1 - c), block(yh, 1 - c), block(1 - yh, c), block(yh, c)])
 
     stored = [along_x(rows_for((x + d) % 4), d) for d in range(4)]
-    second, stored[1], stored[3] = lax.optimization_barrier((second, stored[1], stored[3]))
+    second, stored[1] = lax.optimization_barrier((second, stored[1]))
     second = exchange(second, DP)
-    second, stored[2] = lax.optimization_barrier((second, stored[2]))
+    second, stored[2], stored[3] = lax.optimization_barrier((second, stored[2], stored[3]))
     queries = second[:, :EX_DEV].reshape(32 * EX_DEV, width)
     height = queries.shape[0]
 
@@ -132,12 +132,13 @@
 
     high, low = split(jnp.sum(second[:, EX_DEV:].astype(F32), axis=0))
     doc_part = dot_t(high, queries) + dot_t(low, queries)
-    halves = doc_part.reshape(own_docs, 2, height // 2).transpose(1, 0, 2)
-    halves = jnp.broadcast_to(halves[None], (8, *halves.shape)).reshape(16, own_docs, height // 2)
+    share = height // 8
+    halves = jnp.pad(doc_part.reshape(own_docs, 8, share), ((0, 0), (0, 0), (0, 128 - share))).transpose(1, 0, 2)
+    halves = jnp.broadcast_to(halves[None], (2, *halves.shape)).reshape(16, own_docs, 128)
     halves = jnp.sum(exchange(halves, TENSOR), axis=0)
     halves = (halves * (0.125 / math.sqrt(logs * 32 / DOCS))).astype(BF16)
     halves, left, right = lax.optimization_barrier((halves, left, right))
-    halves = exchange(to_all(halves, 32), DP).reshape(DOCS, height // 2)
+    halves = exchange(to_all(halves, 32), DP).reshape(DOCS, 128)[:, :share].T
 
     across = [along_x(left[: height // 2], 1), along_x(right[height // 2 :], 3)]
 
@@ -146,7 +147,7 @@
     away = swap(away, "c")
     quarter = kept.shape[1] // 2
     beyond = swap((kept[:, :quarter] + away[:, :quarter].astype(F32)).astype(BF16), "yh")
-    doc_influence = lax.all_gather(halves, "c", axis=0).transpose(0, 2, 1).reshape(height, DOCS).astype(F32)
+    doc_influence = exchange(to_all(halves, 8), ("x", "c")).reshape(height, DOCS).astype(F32)
     scores = (kept[:, quarter:] + away[:, quarter:].astype(F32) + beyond.astype(F32)) * 0.125
     return (scores, doc_influence)
 

time: 163 us -> 168 us (1.031)
  blocking collectives: 2.37 us -> 13.5 us
  waiting for transfers between devices: 58.8 us -> 50.5 us
  local copies, waits for them, and re-layouts: 8.65 us -> 10.8 us
    all_to_all x0 -> x1, blocking collectives: none -> 13.5 us  [exchange(): return lax.all_to_all(flat, axes, 0, 0, tiled=True).reshape(shape)]
    ppermute x7, waiting for transfers between devices: 21.8 us -> 12.8 us  [along_x(): lax.ppermute(value, 'x', [(i, (i + distance) % 4) for i in range(4)])]
    all_gather x1 -> x0, blocking collectives: 2.37 us -> none  [per_device(): lax.all_gather(halves, 'c', axis=0).transpose(0, 2, 1).reshape(height, DOCS)]
    ppermute x2, starting transfers between devices: 9.63 us -> 7.37 us  [swap(): return lax.ppermute(value, axis, [(0, 1), (1, 0)])]
    unnamed x16 -> x22, local copies, waits for them, and re-layouts: 1.91 us -> 4.13 us
  transfers between devices with their start and end apart: 14 -> 14, of which waited for: 12 -> 8; matrix products, arithmetic and copies ran while one was open for 8% -> 10% of each run, Pallas kernels for 3% -> 3%
where the time goes in v8:
time: 168 us; the launch traced here: 167 us
  starting transfers between devices  69.7 us (41%)
  waiting for transfers between devices  50.5 us (30%)
  blocking collectives  13.5 us (8%)
  local copies, waits for them, and re-layouts  10.8 us (6%)
  other arithmetic  10.1 us (6%)
  matrix products  6.57 us (4%)
  Pallas kernels  5.01 us (3%)
    all_to_all x5, starting transfers between devices, exchange(): return lax.all_to_all(flat, axes, 0, 0, tiled=True).reshape(shape)  39.9 us
    all_to_all x5, waiting for transfers between devices, exchange(): return lax.all_to_all(flat, axes, 0, 0, tiled=True).reshape(shape)  30.4 us
    ppermute x7, starting transfers between devices, along_x(): lax.ppermute(value, 'x', [(i, (i + distance) % 4) for i in range(4)])  22.5 us
    all_to_all x1, blocking collectives, exchange(): return lax.all_to_all(flat, axes, 0, 0, tiled=True).reshape(shape)  13.5 us
    ppermute x7, waiting for transfers between devices, along_x(): lax.ppermute(value, 'x', [(i, (i + distance) % 4) for i in range(4)])  12.8 us
    ppermute x2, starting transfers between devices, swap(): return lax.ppermute(value, axis, [(0, 1), (1, 0)])  7.37 us
    ppermute x2, waiting for transfers between devices, swap(): return lax.ppermute(value, axis, [(0, 1), (1, 0)])  7.34 us
    pallas_call x1, Pallas kernels, partial(): pl.pallas_call(partial_kernel, grid=(steps,), out_shape=(jax.ShapeDtypeSt...  5.01 us
  transfers between devices with their start and end apart: 14, of which 8 were waited for; matrix products, arithmetic and copies ran while one was open for 10% of the time, Pallas kernels for 3%

profile of v8, /device:TPU:1, one launch (start us, length us, event | category | flops | bytes accessed | tf_op | source)
XLA Modules:
  0.0 167.3 jit_solution(15947980932676510709)
XLA Ops:
  0.6 0.0 copy-start
  0.7 1.2 copy-done
  1.9 1.3 fusion.10
  3.1 1.7 fusion.11
  4.9 0.2 copy.19
  5.1 0.9 pad_maximum_fusion
  6.0 10.3 %all-to-all-start = ((f32[16,72,128]{2,1,0:T(8,128)}), f32[16,72,128]{2,1,0:T(8,128)S(1)}, u32[]{:S(2)}, u32[]{:S(2)}) async-start(f32[16,72,128]{2,1,0:T(8,128)} %pad_maximum_fusion), calls=%async_computation | async-start | bytes 1179648 | tf_op jit(solution)/shard_map/all_to_all | solution.py:31
  16.2 2.5 %dynamic-slice_bitcast_fusion.3 = (bf16[256,256]{1,0:T(8,128)(2,1)S(1)}, bf16[256,256]{1,0:T(8,128)(2,1)S(1)}, bf16[256,256]{1,0:T(8,128)(2,1)S(1)}, bf16[256,25...) fusion(bf16[2,4,2,256,256]{4,3,2,1,0:T(8,128)(2,1)} %bitcast.68, ...), kind=kLoop, calls=%fused_computation.23 | loop fusion | bytes 4194336 | tf_op jit(solution)/shard_map/reshape | solution.py:120
  18.8 3.3 %collective-permute-start = (bf16[1024,256]{1,0:T(8,128)(2,1)S(1)}, bf16[1024,256]{1,0:T(8,128)(2,1)}, u32[]{:S(2)}, u32[]{:S(2)}) collective-permute-start(bf16[1024,256]{1,0:T(8,128)(2,1)S(1)} %pad_maximum_fusion.3), channel_id=1, source_target_pairs={{0,2},{2,4},{4,6},{6,0},{1,3},{3,5},{5,7},{7,1},{8,10},{10,12},{12... | collective-permute-start | bytes 1572872 | tf_op jit(solution)/shard_map/ppermute | solution.py:25
  22.1 0.1 convert_reduce_fusion.1
  22.3 6.2 %all-to-all-done = f32[16,72,128]{2,1,0:T(8,128)S(1)} async-done(((f32[16,72,128]{2,1,0:T(8,128)}), f32[16,72,128]{2,1,0:T(8,128)S(1)}, u32[]{:S(2)}, u32[]{:S(2)}) %all-to-all-start) | async-done | bytes 589856 | tf_op jit(solution)/shard_map/all_to_all | solution.py:31
  28.5 0.8 broadcast_in_dim.13
  29.3 4.6 %all-to-all-start.1 = ((bf16[16,64,128]{2,1,0:T(8,128)(2,1)}), bf16[16,64,128]{2,1,0:T(8,128)(2,1)S(1)}, u32[]{:S(2)}, u32[]{:S(2)}) async-start(bf16[16,64,128]{2,1,0:T(8,128)(2,1)} %broadcast_in_dim.13), calls=%async_computation.1 | async-start | bytes 524288 | tf_op jit(solution)/shard_map/all_to_all | solution.py:31
  33.9 3.0 %fusion.3 = bf16[32,8,256]{2,1,0:T(8,128)(2,1)} fusion(bf16[4096,256]{1,0:T(8,128)(2,1)} %param.12, s32[4096]{0:T(1024)S(1)} %bitcast.72), kind=kOutput, calls=%fused_computation.4 | convolution fusion | flops 537985024 | bytes 2244608 | tf_op jit(solution)/shard_map/dot_general | solution.py:112
  36.9 5.8 %all-to-all-done.1 = bf16[16,64,128]{2,1,0:T(8,128)(2,1)S(1)} async-done(((bf16[16,64,128]{2,1,0:T(8,128)(2,1)}), bf16[16,64,128]{2,1,0:T(8,128)(2,1)S(1)}, u32[]{:S(2)}, u32[]{:S(2)}) %all-to-all-start.1) | async-done | bytes 262176 | tf_op jit(solution)/shard_map/all_to_all | solution.py:31
  42.6 0.1 slice.53
  42.8 0.1 constant_dynamic-slice_fusion
  42.9 0.1 copy.20
  43.1 0.1 broadcast_multiply_fusion
  43.2 0.1 mul.44
  43.2 0.2 fusion.4
  43.4 0.1 reshape.167
  43.5 0.1 divide_convert_fusion
  43.6 1.8 %pad_maximum_fusion.2 = bf16[32,32,256]{2,1,0:T(8,128)(2,1)} fusion(bf16[32,8,256]{2,1,0:T(8,128)(2,1)} %fusion.3, bf16[32,24,256]{2,1,0:T(8,128)(2,1)S(1)} %broadcast_in_dim.14), kind=kLoop, calls=%fused_computation.11 | loop fusion | flops 1048576 | bytes 1048576 | tf_op jit(solution)/shard_map/concatenate | solution.py:114
  45.4 0.0 collective-permute-done.refs_1_
  45.4 13.4 %all-to-all-start.2 = ((bf16[32,32,256]{2,1,0:T(8,128)(2,1)}), bf16[32,32,256]{2,1,0:T(8,128)(2,1)S(1)}, u32[]{:S(2)}, u32[]{:S(2)}) async-start(bf16[32,32,256]{2,1,0:T(8,128)(2,1)} %pad_maximum_fusion.2), calls=%async_computation.2 | async-start | bytes 1048576 | tf_op jit(solution)/shard_map/all_to_all | solution.py:31
  58.9 1.1 pad_maximum_fusion.5
  59.9 3.2 %collective-permute-start.2 = (bf16[1024,256]{1,0:T(8,128)(2,1)S(1)}, bf16[1024,256]{1,0:T(8,128)(2,1)S(1)}, u32[]{:S(2)}, u32[]{:S(2)}) collective-permute-start(bf16[1024,256]{1,0:T(8,128)(2,1)S(1)} %pad_maximum_fusion.5), channel_id=1, source_target_pairs={{0,6},{2,0},{4,2},{6,4},{1,7},{3,1},{5,3},{7,5},{8,14},{10,8},{12,... | collective-permute-start | bytes 1572872 | tf_op jit(solution)/shard_map/ppermute | solution.py:25
  63.2 2.7 %collective-permute-start.1 = (bf16[1024,256]{1,0:T(8,128)(2,1)S(1)}, bf16[1024,256]{1,0:T(8,128)(2,1)S(1)}, u32[]{:S(2)}, u32[]{:S(2)}) collective-permute-start(bf16[1024,256]{1,0:T(8,128)(2,1)S(1)} %pad_maximum_fusion.4), channel_id=1, source_target_pairs={{0,4},{2,6},{4,0},{6,2},{1,5},{3,7},{5,1},{7,3},{8,12},{10,14},{12... | collective-permute-start | bytes 1572872 | tf_op jit(solution)/shard_map/ppermute | solution.py:25
  65.9 8.7 %collective-permute-done.2.refs_3_ = bf16[1024,256]{1,0:T(8,128)(2,1)S(1)} collective-permute-done((bf16[1024,256]{1,0:T(8,128)(2,1)S(1)}, bf16[1024,256]{1,0:T(8,128)(2,1)S(1)}, u32[]{:S(2)}, u32[]{:S(2)}) %collective-permute-start.2) | collective-permute-done | bytes 524320 | tf_op jit(solution)/shard_map/ppermute | solution.py:25
  74.6 0.8 copy-done.7
  75.4 4.1 %collective-permute-done.1.refs_2_ = bf16[1024,256]{1,0:T(8,128)(2,1)S(1)} collective-permute-done((bf16[1024,256]{1,0:T(8,128)(2,1)S(1)}, bf16[1024,256]{1,0:T(8,128)(2,1)S(1)}, u32[]{:S(2)}, u32[]{:S(2)}) %collective-permute-start.1) | collective-permute-done | bytes 524320 | tf_op jit(solution)/shard_map/ppermute | solution.py:25
  79.5 10.0 %all-to-all-done.2 = bf16[32,32,256]{2,1,0:T(8,128)(2,1)S(1)} async-done(((bf16[32,32,256]{2,1,0:T(8,128)(2,1)}), bf16[32,32,256]{2,1,0:T(8,128)(2,1)S(1)}, u32[]{:S(2)}, u32[]{:S(2)}) %all-to-all-start.2) | async-done | bytes 524320 | tf_op jit(solution)/shard_map/all_to_all | solution.py:31
  89.6 4.5 %collective-permute-start.3 = (bf16[768,256]{1,0:T(8,128)(2,1)S(1)}, bf16[768,256]{1,0:T(8,128)(2,1)S(1)}, u32[]{:S(2)}, u32[]{:S(2)}) collective-permute-start(bf16[768,256]{1,0:T(8,128)(2,1)S(1)} %bitcast.61), channel_id=1, source_target_pairs={{0,2},{2,4},{4,6},{6,0},{1,3},{3,5},{5,7},{7,1},{8,10},{10,12},{12... | collective-permute-start | bytes 1179656 | tf_op jit(solution)/shard_map/ppermute | solution.py:25
  94.1 2.3 %collective-permute-start.4 = (bf16[768,256]{1,0:T(8,128)(2,1)S(1)}, bf16[768,256]{1,0:T(8,128)(2,1)}, u32[]{:S(2)}, u32[]{:S(2)}) collective-permute-start(bf16[768,256]{1,0:T(8,128)(2,1)S(1)} %bitcast.62), channel_id=1, source_target_pairs={{0,6},{2,0},{4,2},{6,4},{1,7},{3,1},{5,3},{7,5},{8,14},{10,8},{12,... | collective-permute-start | bytes 1179656 | tf_op jit(solution)/shard_map/ppermute | solution.py:25
  96.4 0.2 fusion.9
  96.6 0.3 convolution_add_fusion
  96.9 0.1 reshape.183
  97.0 13.5 %all_to_all.45 = f32[16,8,128]{2,1,0:T(8,128)S(1)} all-to-all(f32[16,8,128]{2,1,0:T(8,128)S(1)} %bitcast.71), channel_id=1, replica_groups=mesh['z'=16,'yl'=2,'yh'=2,'x'=4,'c'=2] {'yh','x','c'}, dimensions={0} | all-to-all | bytes 131072 | tf_op jit(solution)/shard_map/all_to_all | solution.py:31
  110.6 0.0 collective-permute-done.3.left
  110.6 0.7 copy-done.4
  111.3 2.2 %collective-permute-start.5 = (bf16[384,256]{1,0:T(8,128)(2,1)S(1)}, bf16[384,256]{1,0:T(8,128)(2,1)S(1)}, u32[]{:S(2)}, u32[]{:S(2)}) collective-permute-start(bf16[384,256]{1,0:T(8,128)(2,1)S(1)} %slice.45), channel_id=1, source_target_pairs={{0,2},{2,4},{4,6},{6,0},{1,3},{3,5},{5,7},{7,1},{8,10},{10,12},{12... | collective-permute-start | bytes 589832 | tf_op jit(solution)/shard_map/ppermute | solution.py:25
  113.5 0.9 slice.46
  114.5 4.3 %collective-permute-start.6 = (bf16[384,256]{1,0:T(8,128)(2,1)S(1)}, bf16[384,256]{1,0:T(8,128)(2,1)S(1)}, u32[]{:S(2)}, u32[]{:S(2)}) collective-permute-start(bf16[384,256]{1,0:T(8,128)(2,1)S(1)} %slice.46), channel_id=1, source_target_pairs={{0,6},{2,0},{4,2},{6,4},{1,7},{3,1},{5,3},{7,5},{8,14},{10,8},{12,... | collective-permute-start | bytes 589832 | tf_op jit(solution)/shard_map/ppermute | solution.py:25
  118.8 0.6 broadcast_in_dim.16
  119.4 8.2 %all-to-all-start.4 = ((bf16[32,8,128]{2,1,0:T(8,128)(2,1)}), bf16[32,8,128]{2,1,0:T(8,128)(2,1)S(1)}, u32[]{:S(2)}, u32[]{:S(2)}) async-start(bf16[32,8,128]{2,1,0:T(8,128)(2,1)} %broadcast_in_dim.16), calls=%async_computation.4 | async-start | bytes 131072 | tf_op jit(solution)/shard_map/all_to_all | solution.py:31
  127.6 0.8 pad_maximum_fusion.6.refs_0_
  128.4 0.0 collective-permute-done.5.upper
  128.4 0.0 collective-permute-done.6.lower
  128.4 0.7 copy-done.9
  129.1 0.7 copy-done.10
  129.8 5.0 %shard_map.86 = (bf16[768,512]{1,0:T(8,128)(2,1)}, f32[768,512]{1,0:T(8,128)}) custom-call(bf16[768,256]{1,0:T(8,128)(2,1)} %bitcast.65, bf16[768,256]{1,0:T(8,128)(2,1)} %copy-done.4, bf16[384,256]{1,0:T(8,128)(2,1)} %copy-done.9, bf16[384,256]{1,0:T(8,128)(2,1)} %copy-done.10, bf16[768,256]{1,0:T(8,128)(2,1)} %collective-permute-done.4.right, ...), custom_call_target="tpu_custom_call" | custom-call | flops 1610612736 | bytes 6291456 | tf_op jit(solution)/shard_map/pallas_call | solution.py:67
  134.8 5.3 %all-to-all-done.4 = bf16[32,8,128]{2,1,0:T(8,128)(2,1)S(1)} async-done(((bf16[32,8,128]{2,1,0:T(8,128)(2,1)}), bf16[32,8,128]{2,1,0:T(8,128)(2,1)S(1)}, u32[]{:S(2)}, u32[]{:S(2)}) %all-to-all-start.4) | async-done | bytes 65568 | tf_op jit(solution)/shard_map/all_to_all | solution.py:31
  140.2 4.5 %collective-permute-start.7 = (bf16[768,512]{1,0:T(8,128)(2,1)}, bf16[768,512]{1,0:T(8,128)(2,1)}, u32[]{:S(2)}, u32[]{:S(2)}) collective-permute-start(bf16[768,512]{1,0:T(8,128)(2,1)} %get-tuple-element.24), channel_id=1, source_target_pairs={{0,1},{1,0},{2,3},{3,2},{4,5},{5,4},{6,7},{7,6},{8,9},{9,8},{10,11... | collective-permute-start | bytes 2359304 | tf_op jit(solution)/shard_map/ppermute | solution.py:21
  144.7 0.1 copy.23
  144.8 0.8 broadcast_in_dim.17
  145.6 3.4 %all-to-all-start.5 = ((bf16[8,96,256]{2,1,0:T(8,128)(2,1)}), bf16[8,96,256]{2,1,0:T(8,128)(2,1)S(1)}, u32[]{:S(2)}, u32[]{:S(2)}) async-start(bf16[8,96,256]{2,1,0:T(8,128)(2,1)} %broadcast_in_dim.17), calls=%async_computation.5 | async-start | bytes 786432 | tf_op jit(solution)/shard_map/all_to_all | solution.py:31
  149.0 0.0 collective-permute-done.7
  149.0 2.1 %add_convert_fusion = bf16[768,256]{1,0:T(8,128)(2,1)} fusion(f32[768,512]{1,0:T(8,128)} %get-tuple-element.21, bf16[768,512]{1,0:T(8,128)(2,1)} %collective-permute-done.7), kind=kLoop, calls=%fused_computation.7 | loop fusion | flops 589824 | bytes 1572864 | tf_op jit(solution)/shard_map/convert_element_type | solution.py:149
  151.0 2.9 %collective-permute-start.8 = (bf16[768,256]{1,0:T(8,128)(2,1)}, bf16[768,256]{1,0:T(8,128)(2,1)S(1)}, u32[]{:S(2)}, u32[]{:S(2)}) collective-permute-start(bf16[768,256]{1,0:T(8,128)(2,1)} %add_convert_fusion), channel_id=1, source_target_pairs={{0,8},{8,0},{1,9},{9,1},{2,10},{10,2},{3,11},{11,3},{4,12},{12,4},... | collective-permute-start | bytes 1179656 | tf_op jit(solution)/shard_map/ppermute | solution.py:21
  153.9 3.1 %all-to-all-done.5 = bf16[8,96,256]{2,1,0:T(8,128)(2,1)S(1)} async-done(((bf16[8,96,256]{2,1,0:T(8,128)(2,1)}), bf16[8,96,256]{2,1,0:T(8,128)(2,1)S(1)}, u32[]{:S(2)}, u32[]{:S(2)}) %all-to-all-start.5) | async-done | bytes 393248 | tf_op jit(solution)/shard_map/all_to_all | solution.py:31
  157.0 1.0 bitcast_convert_fusion
  158.0 7.3 %collective-permute-done.8 = bf16[768,256]{1,0:T(8,128)(2,1)S(1)} collective-permute-done((bf16[768,256]{1,0:T(8,128)(2,1)}, bf16[768,256]{1,0:T(8,128)(2,1)S(1)}, u32[]{:S(2)}, u32[]{:S(2)}) %collective-permute-start.8) | collective-permute-done | bytes 393248 | tf_op jit(solution)/shard_map/ppermute | solution.py:21
  165.3 2.0 %add_multiply_fusion = f32[768,256]{1,0:T(8,128)} fusion(bf16[768,256]{1,0:T(8,128)(2,1)S(1)} %collective-permute-done.8, f32[768,512]{1,0:T(8,128)S(1)} %copy-done.2, bf16[768,512]{1,0:T(8,128)(2,1)} %collective-permute-done.7), kind=kLoop, calls=%fused_computation.6 | loop fusion | flops 983040 | bytes 2359296 | tf_op jit(solution)/shard_map/mul | solution.py:151
  (36 shorter events, 0.4 us)
Async XLA Ops:
  0.6 1.2 copy-start
  0.6 4.4 %copy-start.6 = (s32[256]{0:T(256)S(1)}, s32[256]{0:T(256)}, u32[]{:S(2)}) copy-start(s32[256]{0:T(256)} %param.13) | copy-start | bytes 3076
  6.0 22.5 %all-to-all-start = ((f32[16,72,128]{2,1,0:T(8,128)}), f32[16,72,128]{2,1,0:T(8,128)S(1)}, u32[]{:S(2)}, u32[]{:S(2)}) async-start(f32[16,72,128]{2,1,0:T(8,128)} %pad_maximum_fusion), calls=%async_computation | async-start | bytes 1179648 | tf_op jit(solution)/shard_map/all_to_all | solution.py:31
  16.2 5.9 %copy-start.5 = (s32[1,1024]{1,0:T(1,128)S(1)}, s32[1,1024]{1,0:T(1,128)}, u32[]{:S(2)}) copy-start(s32[1,1024]{1,0:T(1,128)} %param.11) | copy-start | bytes 12292
  18.8 26.6 %collective-permute-start = (bf16[1024,256]{1,0:T(8,128)(2,1)S(1)}, bf16[1024,256]{1,0:T(8,128)(2,1)}, u32[]{:S(2)}, u32[]{:S(2)}) collective-permute-start(bf16[1024,256]{1,0:T(8,128)(2,1)S(1)} %pad_maximum_fusion.3), channel_id=1, source_target_pairs={{0,2},{2,4},{4,6},{6,0},{1,3},{3,5},{5,7},{7,1},{8,10},{10,12},{12... | collective-permute-start | bytes 1572872 | tf_op jit(solution)/shard_map/ppermute | solution.py:25
  29.3 13.4 %all-to-all-start.1 = ((bf16[16,64,128]{2,1,0:T(8,128)(2,1)}), bf16[16,64,128]{2,1,0:T(8,128)(2,1)S(1)}, u32[]{:S(2)}, u32[]{:S(2)}) async-start(bf16[16,64,128]{2,1,0:T(8,128)(2,1)} %broadcast_in_dim.13), calls=%async_computation.1 | async-start | bytes 524288 | tf_op jit(solution)/shard_map/all_to_all | solution.py:31
  42.9 15.9 %copy-start.3 = (bf16[256,256]{1,0:T(8,128)(2,1)S(1)}, bf16[256,256]{1,0:T(8,128)(2,1)}, u32[]{:S(2)}) copy-start(bf16[256,256]{1,0:T(8,128)(2,1)} %get-tuple-element.30) | copy-start | bytes 393220
  45.4 44.1 %all-to-all-start.2 = ((bf16[32,32,256]{2,1,0:T(8,128)(2,1)}), bf16[32,32,256]{2,1,0:T(8,128)(2,1)S(1)}, u32[]{:S(2)}, u32[]{:S(2)}) async-start(bf16[32,32,256]{2,1,0:T(8,128)(2,1)} %pad_maximum_fusion.2), calls=%async_computation.2 | async-start | bytes 1048576 | tf_op jit(solution)/shard_map/all_to_all | solution.py:31
  59.9 14.6 %collective-permute-start.2 = (bf16[1024,256]{1,0:T(8,128)(2,1)S(1)}, bf16[1024,256]{1,0:T(8,128)(2,1)S(1)}, u32[]{:S(2)}, u32[]{:S(2)}) collective-permute-start(bf16[1024,256]{1,0:T(8,128)(2,1)S(1)} %pad_maximum_fusion.5), channel_id=1, source_target_pairs={{0,6},{2,0},{4,2},{6,4},{1,7},{3,1},{5,3},{7,5},{8,14},{10,8},{12,... | collective-permute-start | bytes 1572872 | tf_op jit(solution)/shard_map/ppermute | solution.py:25
  63.2 16.3 %collective-permute-start.1 = (bf16[1024,256]{1,0:T(8,128)(2,1)S(1)}, bf16[1024,256]{1,0:T(8,128)(2,1)S(1)}, u32[]{:S(2)}, u32[]{:S(2)}) collective-permute-start(bf16[1024,256]{1,0:T(8,128)(2,1)S(1)} %pad_maximum_fusion.4), channel_id=1, source_target_pairs={{0,4},{2,6},{4,0},{6,2},{1,5},{3,7},{5,1},{7,3},{8,12},{10,14},{12... | collective-permute-start | bytes 1572872 | tf_op jit(solution)/shard_map/ppermute | solution.py:25
  74.6 0.8 copy-start.7
  79.5 10.1 %copy-start.8 = (bf16[1024,256]{1,0:T(8,128)(2,1)}, bf16[1024,256]{1,0:T(8,128)(2,1)S(1)}, u32[]{:S(2)}) copy-start(bf16[1024,256]{1,0:T(8,128)(2,1)S(1)} %collective-permute-done.1.refs_2_) | copy-start | bytes 1572868
  89.5 38.9 %copy-start.1 = (bf16[32,24,256]{2,1,0:T(8,128)(2,1)}, bf16[32,24,256]{2,1,0:T(8,128)(2,1)S(1)}, u32[]{:S(2)}) copy-start(bf16[32,24,256]{2,1,0:T(8,128)(2,1)S(1)} %slice.43) | copy-start | bytes 1179652
  89.6 21.0 %collective-permute-start.3 = (bf16[768,256]{1,0:T(8,128)(2,1)S(1)}, bf16[768,256]{1,0:T(8,128)(2,1)S(1)}, u32[]{:S(2)}, u32[]{:S(2)}) collective-permute-start(bf16[768,256]{1,0:T(8,128)(2,1)S(1)} %bitcast.61), channel_id=1, source_target_pairs={{0,2},{2,4},{4,6},{6,0},{1,3},{3,5},{5,7},{7,1},{8,10},{10,12},{12... | collective-permute-start | bytes 1179656 | tf_op jit(solution)/shard_map/ppermute | solution.py:25
  94.1 16.5 %collective-permute-start.4 = (bf16[768,256]{1,0:T(8,128)(2,1)S(1)}, bf16[768,256]{1,0:T(8,128)(2,1)}, u32[]{:S(2)}, u32[]{:S(2)}) collective-permute-start(bf16[768,256]{1,0:T(8,128)(2,1)S(1)} %bitcast.62), channel_id=1, source_target_pairs={{0,6},{2,0},{4,2},{6,4},{1,7},{3,1},{5,3},{7,5},{8,14},{10,8},{12,... | collective-permute-start | bytes 1179656 | tf_op jit(solution)/shard_map/ppermute | solution.py:25
  110.6 0.7 copy-start.4
  111.3 17.1 %collective-permute-start.5 = (bf16[384,256]{1,0:T(8,128)(2,1)S(1)}, bf16[384,256]{1,0:T(8,128)(2,1)S(1)}, u32[]{:S(2)}, u32[]{:S(2)}) collective-permute-start(bf16[384,256]{1,0:T(8,128)(2,1)S(1)} %slice.45), channel_id=1, source_target_pairs={{0,2},{2,4},{4,6},{6,0},{1,3},{3,5},{5,7},{7,1},{8,10},{10,12},{12... | collective-permute-start | bytes 589832 | tf_op jit(solution)/shard_map/ppermute | solution.py:25
  114.5 14.0 %collective-permute-start.6 = (bf16[384,256]{1,0:T(8,128)(2,1)S(1)}, bf16[384,256]{1,0:T(8,128)(2,1)S(1)}, u32[]{:S(2)}, u32[]{:S(2)}) collective-permute-start(bf16[384,256]{1,0:T(8,128)(2,1)S(1)} %slice.46), channel_id=1, source_target_pairs={{0,6},{2,0},{4,2},{6,4},{1,7},{3,1},{5,3},{7,5},{8,14},{10,8},{12,... | collective-permute-start | bytes 589832 | tf_op jit(solution)/shard_map/ppermute | solution.py:25
  119.4 20.8 %all-to-all-start.4 = ((bf16[32,8,128]{2,1,0:T(8,128)(2,1)}), bf16[32,8,128]{2,1,0:T(8,128)(2,1)S(1)}, u32[]{:S(2)}, u32[]{:S(2)}) async-start(bf16[32,8,128]{2,1,0:T(8,128)(2,1)} %broadcast_in_dim.16), calls=%async_computation.4 | async-start | bytes 131072 | tf_op jit(solution)/shard_map/all_to_all | solution.py:31
  128.4 0.7 copy-start.9
  129.1 0.7 copy-start.10
  140.1 25.2 %copy-start.2 = (f32[768,512]{1,0:T(8,128)S(1)}, f32[768,512]{1,0:T(8,128)}, u32[]{:S(2)}) copy-start(f32[768,512]{1,0:T(8,128)} %get-tuple-element.21) | copy-start | bytes 4718596
  140.2 8.8 %collective-permute-start.7 = (bf16[768,512]{1,0:T(8,128)(2,1)}, bf16[768,512]{1,0:T(8,128)(2,1)}, u32[]{:S(2)}, u32[]{:S(2)}) collective-permute-start(bf16[768,512]{1,0:T(8,128)(2,1)} %get-tuple-element.24), channel_id=1, source_target_pairs={{0,1},{1,0},{2,3},{3,2},{4,5},{5,4},{6,7},{7,6},{8,9},{9,8},{10,11... | collective-permute-start | bytes 2359304 | tf_op jit(solution)/shard_map/ppermute | solution.py:21
  145.6 11.5 %all-to-all-start.5 = ((bf16[8,96,256]{2,1,0:T(8,128)(2,1)}), bf16[8,96,256]{2,1,0:T(8,128)(2,1)S(1)}, u32[]{:S(2)}, u32[]{:S(2)}) async-start(bf16[8,96,256]{2,1,0:T(8,128)(2,1)} %broadcast_in_dim.17), calls=%async_computation.5 | async-start | bytes 786432 | tf_op jit(solution)/shard_map/all_to_all | solution.py:31
  151.0 14.3 %collective-permute-start.8 = (bf16[768,256]{1,0:T(8,128)(2,1)}, bf16[768,256]{1,0:T(8,128)(2,1)S(1)}, u32[]{:S(2)}, u32[]{:S(2)}) collective-permute-start(bf16[768,256]{1,0:T(8,128)(2,1)} %add_convert_fusion), channel_id=1, source_target_pairs={{0,8},{8,0},{1,9},{9,1},{2,10},{10,2},{3,11},{11,3},{4,12},{12,4},... | collective-permute-start | bytes 1179656 | tf_op jit(solution)/shard_map/ppermute | solution.py:21

commit v9 on v7

--- a/solution.py
+++ b/solution.py
@@ -45,14 +45,16 @@
 
 
 def partial_kernel(own, left, upper, lower, right, *refs):
-    stored, (away_ref, kept_ref) = refs[:4], refs[4:]
-    half = away_ref.shape[1]
+    stored, outs = refs[:4], refs[4:]
     first_half = pl.program_id(0) < pl.num_programs(0) // 2
     across = jnp.where(first_half, upper[...], lower[...])
     queries = (own[...], left[...], across, right[...])
-    for first, out_ref in ((0, away_ref), (half, kept_ref)):
-        terms = [dot_t(q, t[pl.ds(first, half), :]) for q, t in zip(queries, stored)]
+    first = 0
+    for out_ref in outs:
+        count = out_ref.shape[1]
+        terms = [dot_t(q, t[pl.ds(first, count), :]) for q, t in zip(queries, stored)]
         out_ref[...] = ((terms[0] + terms[1]) + (terms[2] + terms[3])).astype(out_ref.dtype)
+        first += count
 
 
 def partial(queries, stored):
@@ -63,13 +65,13 @@
     upper = pl.BlockSpec((tile, width), lambda i: (jnp.minimum(i, steps // 2 - 1), 0))
     lower = pl.BlockSpec((tile, width), lambda i: (jnp.maximum(i - steps // 2, 0), 0))
     whole = pl.BlockSpec((count, width), lambda i: (0, 0))
-    out = pl.BlockSpec((tile, half), lambda i: (i, 0))
+    outs = ((half, BF16), (half // 2, F32), (half // 2, F32))
     return pl.pallas_call(
         partial_kernel,
         grid=(steps,),
-        out_shape=(jax.ShapeDtypeStruct((height, half), BF16), jax.ShapeDtypeStruct((height, half), F32)),
+        out_shape=tuple(jax.ShapeDtypeStruct((height, n), kind) for n, kind in outs),
         in_specs=[rows, rows, upper, lower, rows] + [whole] * 4,
-        out_specs=(out, out),
+        out_specs=tuple(pl.BlockSpec((tile, n), lambda i: (i, 0)) for n, _ in outs),
         cost_estimate=pl.CostEstimate(flops=8 * height * count * width, bytes_accessed=6 << 20, transcendentals=0),
     )(*queries, *stored)
 
@@ -122,9 +124,9 @@
         return jnp.concatenate([block(1 - yh, 1 - c), block(yh, 1 - c), block(1 - yh, c), block(yh, c)])
 
     stored = [along_x(rows_for((x + d) % 4), d) for d in range(4)]
-    second, stored[1], stored[3] = lax.optimization_barrier((second, stored[1], stored[3]))
+    second, stored[1] = lax.optimization_barrier((second, stored[1]))
     second = exchange(second, DP)
-    second, stored[2] = lax.optimization_barrier((second, stored[2]))
+    second, stored[2], stored[3] = lax.optimization_barrier((second, stored[2], stored[3]))
     queries = second[:, :EX_DEV].reshape(32 * EX_DEV, width)
     height = queries.shape[0]
 
@@ -141,13 +143,13 @@
 
     across = [along_x(left[: height // 2], 1), along_x(right[height // 2 :], 3)]
 
-    away, kept = partial([queries, left, *across, right], stored)
+    away, far, near = partial([queries, left, *across, right], stored)
     away, halves = lax.optimization_barrier((away, halves))
     away = swap(away, "c")
-    quarter = kept.shape[1] // 2
-    beyond = swap((kept[:, :quarter] + away[:, :quarter].astype(F32)).astype(BF16), "yh")
+    quarter = far.shape[1]
+    beyond = swap((far + away[:, :quarter].astype(F32)).astype(BF16), "yh")
     doc_influence = lax.all_gather(halves, "c", axis=0).transpose(0, 2, 1).reshape(height, DOCS).astype(F32)
-    scores = (kept[:, quarter:] + away[:, quarter:].astype(F32) + beyond.astype(F32)) * 0.125
+    scores = (near + away[:, quarter:].astype(F32) + beyond.astype(F32)) * 0.125
     return (scores, doc_influence)
 
 

time: 163 us -> 166 us (1.018)
  starting transfers between devices: 70.3 us -> 76.7 us
  waiting for transfers between devices: 58.8 us -> 54.9 us
    all_to_all x5, starting transfers between devices: 38.8 us -> 43.3 us  [exchange(): return lax.all_to_all(flat, axes, 0, 0, tiled=True).reshape(shape)]
    all_to_all x5, waiting for transfers between devices: 29 us -> 24.8 us  [exchange(): return lax.all_to_all(flat, axes, 0, 0, tiled=True).reshape(shape)]
  transfers between devices with their start and end apart: 14 -> 14, of which waited for: 12 -> 13; matrix products, arithmetic and copies ran while one was open for 8% -> 8% of each run, Pallas kernels for 3% -> 3%
where the time goes in v9:
time: 166 us; the launch traced here: 165 us
  starting transfers between devices  76.7 us (46%)
  waiting for transfers between devices  54.9 us (33%)
  other arithmetic  9.25 us (6%)
  local copies, waits for them, and re-layouts  8.78 us (5%)
  matrix products  6.57 us (4%)
  Pallas kernels  5 us (3%)
  blocking collectives  2.37 us (1%)
    all_to_all x5, starting transfers between devices, exchange(): return lax.all_to_all(flat, axes, 0, 0, tiled=True).reshape(shape)  43.3 us
    all_to_all x5, waiting for transfers between devices, exchange(): return lax.all_to_all(flat, axes, 0, 0, tiled=True).reshape(shape)  24.8 us
    ppermute x7, starting transfers between devices, along_x(): lax.ppermute(value, 'x', [(i, (i + distance) % 4) for i in range(4)])  22.4 us
    ppermute x7, waiting for transfers between devices, along_x(): lax.ppermute(value, 'x', [(i, (i + distance) % 4) for i in range(4)])  22.1 us
    ppermute x2, starting transfers between devices, swap(): return lax.ppermute(value, axis, [(0, 1), (1, 0)])  11.1 us
    ppermute x2, waiting for transfers between devices, swap(): return lax.ppermute(value, axis, [(0, 1), (1, 0)])  8.01 us
    pallas_call x1, Pallas kernels, partial(): pl.pallas_call(partial_kernel, grid=(steps,), out_shape=tuple((jax.ShapeD...  5 us
  transfers between devices with their start and end apart: 14, of which 13 were waited for; matrix products, arithmetic and copies ran while one was open for 8% of the time, Pallas kernels for 3%

profile of v9, /device:TPU:1, one launch (start us, length us, event | category | flops | bytes accessed | tf_op | source)
XLA Modules:
  0.0 164.6 jit_solution(6124044161334865784)
XLA Ops:
  0.6 0.0 copy-start
  0.6 0.0 copy-start.6
  0.7 1.2 copy-done
  1.9 1.3 fusion.10
  3.1 1.7 %fusion.11 = f32[1024,64]{0,1:T(8,128)S(1)} fusion(bf16[1024,512]{1,0:T(8,128)(2,1)} %param.8, bf16[512,64]{0,1:T(8,128)(2,1)} %param.10), kind=kOutput, calls=%fused_computation.50 | convolution fusion | flops 67108864 | bytes 1376256 | tf_op jit(solution)/shard_map/dot_general | solution.py:89
  4.9 0.2 copy.15
  5.1 0.9 pad_maximum_fusion
  6.0 10.3 %all-to-all-start = ((f32[16,72,128]{2,1,0:T(8,128)}), f32[16,72,128]{2,1,0:T(8,128)S(1)}, u32[]{:S(2)}, u32[]{:S(2)}) async-start(f32[16,72,128]{2,1,0:T(8,128)} %pad_maximum_fusion), calls=%async_computation | async-start | bytes 1179648 | tf_op jit(solution)/shard_map/all_to_all | solution.py:31
  16.2 2.5 %dynamic-slice_bitcast_fusion.3 = (bf16[256,256]{1,0:T(8,128)(2,1)S(1)}, bf16[256,256]{1,0:T(8,128)(2,1)S(1)}, bf16[256,256]{1,0:T(8,128)(2,1)S(1)}, bf16[256,25...) fusion(bf16[2,4,2,256,256]{4,3,2,1,0:T(8,128)(2,1)} %bitcast.69, ...), kind=kLoop, calls=%fused_computation.23 | loop fusion | bytes 4194336 | tf_op jit(solution)/shard_map/reshape | solution.py:122
  18.8 3.3 %collective-permute-start = (bf16[1024,256]{1,0:T(8,128)(2,1)S(1)}, bf16[1024,256]{1,0:T(8,128)(2,1)}, u32[]{:S(2)}, u32[]{:S(2)}) collective-permute-start(bf16[1024,256]{1,0:T(8,128)(2,1)S(1)} %pad_maximum_fusion.3), channel_id=1, source_target_pairs={{0,2},{2,4},{4,6},{6,0},{1,3},{3,5},{5,7},{7,1},{8,10},{10,12},{12... | collective-permute-start | bytes 1572872 | tf_op jit(solution)/shard_map/ppermute | solution.py:25
  22.1 0.1 convert_reduce_fusion.1
  22.3 6.2 %all-to-all-done = f32[16,72,128]{2,1,0:T(8,128)S(1)} async-done(((f32[16,72,128]{2,1,0:T(8,128)}), f32[16,72,128]{2,1,0:T(8,128)S(1)}, u32[]{:S(2)}, u32[]{:S(2)}) %all-to-all-start) | async-done | bytes 589856 | tf_op jit(solution)/shard_map/all_to_all | solution.py:31
  28.5 0.8 broadcast_in_dim.11
  29.3 4.6 %all-to-all-start.1 = ((bf16[16,64,128]{2,1,0:T(8,128)(2,1)}), bf16[16,64,128]{2,1,0:T(8,128)(2,1)S(1)}, u32[]{:S(2)}, u32[]{:S(2)}) async-start(bf16[16,64,128]{2,1,0:T(8,128)(2,1)} %broadcast_in_dim.11), calls=%async_computation.1 | async-start | bytes 524288 | tf_op jit(solution)/shard_map/all_to_all | solution.py:31
  33.9 3.0 %fusion.3 = bf16[32,8,256]{2,1,0:T(8,128)(2,1)} fusion(bf16[4096,256]{1,0:T(8,128)(2,1)} %param.12, s32[4096]{0:T(1024)S(1)} %bitcast.75), kind=kOutput, calls=%fused_computation.4 | convolution fusion | flops 537985024 | bytes 2244608 | tf_op jit(solution)/shard_map/dot_general | solution.py:114
  36.9 5.8 %all-to-all-done.1 = bf16[16,64,128]{2,1,0:T(8,128)(2,1)S(1)} async-done(((bf16[16,64,128]{2,1,0:T(8,128)(2,1)}), bf16[16,64,128]{2,1,0:T(8,128)(2,1)S(1)}, u32[]{:S(2)}, u32[]{:S(2)}) %all-to-all-start.1) | async-done | bytes 262176 | tf_op jit(solution)/shard_map/all_to_all | solution.py:31
  42.6 0.1 slice.41
  42.8 0.1 constant_dynamic-slice_fusion
  42.9 0.1 copy.16
  43.0 0.1 broadcast_multiply_fusion
  43.2 0.1 mul.44
  43.2 0.2 fusion.4
  43.4 0.1 reshape.163
  43.5 0.1 divide_convert_fusion
  43.6 1.8 %pad_maximum_fusion.2 = bf16[32,32,256]{2,1,0:T(8,128)(2,1)} fusion(bf16[32,8,256]{2,1,0:T(8,128)(2,1)} %fusion.3, bf16[32,24,256]{2,1,0:T(8,128)(2,1)S(1)} %broadcast_in_dim.12), kind=kLoop, calls=%fused_computation.12 | loop fusion | flops 1048576 | bytes 1048576 | tf_op jit(solution)/shard_map/concatenate | solution.py:116
  45.4 0.0 collective-permute-done.refs_1_
  45.4 13.4 %all-to-all-start.2 = ((bf16[32,32,256]{2,1,0:T(8,128)(2,1)}), bf16[32,32,256]{2,1,0:T(8,128)(2,1)S(1)}, u32[]{:S(2)}, u32[]{:S(2)}) async-start(bf16[32,32,256]{2,1,0:T(8,128)(2,1)} %pad_maximum_fusion.2), calls=%async_computation.2 | async-start | bytes 1048576 | tf_op jit(solution)/shard_map/all_to_all | solution.py:31
  58.8 1.1 pad_maximum_fusion.5
  60.0 3.2 %collective-permute-start.2 = (bf16[1024,256]{1,0:T(8,128)(2,1)S(1)}, bf16[1024,256]{1,0:T(8,128)(2,1)S(1)}, u32[]{:S(2)}, u32[]{:S(2)}) collective-permute-start(bf16[1024,256]{1,0:T(8,128)(2,1)S(1)} %pad_maximum_fusion.5), channel_id=1, source_target_pairs={{0,6},{2,0},{4,2},{6,4},{1,7},{3,1},{5,3},{7,5},{8,14},{10,8},{12,... | collective-permute-start | bytes 1572872 | tf_op jit(solution)/shard_map/ppermute | solution.py:25
  63.2 2.7 %collective-permute-start.1 = (bf16[1024,256]{1,0:T(8,128)(2,1)S(1)}, bf16[1024,256]{1,0:T(8,128)(2,1)}, u32[]{:S(2)}, u32[]{:S(2)}) collective-permute-start(bf16[1024,256]{1,0:T(8,128)(2,1)S(1)} %pad_maximum_fusion.4), channel_id=1, source_target_pairs={{0,4},{2,6},{4,0},{6,2},{1,5},{3,7},{5,1},{7,3},{8,12},{10,14},{12... | collective-permute-start | bytes 1572872 | tf_op jit(solution)/shard_map/ppermute | solution.py:25
  65.9 8.7 %collective-permute-done.2.refs_3_ = bf16[1024,256]{1,0:T(8,128)(2,1)S(1)} collective-permute-done((bf16[1024,256]{1,0:T(8,128)(2,1)S(1)}, bf16[1024,256]{1,0:T(8,128)(2,1)S(1)}, u32[]{:S(2)}, u32[]{:S(2)}) %collective-permute-start.2) | collective-permute-done | bytes 524320 | tf_op jit(solution)/shard_map/ppermute | solution.py:25
  74.6 0.8 copy-done.7
  75.4 4.2 %collective-permute-done.1.refs_2_ = bf16[1024,256]{1,0:T(8,128)(2,1)} collective-permute-done((bf16[1024,256]{1,0:T(8,128)(2,1)S(1)}, bf16[1024,256]{1,0:T(8,128)(2,1)}, u32[]{:S(2)}, u32[]{:S(2)}) %collective-permute-start.1) | collective-permute-done | bytes 524320 | tf_op jit(solution)/shard_map/ppermute | solution.py:25
  79.6 9.9 %all-to-all-done.2 = bf16[32,32,256]{2,1,0:T(8,128)(2,1)S(1)} async-done(((bf16[32,32,256]{2,1,0:T(8,128)(2,1)}), bf16[32,32,256]{2,1,0:T(8,128)(2,1)S(1)}, u32[]{:S(2)}, u32[]{:S(2)}) %all-to-all-start.2) | async-done | bytes 524320 | tf_op jit(solution)/shard_map/all_to_all | solution.py:31
  89.6 0.2 fusion.9
  89.8 0.3 convolution_add_fusion
  90.0 0.7 broadcast_in_dim.13
  90.8 6.9 %all-to-all-start.3 = ((f32[16,8,384]{2,1,0:T(8,128)}), f32[16,8,384]{2,1,0:T(8,128)S(1)}, u32[]{:S(2)}, u32[]{:S(2)}) async-start(f32[16,8,384]{2,1,0:T(8,128)} %bitcast.22), calls=%async_computation.3 | async-start | bytes 393216 | tf_op jit(solution)/shard_map/all_to_all | solution.py:31
  97.7 3.3 %collective-permute-start.3 = (bf16[768,256]{1,0:T(8,128)(2,1)S(1)}, bf16[768,256]{1,0:T(8,128)(2,1)S(1)}, u32[]{:S(2)}, u32[]{:S(2)}) collective-permute-start(bf16[768,256]{1,0:T(8,128)(2,1)S(1)} %bitcast.64), channel_id=1, source_target_pairs={{0,2},{2,4},{4,6},{6,0},{1,3},{3,5},{5,7},{7,1},{8,10},{10,12},{12... | collective-permute-start | bytes 1179656 | tf_op jit(solution)/shard_map/ppermute | solution.py:25
  101.0 3.2 %collective-permute-start.4 = (bf16[768,256]{1,0:T(8,128)(2,1)S(1)}, bf16[768,256]{1,0:T(8,128)(2,1)S(1)}, u32[]{:S(2)}, u32[]{:S(2)}) collective-permute-start(bf16[768,256]{1,0:T(8,128)(2,1)S(1)} %bitcast.65), channel_id=1, source_target_pairs={{0,6},{2,0},{4,2},{6,4},{1,7},{3,1},{5,3},{7,5},{8,14},{10,8},{12,... | collective-permute-start | bytes 1179656 | tf_op jit(solution)/shard_map/ppermute | solution.py:25
  104.2 1.6 all-to-all-done.3
  105.9 6.2 %collective-permute-done.3.left = bf16[768,256]{1,0:T(8,128)(2,1)S(1)} collective-permute-done((bf16[768,256]{1,0:T(8,128)(2,1)S(1)}, bf16[768,256]{1,0:T(8,128)(2,1)S(1)}, u32[]{:S(2)}, u32[]{:S(2)}) %collective-permute-start.3) | collective-permute-done | bytes 393248 | tf_op jit(solution)/shard_map/ppermute | solution.py:25
  112.1 0.8 collective-permute-done.4.right
  112.9 0.8 broadcast_in_dim.14
  113.7 8.0 %all-to-all-start.4 = ((bf16[32,8,384]{2,1,0:T(8,128)(2,1)}), bf16[32,8,384]{2,1,0:T(8,128)(2,1)S(1)}, u32[]{:S(2)}, u32[]{:S(2)}) async-start(bf16[32,8,384]{2,1,0:T(8,128)(2,1)} %broadcast_in_dim.14), calls=%async_computation.4 | async-start | bytes 393216 | tf_op jit(solution)/shard_map/all_to_all | solution.py:31
  121.7 3.1 %collective-permute-start.5 = (bf16[384,256]{1,0:T(8,128)(2,1)S(1)}, bf16[384,256]{1,0:T(8,128)(2,1)S(1)}, u32[]{:S(2)}, u32[]{:S(2)}) collective-permute-start(bf16[384,256]{1,0:T(8,128)(2,1)S(1)} %slice.36), channel_id=1, source_target_pairs={{0,2},{2,4},{4,6},{6,0},{1,3},{3,5},{5,7},{7,1},{8,10},{10,12},{12... | collective-permute-start | bytes 589832 | tf_op jit(solution)/shard_map/ppermute | solution.py:25
  124.8 3.6 %collective-permute-start.6 = (bf16[384,256]{1,0:T(8,128)(2,1)S(1)}, bf16[384,256]{1,0:T(8,128)(2,1)}, u32[]{:S(2)}, u32[]{:S(2)}) collective-permute-start(bf16[384,256]{1,0:T(8,128)(2,1)S(1)} %slice.37), channel_id=1, source_target_pairs={{0,6},{2,0},{4,2},{6,4},{1,7},{3,1},{5,3},{7,5},{8,14},{10,8},{12,... | collective-permute-start | bytes 589832 | tf_op jit(solution)/shard_map/ppermute | solution.py:25
  128.4 0.8 pad_maximum_fusion.6.refs_0_
  129.3 0.5 collective-permute-done.5.upper
  129.8 1.7 %collective-permute-done.6.lower = bf16[384,256]{1,0:T(8,128)(2,1)} collective-permute-done((bf16[384,256]{1,0:T(8,128)(2,1)S(1)}, bf16[384,256]{1,0:T(8,128)(2,1)}, u32[]{:S(2)}, u32[]{:S(2)}) %collective-permute-start.6) | collective-permute-done | bytes 196640 | tf_op jit(solution)/shard_map/ppermute | solution.py:25
  131.6 0.0 copy-done.3
  131.6 0.0 copy-done.8
  131.6 5.0 %shard_map.86 = (bf16[768,512]{1,0:T(8,128)(2,1)}, f32[768,256]{1,0:T(8,128)}, f32[768,256]{1,0:T(8,128)}) custom-call(bf16[768,256]{1,0:T(8,128)(2,1)} %bitcast.66, bf16[768,256]{1,0:T(8,128)(2,1)} %copy-done.3, bf16[384,256]{1,0:T(8,128)(2,1)} %copy-done.8, bf16[384,256]{1,0:T(8,128)(2,1)} %collective-permute-done.6.lower, bf16[768,256]{1,0:T(8,128)(2,1)} %copy-done.4, ...), custom_call_target="tpu_custom_call" | custom-call | flops 1610612736 | bytes 6291456 | tf_op jit(solution)/shard_map/pallas_call | solution.py:69
  136.6 1.3 all-to-all-done.4
  137.8 5.9 %collective-permute-start.7 = (bf16[768,512]{1,0:T(8,128)(2,1)}, bf16[768,512]{1,0:T(8,128)(2,1)S(1)}, u32[]{:S(2)}, u32[]{:S(2)}) collective-permute-start(bf16[768,512]{1,0:T(8,128)(2,1)} %get-tuple-element.25), channel_id=1, source_target_pairs={{0,1},{1,0},{2,3},{3,2},{4,5},{5,4},{6,7},{7,6},{8,9},{9,8},{10,11... | collective-permute-start | bytes 2359304 | tf_op jit(solution)/shard_map/ppermute | solution.py:21
  143.7 2.1 %collective-permute-done.7 = bf16[768,512]{1,0:T(8,128)(2,1)S(1)} collective-permute-done((bf16[768,512]{1,0:T(8,128)(2,1)}, bf16[768,512]{1,0:T(8,128)(2,1)S(1)}, u32[]{:S(2)}, u32[]{:S(2)}) %collective-permute-start.7) | collective-permute-done | bytes 786464 | tf_op jit(solution)/shard_map/ppermute | solution.py:21
  145.8 2.0 %add_convert_fusion = bf16[768,256]{1,0:T(8,128)(2,1)} fusion(f32[768,256]{1,0:T(8,128)} %get-tuple-element.26, bf16[768,512]{1,0:T(8,128)(2,1)S(1)} %collective-permute-done.7), kind=kLoop, calls=%fused_computation.8 | loop fusion | flops 589824 | bytes 1572864 | tf_op jit(solution)/shard_map/convert_element_type | solution.py:150
  147.9 5.2 %collective-permute-start.8 = (bf16[768,256]{1,0:T(8,128)(2,1)}, bf16[768,256]{1,0:T(8,128)(2,1)}, u32[]{:S(2)}, u32[]{:S(2)}) collective-permute-start(bf16[768,256]{1,0:T(8,128)(2,1)} %add_convert_fusion), channel_id=1, source_target_pairs={{0,8},{8,0},{1,9},{9,1},{2,10},{10,2},{3,11},{11,3},{4,12},{12,4},... | collective-permute-start | bytes 1179656 | tf_op jit(solution)/shard_map/ppermute | solution.py:21
  153.1 2.4 %all-gather = bf16[512,384]{1,0:T(8,128)(2,1)S(1)} all-gather(bf16[256,384]{1,0:T(8,128)(2,1)S(1)} %bitcast.73), channel_id=2, replica_groups=mesh['z'=16,'yl'=2,'yh'=2,'x'=4,'c'=2] {'c'}, dimensions={0}, use_global_device_ids=true | all-gather | bytes 589824 | tf_op jit(solution)/shard_map/all_gather | solution.py:151
  155.4 0.1 convert_bitcast_fusion
  155.5 1.1 copy.18
  156.6 5.9 %collective-permute-done.8 = bf16[768,256]{1,0:T(8,128)(2,1)} collective-permute-done((bf16[768,256]{1,0:T(8,128)(2,1)}, bf16[768,256]{1,0:T(8,128)(2,1)}, u32[]{:S(2)}, u32[]{:S(2)}) %collective-permute-start.8) | collective-permute-done | bytes 393248 | tf_op jit(solution)/shard_map/ppermute | solution.py:21
  162.6 0.0 copy-done.2
  162.6 2.0 %add_multiply_fusion = f32[768,256]{1,0:T(8,128)} fusion(bf16[768,256]{1,0:T(8,128)(2,1)} %collective-permute-done.8, f32[768,256]{1,0:T(8,128)S(1)} %copy-done.2, bf16[768,512]{1,0:T(8,128)(2,1)S(1)} %collective-permute-done.7), kind=kLoop, calls=%fused_computation.7 | loop fusion | flops 983040 | bytes 2359296 | tf_op jit(solution)/shard_map/mul | solution.py:152
  (27 shorter events, 0.4 us)
Async XLA Ops:
  0.6 1.2 copy-start
  0.6 4.4 %copy-start.6 = (s32[256]{0:T(256)S(1)}, s32[256]{0:T(256)}, u32[]{:S(2)}) copy-start(s32[256]{0:T(256)} %param.13) | copy-start | bytes 3076
  6.0 22.5 %all-to-all-start = ((f32[16,72,128]{2,1,0:T(8,128)}), f32[16,72,128]{2,1,0:T(8,128)S(1)}, u32[]{:S(2)}, u32[]{:S(2)}) async-start(f32[16,72,128]{2,1,0:T(8,128)} %pad_maximum_fusion), calls=%async_computation | async-start | bytes 1179648 | tf_op jit(solution)/shard_map/all_to_all | solution.py:31
  16.2 5.9 %copy-start.5 = (s32[1,1024]{1,0:T(1,128)S(1)}, s32[1,1024]{1,0:T(1,128)}, u32[]{:S(2)}) copy-start(s32[1,1024]{1,0:T(1,128)} %param.11) | copy-start | bytes 12292
  18.8 26.6 %collective-permute-start = (bf16[1024,256]{1,0:T(8,128)(2,1)S(1)}, bf16[1024,256]{1,0:T(8,128)(2,1)}, u32[]{:S(2)}, u32[]{:S(2)}) collective-permute-start(bf16[1024,256]{1,0:T(8,128)(2,1)S(1)} %pad_maximum_fusion.3), channel_id=1, source_target_pairs={{0,2},{2,4},{4,6},{6,0},{1,3},{3,5},{5,7},{7,1},{8,10},{10,12},{12... | collective-permute-start | bytes 1572872 | tf_op jit(solution)/shard_map/ppermute | solution.py:25
  29.3 13.4 %all-to-all-start.1 = ((bf16[16,64,128]{2,1,0:T(8,128)(2,1)}), bf16[16,64,128]{2,1,0:T(8,128)(2,1)S(1)}, u32[]{:S(2)}, u32[]{:S(2)}) async-start(bf16[16,64,128]{2,1,0:T(8,128)(2,1)} %broadcast_in_dim.11), calls=%async_computation.1 | async-start | bytes 524288 | tf_op jit(solution)/shard_map/all_to_all | solution.py:31
  45.4 44.1 %all-to-all-start.2 = ((bf16[32,32,256]{2,1,0:T(8,128)(2,1)}), bf16[32,32,256]{2,1,0:T(8,128)(2,1)S(1)}, u32[]{:S(2)}, u32[]{:S(2)}) async-start(bf16[32,32,256]{2,1,0:T(8,128)(2,1)} %pad_maximum_fusion.2), calls=%async_computation.2 | async-start | bytes 1048576 | tf_op jit(solution)/shard_map/all_to_all | solution.py:31
  60.0 14.6 %collective-permute-start.2 = (bf16[1024,256]{1,0:T(8,128)(2,1)S(1)}, bf16[1024,256]{1,0:T(8,128)(2,1)S(1)}, u32[]{:S(2)}, u32[]{:S(2)}) collective-permute-start(bf16[1024,256]{1,0:T(8,128)(2,1)S(1)} %pad_maximum_fusion.5), channel_id=1, source_target_pairs={{0,6},{2,0},{4,2},{6,4},{1,7},{3,1},{5,3},{7,5},{8,14},{10,8},{12,... | collective-permute-start | bytes 1572872 | tf_op jit(solution)/shard_map/ppermute | solution.py:25
  63.2 16.4 %collective-permute-start.1 = (bf16[1024,256]{1,0:T(8,128)(2,1)S(1)}, bf16[1024,256]{1,0:T(8,128)(2,1)}, u32[]{:S(2)}, u32[]{:S(2)}) collective-permute-start(bf16[1024,256]{1,0:T(8,128)(2,1)S(1)} %pad_maximum_fusion.4), channel_id=1, source_target_pairs={{0,4},{2,6},{4,0},{6,2},{1,5},{3,7},{5,1},{7,3},{8,12},{10,14},{12... | collective-permute-start | bytes 1572872 | tf_op jit(solution)/shard_map/ppermute | solution.py:25
  74.6 0.8 copy-start.7
  89.5 39.8 %copy-start.1 = (bf16[32,24,256]{2,1,0:T(8,128)(2,1)}, bf16[32,24,256]{2,1,0:T(8,128)(2,1)S(1)}, u32[]{:S(2)}) copy-start(bf16[32,24,256]{2,1,0:T(8,128)(2,1)S(1)} %slice.34) | copy-start | bytes 1179652
  90.8 15.1 %all-to-all-start.3 = ((f32[16,8,384]{2,1,0:T(8,128)}), f32[16,8,384]{2,1,0:T(8,128)S(1)}, u32[]{:S(2)}, u32[]{:S(2)}) async-start(f32[16,8,384]{2,1,0:T(8,128)} %bitcast.22), calls=%async_computation.3 | async-start | bytes 393216 | tf_op jit(solution)/shard_map/all_to_all | solution.py:31
  97.7 14.4 %collective-permute-start.3 = (bf16[768,256]{1,0:T(8,128)(2,1)S(1)}, bf16[768,256]{1,0:T(8,128)(2,1)S(1)}, u32[]{:S(2)}, u32[]{:S(2)}) collective-permute-start(bf16[768,256]{1,0:T(8,128)(2,1)S(1)} %bitcast.64), channel_id=1, source_target_pairs={{0,2},{2,4},{4,6},{6,0},{1,3},{3,5},{5,7},{7,1},{8,10},{10,12},{12... | collective-permute-start | bytes 1179656 | tf_op jit(solution)/shard_map/ppermute | solution.py:25
  101.0 11.9 %collective-permute-start.4 = (bf16[768,256]{1,0:T(8,128)(2,1)S(1)}, bf16[768,256]{1,0:T(8,128)(2,1)S(1)}, u32[]{:S(2)}, u32[]{:S(2)}) collective-permute-start(bf16[768,256]{1,0:T(8,128)(2,1)S(1)} %bitcast.65), channel_id=1, source_target_pairs={{0,6},{2,0},{4,2},{6,4},{1,7},{3,1},{5,3},{7,5},{8,14},{10,8},{12,... | collective-permute-start | bytes 1179656 | tf_op jit(solution)/shard_map/ppermute | solution.py:25
  112.1 19.5 %copy-start.3 = (bf16[768,256]{1,0:T(8,128)(2,1)}, bf16[768,256]{1,0:T(8,128)(2,1)S(1)}, u32[]{:S(2)}) copy-start(bf16[768,256]{1,0:T(8,128)(2,1)S(1)} %collective-permute-done.3.left) | copy-start | bytes 1179652
  112.9 18.7 %copy-start.4 = (bf16[768,256]{1,0:T(8,128)(2,1)}, bf16[768,256]{1,0:T(8,128)(2,1)S(1)}, u32[]{:S(2)}) copy-start(bf16[768,256]{1,0:T(8,128)(2,1)S(1)} %collective-permute-done.4.right) | copy-start | bytes 1179652
  113.7 24.2 %all-to-all-start.4 = ((bf16[32,8,384]{2,1,0:T(8,128)(2,1)}), bf16[32,8,384]{2,1,0:T(8,128)(2,1)S(1)}, u32[]{:S(2)}, u32[]{:S(2)}) async-start(bf16[32,8,384]{2,1,0:T(8,128)(2,1)} %broadcast_in_dim.14), calls=%async_computation.4 | async-start | bytes 393216 | tf_op jit(solution)/shard_map/all_to_all | solution.py:31
  121.7 8.1 %collective-permute-start.5 = (bf16[384,256]{1,0:T(8,128)(2,1)S(1)}, bf16[384,256]{1,0:T(8,128)(2,1)S(1)}, u32[]{:S(2)}, u32[]{:S(2)}) collective-permute-start(bf16[384,256]{1,0:T(8,128)(2,1)S(1)} %slice.36), channel_id=1, source_target_pairs={{0,2},{2,4},{4,6},{6,0},{1,3},{3,5},{5,7},{7,1},{8,10},{10,12},{12... | collective-permute-start | bytes 589832 | tf_op jit(solution)/shard_map/ppermute | solution.py:25
  124.8 6.7 %collective-permute-start.6 = (bf16[384,256]{1,0:T(8,128)(2,1)S(1)}, bf16[384,256]{1,0:T(8,128)(2,1)}, u32[]{:S(2)}, u32[]{:S(2)}) collective-permute-start(bf16[384,256]{1,0:T(8,128)(2,1)S(1)} %slice.37), channel_id=1, source_target_pairs={{0,6},{2,0},{4,2},{6,4},{1,7},{3,1},{5,3},{7,5},{8,14},{10,8},{12,... | collective-permute-start | bytes 589832 | tf_op jit(solution)/shard_map/ppermute | solution.py:25
  129.8 1.7 %copy-start.8 = (bf16[384,256]{1,0:T(8,128)(2,1)}, bf16[384,256]{1,0:T(8,128)(2,1)S(1)}, u32[]{:S(2)}) copy-start(bf16[384,256]{1,0:T(8,128)(2,1)S(1)} %collective-permute-done.5.upper) | copy-start | bytes 589828
  137.8 8.0 %collective-permute-start.7 = (bf16[768,512]{1,0:T(8,128)(2,1)}, bf16[768,512]{1,0:T(8,128)(2,1)S(1)}, u32[]{:S(2)}, u32[]{:S(2)}) collective-permute-start(bf16[768,512]{1,0:T(8,128)(2,1)} %get-tuple-element.25), channel_id=1, source_target_pairs={{0,1},{1,0},{2,3},{3,2},{4,5},{5,4},{6,7},{7,6},{8,9},{9,8},{10,11... | collective-permute-start | bytes 2359304 | tf_op jit(solution)/shard_map/ppermute | solution.py:21
  145.8 16.7 %copy-start.2 = (f32[768,256]{1,0:T(8,128)S(1)}, f32[768,256]{1,0:T(8,128)}, u32[]{:S(2)}) copy-start(f32[768,256]{1,0:T(8,128)} %get-tuple-element.22) | copy-start | bytes 2359300
  147.9 14.7 %collective-permute-start.8 = (bf16[768,256]{1,0:T(8,128)(2,1)}, bf16[768,256]{1,0:T(8,128)(2,1)}, u32[]{:S(2)}, u32[]{:S(2)}) collective-permute-start(bf16[768,256]{1,0:T(8,128)(2,1)} %add_convert_fusion), channel_id=1, source_target_pairs={{0,8},{8,0},{1,9},{9,1},{2,10},{10,2},{3,11},{11,3},{4,12},{12,4},... | collective-permute-start | bytes 1179656 | tf_op jit(solution)/shard_map/ppermute | solution.py:21
